TPU v7x, 128 devices: a whole 4x4x4 slice. The times are simulated.
128 devices in a mesh: leaf: 128 (over z, y, x, core).
Axes of the slice: x: 4, y: 4, z: 4, core: 2. Of those that a mesh axis runs over, the one named last changes fastest.
Arguments:
- points: bfloat16 [262144, 128], P('leaf'), may hold values from -6 to 6
- charges: bfloat16 [262144, 256], P('leaf'), may hold values from -6 to 6
- order: int32 [128, 2048], P('leaf'), may hold values from 0 to 2047, each once within a row
- near: int32 [128, 2], P('leaf'), may hold values from 0 to 127, as said below
- bases: bfloat16 [262144, 256], P('leaf'), may hold values from -0.125 to 0.125
- lift_leaf: float32 [32768, 256], P('leaf'), may hold values from -0.1875 to 0.1875
- lift_node: float32 [8192, 256], P('leaf'), may hold values from -0.1875 to 0.1875
- proxy_leaf: float32 [32768, 128], P('leaf'), may hold values from -5 to 5
- proxy_node: float32 [8192, 128], P('leaf'), may hold values from -5 to 5
- proxy_top: float32 [2048, 128], P('leaf'), may hold values from -5 to 5
Outputs:
- potential: bfloat16 [262144, 256], P('leaf')
Inputs may be any that keep to these rules, and one draw needn't show every extreme that they name: `order`: each row is a permutation of the leaf's 2048 positions. `near`: row l names two distinct leaves other than l from l's aligned group of four leaves; the relation is symmetric, and the group's remaining leaf is l's far partner, whose index differs from l in exactly one of the two lowest bits.
All inputs are finite; a program needn't handle non-finite values.
Results may differ from a plain program's by a relative error of at most 0.0049.
Values may be sent and summed in bfloat16 or wider, within the bound.
No kernel may reach another device: no remote copies, remote signals or barrier semaphores. Data moves between devices by JAX's collectives and lax.ppermute only.
A program may use at most 64 MiB of HBM per device.

v0:
```python
import jax
import jax.numpy as jnp
from jax import lax
from jax.sharding import Mesh
from jax.sharding import PartitionSpec as P

D = 128
NRHS = 256
RANK = 256
LEAF = 2048
LEAF_AXES = ("leaf_0", "leaf_1", "leaf_2", "leaf_3")


highest = lax.Precision.HIGHEST


def shortened(shard):
    return jax.tree.map(lambda a: a.astype(jnp.bfloat16) if a.dtype == jnp.float32 else a, shard)


def from_partner(shard, axis, stride):
    return lax.ppermute(shard, axis, [(i, i ^ 1 << stride) for i in range(lax.axis_size(axis))])


def sent_to_all(shard, axis):
    peers = lax.axis_size(axis)
    return lax.all_to_all(
        jnp.broadcast_to(shard[None], (peers, *shard.shape)), axis, 0, 0, tiled=True
    )


def laid_out(pieces, dim):
    shape = list(pieces.shape[1:])
    shape[dim] *= pieces.shape[0]
    return jnp.moveaxis(pieces, 0, dim).reshape(shape)


def gather_axes(shard, axes, dim):
    far, near = axes
    pieces = sent_to_all(sent_to_all(shard, far), near)
    return laid_out(pieces.swapaxes(0, 1).reshape(-1, *shard.shape), dim)


def couple(left, right):
    products = jnp.dot(left, right.T, precision=highest)
    left_norm = jnp.sum(left * left, axis=1)
    right_norm = jnp.sum(right * right, axis=1)
    return jnp.exp((2.0 * products - left_norm[:, None] - right_norm[None, :]) * (2.0 / D))


def near_term(own, other, values):
    block_rows = min(512, LEAF)
    other_norm = jnp.sum(jnp.square(other.astype(jnp.float32)), axis=1)

    def one_block(row_points):
        products = jnp.dot(row_points, other.T, preferred_element_type=jnp.float32)
        row_norm = jnp.sum(jnp.square(row_points.astype(jnp.float32)), axis=1)
        tile = jnp.exp((2.0 * products - row_norm[:, None] - other_norm[None, :]) * (2.0 / D))
        return jnp.dot(tile.astype(jnp.bfloat16), values, preferred_element_type=jnp.float32)

    blocks = lax.map(one_block, own.reshape(LEAF // block_rows, block_rows, D))
    return blocks.reshape(LEAF, NRHS)


def group_collect(pieces, low_bit, position):
    partner = jax.tree.map(
        lambda part, own: part.astype(own.dtype),
        from_partner(shortened(pieces), LEAF_AXES, low_bit),
        pieces,
    )
    low_value = position // 2**low_bit % 2
    pairs = tuple(
        (
            jnp.where(low_value == 0, jnp.stack([mine, other]), jnp.stack([other, mine]))
            for mine, other in zip(pieces, partner)
        )
    )
    partner_pairs = jax.tree.map(
        lambda part, own: part.astype(own.dtype),
        from_partner(shortened(pairs), LEAF_AXES, low_bit + 1),
        pairs,
    )
    high_value = position // 2 ** (low_bit + 1) % 2
    return tuple(
        (
            jnp.where(
                high_value == 0,
                jnp.concatenate([mine, other], 0),
                jnp.concatenate([other, mine], 0),
            )
            for mine, other in zip(pairs, partner_pairs)
        )
    )


def pick_sibling(relation, near_one, near_two, near_three):
    chosen_points = jnp.where(
        relation == 1, near_one[0], jnp.where(relation == 2, near_two[0], near_three[0])
    )
    chosen_rhs = jnp.where(
        relation == 1, near_one[1], jnp.where(relation == 2, near_two[1], near_three[1])
    )
    return (chosen_points, chosen_rhs)


def per_device(
    points, charges, order, near, bases, lift_leaf, lift_node, proxy_leaf, proxy_node, proxy_top
):
    leaf_index = lax.axis_index(LEAF_AXES)
    leaf_slot = leaf_index % 4
    group_slot = leaf_index // 4 % 4
    top_part = leaf_index % 16
    top_nodes = lax.axis_size(LEAF_AXES) // 16
    own_node = leaf_index // 16
    rhs = jnp.take(charges, order[0], axis=0)
    near_one = from_partner((points, rhs), LEAF_AXES, 0)
    near_two = from_partner((points, rhs), LEAF_AXES, 1)
    near_three = from_partner((near_two[0], near_two[1]), LEAF_AXES, 0)
    coefficient = lax.dot_general(
        bases, rhs, (((0,), (0,)), ((), ())), preferred_element_type=jnp.float32
    )
    up_term = lax.dot_general(lift_leaf, coefficient, (((0,), (0,)), ((), ())), precision=highest)
    own_block = jnp.concatenate([coefficient, proxy_leaf], 1)
    total = near_term(points, points, rhs)
    for column in range(2):
        relation = jnp.bitwise_xor(near[0, column] % 4, leaf_slot)
        chosen_points, chosen_rhs = pick_sibling(relation, near_one, near_two, near_three)
        total = total + near_term(points, chosen_points, chosen_rhs)
    first_quad = group_collect((own_block, up_term, proxy_node, lift_node), 0, leaf_index)
    leaf_data = first_quad[0].reshape(4 * RANK, NRHS + D)
    node_coeff = jnp.sum(first_quad[1], axis=0)
    node_proxy = first_quad[2].reshape(RANK, D)
    node_lift = first_quad[3].reshape(RANK, RANK)
    top_term = lax.dot_general(node_lift, node_coeff, (((0,), (0,)), ((), ())), precision=highest)
    node_block = jnp.concatenate([node_coeff, node_proxy], 1)
    top_rows = RANK // 16
    second_quad = group_collect((node_block, top_term), 2, leaf_index)
    group_data = second_quad[0].reshape(4 * RANK, NRHS + D)
    top_coeff = jnp.sum(second_quad[1], axis=0)
    top_piece = jnp.concatenate(
        [lax.dynamic_slice_in_dim(top_coeff, top_part * top_rows, top_rows, 0), proxy_top], 1
    )
    top_all = gather_axes(top_piece, (("leaf_0", "leaf_1", "leaf_2"), "leaf_3"), 0)
    owner = jnp.arange(top_nodes * RANK, dtype=jnp.int32) // RANK
    top_proxy_all = top_all[:, NRHS:]
    own_top_proxy = lax.dynamic_slice_in_dim(top_proxy_all, own_node * RANK, RANK, 0)
    top_kernel = jnp.where(owner[None, :] != own_node, couple(own_top_proxy, top_proxy_all), 0.0)
    field_top = jnp.dot(top_kernel, top_all[:, :NRHS], precision=highest)
    sibling_owner = jnp.arange(4 * RANK, dtype=jnp.int32) // RANK
    node_kernel = jnp.where(
        sibling_owner[None, :] != group_slot, couple(node_proxy, group_data[:, NRHS:]), 0.0
    )
    field_node = jnp.dot(node_kernel, group_data[:, :NRHS], precision=highest)
    field_node = field_node + jnp.dot(node_lift, field_top, precision=highest)
    partner = 6 - leaf_slot - near[0, 0] % 4 - near[0, 1] % 4
    leaf_kernel = jnp.where(
        sibling_owner[None, :] == partner, couple(proxy_leaf, leaf_data[:, NRHS:]), 0.0
    )
    field_leaf = jnp.dot(leaf_kernel, leaf_data[:, :NRHS], precision=highest)
    field_leaf = (field_leaf + jnp.dot(lift_leaf, field_node, precision=highest)).astype(
        jnp.bfloat16
    )
    descent = jnp.dot(bases, field_leaf, preferred_element_type=jnp.float32)
    return (total + descent).astype(jnp.bfloat16)


def solution(mesh):
    finer = Mesh(mesh.devices.reshape(4, 4, 4, 2), ("leaf_0", "leaf_1", "leaf_2", "leaf_3"))
    return jax.shard_map(
        per_device,
        mesh=finer,
        in_specs=(
            P(LEAF_AXES, None),
            P(LEAF_AXES, None),
            P(LEAF_AXES, None),
            P(LEAF_AXES, None),
            P(LEAF_AXES, None),
            P(LEAF_AXES, None),
            P(LEAF_AXES, None),
            P(LEAF_AXES, None),
            P(LEAF_AXES, None),
            P(LEAF_AXES, None),
        ),
        out_specs=P(LEAF_AXES, None),
        check_vma=False,
    )
```

profile of v0, /device:TPU:1, one launch (start us, length us, event | category | flops | bytes accessed | tf_op | source)
XLA Modules:
  0.0 180.1 jit_solution(15892092054579698156)
XLA Ops:
  1.5 8.0 %gather_fusion = bf16[2048,256]{1,0:T(8,128)(2,1)S(1)} fusion(bf16[2048,256]{1,0:T(8,128)(2,1)} %param.17, s32[2048]{0:T(1024)S(1)} %broadcast_clamp_fusion), kind=kCustom, calls=%fused_computation | custom fusion | bytes 2105344 | tf_op jit(solution)/shard_map/jit(_take)/gather | solution.py:115
  10.8 2.0 %collective-permute-start.4 = (bf16[2048,256]{1,0:T(8,128)(2,1)}, bf16[2048,256]{1,0:T(8,128)(2,1)}, u32[]{:S(2)}, u32[]{:S(2)}) collective-permute-start(bf16[2048,256]{1,0:T(8,128)(2,1)} %broadcast_select_fusion), channel_id=1, source_target_pairs={{0,2},{1,3},{2,0},{3,1},{4,6},{5,7},{6,4},{7,5},{8,10},{9,11},{10,... | collective-permute-start | bytes 3145736 | tf_op jit(solution)/shard_map/ppermute | solution.py:22
  25.7 15.5 %while.30 = (s32[]{:T(128)}, f32[4,512,256]{2,1,0:T(8,128)S(1)}, bf16[4,512,128]{2,1,0:T(8,128)(2,1)}, bf16[2048,128]{1,0:T(8,128)(2,1)}, f32[2048]{0:T(1024)S(1)}, /*index=5*/bf16[2048,256]{1,0:T(8,128)(2,1)}, s32[]{:T(128)}) while((s32[]{:T(128)}, f32[4,512,256]{2,1,0:T(8,128)S(1)}, bf16[4,512,128]{2,1,0:T(8,128)(2,1)}, ...), condition=%wide.region_3.4_spmd, body=%wide.region_1.3_spmd.sunk | while | flops 810745344 | bytes 2372689 | solution.py:61
  26.8 2.8 %fusion.125 = f32[4,512,256]{2,1,0:T(8,128)S(1)} fusion(f32[4,512,256]{2,1,0:T(8,128)S(1)} %get-tuple-element.310, s32[]{:T(128)} %get-tuple-element.309, bf16[2048,256]{1,0:T(8,128)(2,1)} %get-tuple-element.321, bf16[2048,128]{1,0:T(8,128)(2,1)} %get-tuple-element.319, f32[2048]{0:T(1024)S(1)} %get-tuple-element.320, ...), kind=kOutput, calls=%fused_computation.4.clone.1 | convolution fusion | flops 810549248 | bytes 2239488 | tf_op jit(solution)/shard_map/while/body/eval_jaxpr/dot_general | solution.py:59
  30.7 2.8 %fusion.125 = f32[4,512,256]{2,1,0:T(8,128)S(1)} fusion(f32[4,512,256]{2,1,0:T(8,128)S(1)} %get-tuple-element.310, s32[]{:T(128)} %get-tuple-element.309, bf16[2048,256]{1,0:T(8,128)(2,1)} %get-tuple-element.321, bf16[2048,128]{1,0:T(8,128)(2,1)} %get-tuple-element.319, f32[2048]{0:T(1024)S(1)} %get-tuple-element.320, ...), kind=kOutput, calls=%fused_computation.4.clone.1 | convolution fusion | flops 810549248 | bytes 2239488 | tf_op jit(solution)/shard_map/while/body/eval_jaxpr/dot_general | solution.py:59
  34.6 2.8 %fusion.125 = f32[4,512,256]{2,1,0:T(8,128)S(1)} fusion(f32[4,512,256]{2,1,0:T(8,128)S(1)} %get-tuple-element.310, s32[]{:T(128)} %get-tuple-element.309, bf16[2048,256]{1,0:T(8,128)(2,1)} %get-tuple-element.321, bf16[2048,128]{1,0:T(8,128)(2,1)} %get-tuple-element.319, f32[2048]{0:T(1024)S(1)} %get-tuple-element.320, ...), kind=kOutput, calls=%fused_computation.4.clone.1 | convolution fusion | flops 810549248 | bytes 2239488 | tf_op jit(solution)/shard_map/while/body/eval_jaxpr/dot_general | solution.py:59
  38.5 2.8 %fusion.125 = f32[4,512,256]{2,1,0:T(8,128)S(1)} fusion(f32[4,512,256]{2,1,0:T(8,128)S(1)} %get-tuple-element.310, s32[]{:T(128)} %get-tuple-element.309, bf16[2048,256]{1,0:T(8,128)(2,1)} %get-tuple-element.321, bf16[2048,128]{1,0:T(8,128)(2,1)} %get-tuple-element.319, f32[2048]{0:T(1024)S(1)} %get-tuple-element.320, ...), kind=kOutput, calls=%fused_computation.4.clone.1 | convolution fusion | flops 810549248 | bytes 2239488 | tf_op jit(solution)/shard_map/while/body/eval_jaxpr/dot_general | solution.py:59
  59.5 6.2 %collective-permute-done.11 = bf16[2,256,256]{1,2,0:T(8,128)(2,1)S(1)} collective-permute-done((bf16[2,256,256]{1,2,0:T(8,128)(2,1)S(1)}, bf16[2,256,256]{1,2,0:T(8,128)(2,1)S(1)}, u32[]{:S(2)}, u32[]{:S(2)}) %collective-permute-start.11) | collective-permute-done | bytes 262176 | tf_op jit(solution)/shard_map/ppermute | solution.py:22
  66.4 3.1 %collective-permute-start.16 = (bf16[256,256]{1,0:T(8,128)(2,1)S(1)}, bf16[256,256]{1,0:T(8,128)(2,1)S(1)}, u32[]{:S(2)}, u32[]{:S(2)}) collective-permute-start(bf16[256,256]{1,0:T(8,128)(2,1)S(1)} %get-tuple-element.168), channel_id=1, source_target_pairs={{0,4},{1,5},{2,6},{3,7},{4,0},{5,1},{6,2},{7,3},{8,12},{9,13},{10,... | collective-permute-start | bytes 393224 | tf_op jit(solution)/shard_map/ppermute | solution.py:22
  69.6 9.8 %collective-permute-done.16 = bf16[256,256]{1,0:T(8,128)(2,1)S(1)} collective-permute-done((bf16[256,256]{1,0:T(8,128)(2,1)S(1)}, bf16[256,256]{1,0:T(8,128)(2,1)S(1)}, u32[]{:S(2)}, u32[]{:S(2)}) %collective-permute-start.16) | collective-permute-done | bytes 131104 | tf_op jit(solution)/shard_map/ppermute | solution.py:22
  80.9 5.7 %collective-permute-done.12 = bf16[256,384]{0,1:T(8,128)(2,1)S(1)} collective-permute-done((bf16[256,384]{0,1:T(8,128)(2,1)S(1)}, bf16[256,384]{0,1:T(8,128)(2,1)S(1)}, u32[]{:S(2)}, u32[]{:S(2)}) %collective-permute-start.12) | collective-permute-done | bytes 196640 | tf_op jit(solution)/shard_map/ppermute | solution.py:22
  90.2 1.9 %copy.27 = f32[4,256,384]{2,1,0:T(8,128)S(1)} copy(f32[4,256,384]{1,2,0:T(8,128)} %maximum_select_fusion) | data formatting | bytes 3145728 | tf_op jit(solution)/shard_map/jit(_where)/select_n | solution.py:86
  93.5 2.5 %fusion.56 = f32[256,256]{1,0:T(8,128)} fusion(f32[1024,256]{1,0:T(8,128)S(1)} %fusion.51, f32[1024,384]{1,0:T(8,128)S(1)} %bitcast.146), kind=kOutput, calls=%fused_computation.63 | convolution fusion | flops 805306368 | bytes 2359296 | tf_op jit(solution)/shard_map/dot_general | solution.py:159
  96.1 2.2 %collective-permute-start = (bf16[2048,128]{1,0:T(8,128)(2,1)}, bf16[2048,128]{1,0:T(8,128)(2,1)}, u32[]{:S(2)}, u32[]{:S(2)}) collective-permute-start(bf16[2048,128]{1,0:T(8,128)(2,1)} %param.16), channel_id=1, source_target_pairs={{0,1},{1,0},{2,3},{3,2},{4,5},{5,4},{6,7},{7,6},{8,9},{9,8},{10,11... | collective-permute-start | bytes 1572872 | tf_op jit(solution)/shard_map/ppermute | solution.py:22
  100.9 9.1 %all-to-all-start = ((f32[64,16,384]{2,1,0:T(8,128)}), f32[64,16,384]{2,1,0:T(8,128)}, u32[]{:S(2)}, u32[]{:S(2)}) async-start(f32[64,16,384]{2,1,0:T(8,128)} %broadcast_in_dim.83), calls=%async_computation | async-start | bytes 3145728 | tf_op jit(solution)/shard_map/all_to_all | solution.py:27
  117.8 2.9 %multiply_reduce_fusion.5 = (f32[2048]{0:T(1024)S(1)}, bf16[2048,128]{1,0:T(8,128)(2,1)}, f32[2048]{0:T(1024)S(1)}, bf16[2048,128]{1,0:T(8,128)(2,1)}) fusion(bf16[2048,128]{1,0:T(8,128)(2,1)} %collective-permute-done, bf16[2048,128]{1,0:T(8,128)(2,1)} %collective-permute-done.1, bf16[2048,128]{1,0:T(8,128)(2,1)} %collective-permute-done.2, pred[]{:T(512)S(6)} %eq.60, ...), kind=kLoop, calls=%fused_computation.73 | loop fusion | flops 2617344 | bytes 2637828 | tf_op jit(solution)/shard_map/reduce_sum | solution.py:53
  120.7 3.3 %select_select_fusion.1 = (bf16[2048,256]{1,0:T(8,128)(2,1)}, bf16[2048,256]{1,0:T(8,128)(2,1)}) fusion(bf16[2048,256]{1,0:T(8,128)(2,1)} %collective-permute-done.3, bf16[2048,256]{1,0:T(8,128)(2,1)} %collective-permute-done.4, bf16[2048,256]{1,0:T(8,128)(2,1)} %collective-permute-done.5, pred[]{:T(512)S(6)} %eq.60, pred[]{:T(512)S(6)} %eq.59, pred[]{:T(512)S(6)} %eq.62, ...), kind=kLoop, calls=%fused_computation.72 | loop fusion | flops 2097152 | bytes 5242884 | tf_op jit(solution)/shard_map/jit(_where)/select_n | solution.py:100
  124.2 15.5 %while.31 = (s32[]{:T(128)}, f32[4,512,256]{2,1,0:T(8,128)S(1)}, bf16[4,512,128]{2,1,0:T(8,128)(2,1)}, bf16[2048,128]{1,0:T(8,128)(2,1)}, f32[2048]{0:T(1024)S(1)}, /*index=5*/bf16[2048,256]{1,0:T(8,128)(2,1)}, s32[]{:T(128)}) while((s32[]{:T(128)}, f32[4,512,256]{2,1,0:T(8,128)S(1)}, bf16[4,512,128]{2,1,0:T(8,128)(2,1)}, ...), condition=%wide.region_7.8_spmd, body=%wide.region_5.7_spmd.sunk | while | flops 810745344 | bytes 2372689 | solution.py:61
  125.3 2.8 %fusion.129 = f32[4,512,256]{2,1,0:T(8,128)S(1)} fusion(f32[4,512,256]{2,1,0:T(8,128)S(1)} %get-tuple-element.331, s32[]{:T(128)} %get-tuple-element.330, bf16[2048,256]{1,0:T(8,128)(2,1)} %get-tuple-element.342, bf16[2048,128]{1,0:T(8,128)(2,1)} %get-tuple-element.340, f32[2048]{0:T(1024)S(1)} %get-tuple-element.341, ...), kind=kOutput, calls=%fused_computation.14.clone.1 | convolution fusion | flops 810549248 | bytes 2239488 | tf_op jit(solution)/shard_map/while/body/eval_jaxpr/dot_general | solution.py:59
  129.2 2.8 %fusion.129 = f32[4,512,256]{2,1,0:T(8,128)S(1)} fusion(f32[4,512,256]{2,1,0:T(8,128)S(1)} %get-tuple-element.331, s32[]{:T(128)} %get-tuple-element.330, bf16[2048,256]{1,0:T(8,128)(2,1)} %get-tuple-element.342, bf16[2048,128]{1,0:T(8,128)(2,1)} %get-tuple-element.340, f32[2048]{0:T(1024)S(1)} %get-tuple-element.341, ...), kind=kOutput, calls=%fused_computation.14.clone.1 | convolution fusion | flops 810549248 | bytes 2239488 | tf_op jit(solution)/shard_map/while/body/eval_jaxpr/dot_general | solution.py:59
  133.0 2.8 %fusion.129 = f32[4,512,256]{2,1,0:T(8,128)S(1)} fusion(f32[4,512,256]{2,1,0:T(8,128)S(1)} %get-tuple-element.331, s32[]{:T(128)} %get-tuple-element.330, bf16[2048,256]{1,0:T(8,128)(2,1)} %get-tuple-element.342, bf16[2048,128]{1,0:T(8,128)(2,1)} %get-tuple-element.340, f32[2048]{0:T(1024)S(1)} %get-tuple-element.341, ...), kind=kOutput, calls=%fused_computation.14.clone.1 | convolution fusion | flops 810549248 | bytes 2239488 | tf_op jit(solution)/shard_map/while/body/eval_jaxpr/dot_general | solution.py:59
  136.9 2.8 %fusion.129 = f32[4,512,256]{2,1,0:T(8,128)S(1)} fusion(f32[4,512,256]{2,1,0:T(8,128)S(1)} %get-tuple-element.331, s32[]{:T(128)} %get-tuple-element.330, bf16[2048,256]{1,0:T(8,128)(2,1)} %get-tuple-element.342, bf16[2048,128]{1,0:T(8,128)(2,1)} %get-tuple-element.340, f32[2048]{0:T(1024)S(1)} %get-tuple-element.341, ...), kind=kOutput, calls=%fused_computation.14.clone.1 | convolution fusion | flops 810549248 | bytes 2239488 | tf_op jit(solution)/shard_map/while/body/eval_jaxpr/dot_general | solution.py:59
  141.2 15.5 %while.32 = (s32[]{:T(128)}, f32[4,512,256]{2,1,0:T(8,128)S(1)}, bf16[4,512,128]{2,1,0:T(8,128)(2,1)}, bf16[2048,128]{1,0:T(8,128)(2,1)}, f32[2048]{0:T(1024)S(1)}, /*index=5*/bf16[2048,256]{1,0:T(8,128)(2,1)}, s32[]{:T(128)}) while((s32[]{:T(128)}, f32[4,512,256]{2,1,0:T(8,128)S(1)}, bf16[4,512,128]{2,1,0:T(8,128)(2,1)}, ...), condition=%wide.region_11.12_spmd, body=%wide.region_9.11_spmd.sunk | while | flops 810745344 | bytes 2372689 | solution.py:61
  142.3 2.8 %fusion.133 = f32[4,512,256]{2,1,0:T(8,128)S(1)} fusion(f32[4,512,256]{2,1,0:T(8,128)S(1)} %get-tuple-element.289, s32[]{:T(128)} %get-tuple-element.288, bf16[2048,256]{1,0:T(8,128)(2,1)} %get-tuple-element.300, bf16[2048,128]{1,0:T(8,128)(2,1)} %get-tuple-element.298, f32[2048]{0:T(1024)S(1)} %get-tuple-element.299, ...), kind=kOutput, calls=%fused_computation.24.clone.1 | convolution fusion | flops 810549248 | bytes 2239488 | tf_op jit(solution)/shard_map/while/body/eval_jaxpr/dot_general | solution.py:59
  146.2 2.8 %fusion.133 = f32[4,512,256]{2,1,0:T(8,128)S(1)} fusion(f32[4,512,256]{2,1,0:T(8,128)S(1)} %get-tuple-element.289, s32[]{:T(128)} %get-tuple-element.288, bf16[2048,256]{1,0:T(8,128)(2,1)} %get-tuple-element.300, bf16[2048,128]{1,0:T(8,128)(2,1)} %get-tuple-element.298, f32[2048]{0:T(1024)S(1)} %get-tuple-element.299, ...), kind=kOutput, calls=%fused_computation.24.clone.1 | convolution fusion | flops 810549248 | bytes 2239488 | tf_op jit(solution)/shard_map/while/body/eval_jaxpr/dot_general | solution.py:59
  150.0 2.8 %fusion.133 = f32[4,512,256]{2,1,0:T(8,128)S(1)} fusion(f32[4,512,256]{2,1,0:T(8,128)S(1)} %get-tuple-element.289, s32[]{:T(128)} %get-tuple-element.288, bf16[2048,256]{1,0:T(8,128)(2,1)} %get-tuple-element.300, bf16[2048,128]{1,0:T(8,128)(2,1)} %get-tuple-element.298, f32[2048]{0:T(1024)S(1)} %get-tuple-element.299, ...), kind=kOutput, calls=%fused_computation.24.clone.1 | convolution fusion | flops 810549248 | bytes 2239488 | tf_op jit(solution)/shard_map/while/body/eval_jaxpr/dot_general | solution.py:59
  153.9 2.8 %fusion.133 = f32[4,512,256]{2,1,0:T(8,128)S(1)} fusion(f32[4,512,256]{2,1,0:T(8,128)S(1)} %get-tuple-element.289, s32[]{:T(128)} %get-tuple-element.288, bf16[2048,256]{1,0:T(8,128)(2,1)} %get-tuple-element.300, bf16[2048,128]{1,0:T(8,128)(2,1)} %get-tuple-element.298, f32[2048]{0:T(1024)S(1)} %get-tuple-element.299, ...), kind=kOutput, calls=%fused_computation.24.clone.1 | convolution fusion | flops 810549248 | bytes 2239488 | tf_op jit(solution)/shard_map/while/body/eval_jaxpr/dot_general | solution.py:59
  156.7 3.9 %add_add_fusion = f32[4,512,256]{2,1,0:T(8,128)} fusion(f32[4,512,256]{2,1,0:T(8,128)S(1)} %get-tuple-element.103, f32[4,512,256]{2,1,0:T(8,128)} %copy-done.1, f32[4,512,256]{2,1,0:T(8,128)} %copy-done.2), kind=kLoop, calls=%fused_computation.42 | loop fusion | flops 1048576 | bytes 8388608 | tf_op jit(solution)/shard_map/add | solution.py:128
  160.7 1.9 %copy.34 = f32[2048,256]{0,1:T(8,128)S(1)} copy(f32[2048,256]{1,0:T(8,128)} %bitcast.140) | data formatting | bytes 4194304 | tf_op jit(solution)/shard_map/add | solution.py:128
  164.2 6.2 %all_to_all.10 = f32[2,64,16,384]{3,2,1,0:T(8,128)S(1)} all-to-all(f32[2,64,16,384]{3,2,1,0:T(8,128)S(1)} %broadcast_in_dim.84), channel_id=1, replica_groups=mesh['leaf_0'=4,'leaf_1'=4,'leaf_2'=4,'leaf_3'=2] {'leaf_3'}, dimensions={0} | all-to-all | bytes 6291456 | tf_op jit(solution)/shard_map/all_to_all | solution.py:27
  171.3 2.2 %fusion.38 = f32[256,2048]{1,0:T(8,128)S(1)} fusion(f32[2048,128]{1,0:T(8,128)S(1)} %get-tuple-element.159, f32[2048]{0:T(1024)S(1)} %get-tuple-element.158, f32[256]{0:T(256)S(1)} %multiply_reduce_fusion.9, pred[2048]{0:T(1024)(128)(4,1)S(1)} %fusion.67, s32[]{:T(128)S(6)} %select_n.339), kind=kOutput, calls=%fused_computation.38 | convolution fusion | flops 807927808 | bytes 3288068 | tf_op jit(solution)/shard_map/dot_general | solution.py:45
  177.8 2.3 %copy.32 = bf16[2048,256]{1,0:T(8,128)(2,1)} copy(bf16[2048,256]{0,1:T(8,128)(2,1)} %fusion.39) | data formatting | bytes 2097152 | tf_op jit(solution)/shard_map/convert_element_type | solution.py:164
  (145 shorter events, 68.5 us)
Async XLA Ops:
  0.0 13.8 %copy-start = (bf16[2048,256]{1,0:T(8,128)(2,1)S(1)}, bf16[2048,256]{1,0:T(8,128)(2,1)}, u32[]{:S(2)}) copy-start(bf16[2048,256]{1,0:T(8,128)(2,1)} %param.20) | copy-start | bytes 3145732
  9.5 6.0 %copy-start.7 = (f32[256,256]{1,0:T(8,128)S(1)}, f32[256,256]{1,0:T(8,128)}, u32[]{:S(2)}) copy-start(f32[256,256]{1,0:T(8,128)} %param.21) | copy-start | bytes 786436
  10.8 5.9 %copy-start.13 = (f32[64,128]{1,0:T(8,128)S(1)}, f32[64,128]{1,0:T(8,128)}, u32[]{:S(2)}) copy-start(f32[64,128]{1,0:T(8,128)} %param.24) | copy-start | bytes 98308
  10.8 7.2 %copy-start.10 = (f32[256,128]{1,0:T(8,128)S(1)}, f32[256,128]{1,0:T(8,128)}, u32[]{:S(2)}) copy-start(f32[256,128]{1,0:T(8,128)} %param.23) | copy-start | bytes 393220
  10.8 8.0 %copy-start.15 = (s32[1,2]{1,0:T(1,128)S(1)}, s32[1,2]{1,0:T(1,128)}, u32[]{:S(2)}) copy-start(s32[1,2]{1,0:T(1,128)} %param.19) | copy-start | bytes 28
  10.8 100.3 %collective-permute-start.4 = (bf16[2048,256]{1,0:T(8,128)(2,1)}, bf16[2048,256]{1,0:T(8,128)(2,1)}, u32[]{:S(2)}, u32[]{:S(2)}) collective-permute-start(bf16[2048,256]{1,0:T(8,128)(2,1)} %broadcast_select_fusion), channel_id=1, source_target_pairs={{0,2},{1,3},{2,0},{3,1},{4,6},{5,7},{6,4},{7,5},{8,10},{9,11},{10,... | collective-permute-start | bytes 3145736 | tf_op jit(solution)/shard_map/ppermute | solution.py:22
  12.8 107.9 %collective-permute-start.3 = (bf16[2048,256]{1,0:T(8,128)(2,1)}, bf16[2048,256]{1,0:T(8,128)(2,1)}, u32[]{:S(2)}, u32[]{:S(2)}) collective-permute-start(bf16[2048,256]{1,0:T(8,128)(2,1)} %broadcast_select_fusion), channel_id=1, source_target_pairs={{0,1},{1,0},{2,3},{3,2},{4,5},{5,4},{6,7},{7,6},{8,9},{9,8},{10,11... | collective-permute-start | bytes 3145736 | tf_op jit(solution)/shard_map/ppermute | solution.py:22
  16.6 38.9 %collective-permute-start.10 = (bf16[256,256]{0,1:T(8,128)(2,1)}, bf16[256,256]{0,1:T(8,128)(2,1)}, u32[]{:S(2)}, u32[]{:S(2)}) collective-permute-start(bf16[256,256]{0,1:T(8,128)(2,1)} %get-tuple-element.166), channel_id=1, source_target_pairs={{0,1},{1,0},{2,3},{3,2},{4,5},{5,4},{6,7},{7,6},{8,9},{9,8},{10,11... | collective-permute-start | bytes 393224 | tf_op jit(solution)/shard_map/ppermute | solution.py:22
  17.3 25.7 %collective-permute-start.8 = (bf16[64,128]{1,0:T(8,128)(2,1)}, bf16[64,128]{1,0:T(8,128)(2,1)}, u32[]{:S(2)}, u32[]{:S(2)}) collective-permute-start(bf16[64,128]{1,0:T(8,128)(2,1)} %convert_element_type.99), channel_id=1, source_target_pairs={{0,1},{1,0},{2,3},{3,2},{4,5},{5,4},{6,7},{7,6},{8,9},{9,8},{10,11... | collective-permute-start | bytes 49160 | tf_op jit(solution)/shard_map/ppermute | solution.py:22
  17.8 78.3 %collective-permute-start.1 = (bf16[2048,128]{1,0:T(8,128)(2,1)}, bf16[2048,128]{1,0:T(8,128)(2,1)}, u32[]{:S(2)}, u32[]{:S(2)}) collective-permute-start(bf16[2048,128]{1,0:T(8,128)(2,1)} %param.16), channel_id=1, source_target_pairs={{0,2},{1,3},{2,0},{3,1},{4,6},{5,7},{6,4},{7,5},{8,10},{9,11},{10,... | collective-permute-start | bytes 1572872 | tf_op jit(solution)/shard_map/ppermute | solution.py:22
  41.3 18.0 %copy-start.1 = (f32[4,512,256]{2,1,0:T(8,128)}, f32[4,512,256]{2,1,0:T(8,128)S(1)}, u32[]{:S(2)}) copy-start(f32[4,512,256]{2,1,0:T(8,128)S(1)} %get-tuple-element.101) | copy-start | bytes 6291460
  43.0 1.9 %collective-permute-start.14 = (bf16[64,256]{1,0:T(8,128)(2,1)}, bf16[64,256]{1,0:T(8,128)(2,1)S(1)}, u32[]{:S(2)}, u32[]{:S(2)}) collective-permute-start(bf16[64,256]{1,0:T(8,128)(2,1)} %convert_element_type.108), channel_id=1, source_target_pairs={{0,1},{1,0},{2,3},{3,2},{4,5},{5,4},{6,7},{7,6},{8,9},{9,8},{10,11... | collective-permute-start | bytes 98312 | tf_op jit(solution)/shard_map/ppermute | solution.py:22
  44.9 3.5 %collective-permute-start.9 = (bf16[2,64,128]{2,1,0:T(8,128)(2,1)S(1)}, bf16[2,64,128]{2,1,0:T(8,128)(2,1)S(1)}, u32[]{:S(2)}, u32[]{:S(2)}) collective-permute-start(bf16[2,64,128]{2,1,0:T(8,128)(2,1)S(1)} %get-tuple-element.150), channel_id=1, source_target_pairs={{0,2},{1,3},{2,0},{3,1},{4,6},{5,7},{6,4},{7,5},{8,10},{9,11},{10,... | collective-permute-start | bytes 98312 | tf_op jit(solution)/shard_map/ppermute | solution.py:22
  48.3 3.9 %collective-permute-start.15 = (bf16[2,64,256]{2,1,0:T(8,128)(2,1)}, bf16[2,64,256]{2,1,0:T(8,128)(2,1)}, u32[]{:S(2)}, u32[]{:S(2)}) collective-permute-start(bf16[2,64,256]{2,1,0:T(8,128)(2,1)} %get-tuple-element.142), channel_id=1, source_target_pairs={{0,2},{1,3},{2,0},{3,1},{4,6},{5,7},{6,4},{7,5},{8,10},{9,11},{10,... | collective-permute-start | bytes 196616 | tf_op jit(solution)/shard_map/ppermute | solution.py:22
  52.2 7.0 %collective-permute-start.6 = (bf16[256,384]{0,1:T(8,128)(2,1)}, bf16[256,384]{0,1:T(8,128)(2,1)S(1)}, u32[]{:S(2)}, u32[]{:S(2)}) collective-permute-start(bf16[256,384]{0,1:T(8,128)(2,1)} %fusion.64), channel_id=1, source_target_pairs={{0,1},{1,0},{2,3},{3,2},{4,5},{5,4},{6,7},{7,6},{8,9},{9,8},{10,11... | collective-permute-start | bytes 589832 | tf_op jit(solution)/shard_map/ppermute | solution.py:22
  55.5 10.3 %copy-start.3 = (f32[4,64,256]{2,1,0:T(8,128)}, f32[4,64,256]{2,1,0:T(8,128)S(1)}, u32[]{:S(2)}) copy-start(f32[4,64,256]{2,1,0:T(8,128)S(1)} %maximum_select_fusion.8) | copy-start | bytes 786436
  57.7 8.0 %collective-permute-start.11 = (bf16[2,256,256]{1,2,0:T(8,128)(2,1)S(1)}, bf16[2,256,256]{1,2,0:T(8,128)(2,1)S(1)}, u32[]{:S(2)}, u32[]{:S(2)}) collective-permute-start(bf16[2,256,256]{1,2,0:T(8,128)(2,1)S(1)} %get-tuple-element.148), channel_id=1, source_target_pairs={{0,2},{1,3},{2,0},{3,1},{4,6},{5,7},{6,4},{7,5},{8,10},{9,11},{10,... | collective-permute-start | bytes 786440 | tf_op jit(solution)/shard_map/ppermute | solution.py:22
  59.3 10.2 %copy-start.6 = (f32[256,128]{0,1:T(8,128)S(1)}, f32[256,128]{0,1:T(8,128)}, u32[]{:S(2)}) copy-start(f32[256,128]{0,1:T(8,128)} %copy.28) | copy-start | bytes 393220
  59.4 29.3 %collective-permute-start.7 = (bf16[2,256,384]{1,2,0:T(8,128)(2,1)S(1)}, bf16[2,256,384]{1,2,0:T(8,128)(2,1)S(1)}, u32[]{:S(2)}, u32[]{:S(2)}) collective-permute-start(bf16[2,256,384]{1,2,0:T(8,128)(2,1)S(1)} %get-tuple-element.152), channel_id=1, source_target_pairs={{0,2},{1,3},{2,0},{3,1},{4,6},{5,7},{6,4},{7,5},{8,10},{9,11},{10,... | collective-permute-start | bytes 1179656 | tf_op jit(solution)/shard_map/ppermute | solution.py:22
  66.4 12.9 %collective-permute-start.16 = (bf16[256,256]{1,0:T(8,128)(2,1)S(1)}, bf16[256,256]{1,0:T(8,128)(2,1)S(1)}, u32[]{:S(2)}, u32[]{:S(2)}) collective-permute-start(bf16[256,256]{1,0:T(8,128)(2,1)S(1)} %get-tuple-element.168), channel_id=1, source_target_pairs={{0,4},{1,5},{2,6},{3,7},{4,0},{5,1},{6,2},{7,3},{8,12},{9,13},{10,... | collective-permute-start | bytes 393224 | tf_op jit(solution)/shard_map/ppermute | solution.py:22
  79.4 7.1 %collective-permute-start.12 = (bf16[256,384]{0,1:T(8,128)(2,1)S(1)}, bf16[256,384]{0,1:T(8,128)(2,1)S(1)}, u32[]{:S(2)}, u32[]{:S(2)}) collective-permute-start(bf16[256,384]{0,1:T(8,128)(2,1)S(1)} %fusion.62), channel_id=1, source_target_pairs={{0,4},{1,5},{2,6},{3,7},{4,0},{5,1},{6,2},{7,3},{8,12},{9,13},{10,... | collective-permute-start | bytes 589832 | tf_op jit(solution)/shard_map/ppermute | solution.py:22
  86.5 11.8 %collective-permute-start.17 = (bf16[2,256,256]{2,1,0:T(8,128)(2,1)}, bf16[2,256,256]{2,1,0:T(8,128)(2,1)}, u32[]{:S(2)}, u32[]{:S(2)}) collective-permute-start(bf16[2,256,256]{2,1,0:T(8,128)(2,1)} %get-tuple-element.140), channel_id=1, source_target_pairs={{0,8},{1,9},{2,10},{3,11},{4,12},{5,13},{6,14},{7,15},{8,0},{9,1},... | collective-permute-start | bytes 786440 | tf_op jit(solution)/shard_map/ppermute | solution.py:22
  88.7 21.3 %collective-permute-start.13 = (bf16[2,256,384]{1,2,0:T(8,128)(2,1)}, bf16[2,256,384]{1,2,0:T(8,128)(2,1)}, u32[]{:S(2)}, u32[]{:S(2)}) collective-permute-start(bf16[2,256,384]{1,2,0:T(8,128)(2,1)} %get-tuple-element.146), channel_id=1, source_target_pairs={{0,8},{1,9},{2,10},{3,11},{4,12},{5,13},{6,14},{7,15},{8,0},{9,1},... | collective-permute-start | bytes 1179656 | tf_op jit(solution)/shard_map/ppermute | solution.py:22
  90.2 2.1 %copy-start.16 = (f32[256]{0:T(256)S(1)}, f32[256]{0:T(256)}, u32[]{:S(2)}) copy-start(f32[256]{0:T(256)} %multiply_reduce_fusion.11) | copy-start | bytes 3076
  92.4 7.0 %copy-start.5 = (f32[2,256,256]{2,1,0:T(8,128)S(1)}, f32[2,256,256]{2,1,0:T(8,128)}, u32[]{:S(2)}) copy-start(f32[2,256,256]{2,1,0:T(8,128)} %get-tuple-element.141) | copy-start | bytes 1572868
  93.5 6.0 %copy-start.14 = (f32[16,128]{1,0:T(8,128)S(1)}, f32[16,128]{1,0:T(8,128)}, u32[]{:S(2)}) copy-start(f32[16,128]{1,0:T(8,128)} %param.25) | copy-start | bytes 24580
  96.1 21.7 %collective-permute-start = (bf16[2048,128]{1,0:T(8,128)(2,1)}, bf16[2048,128]{1,0:T(8,128)(2,1)}, u32[]{:S(2)}, u32[]{:S(2)}) collective-permute-start(bf16[2048,128]{1,0:T(8,128)(2,1)} %param.16), channel_id=1, source_target_pairs={{0,1},{1,0},{2,3},{3,2},{4,5},{5,4},{6,7},{7,6},{8,9},{9,8},{10,11... | collective-permute-start | bytes 1572872 | tf_op jit(solution)/shard_map/ppermute | solution.py:22
  98.3 19.5 %collective-permute-start.2 = (bf16[2048,128]{1,0:T(8,128)(2,1)}, bf16[2048,128]{1,0:T(8,128)(2,1)}, u32[]{:S(2)}, u32[]{:S(2)}) collective-permute-start(bf16[2048,128]{1,0:T(8,128)(2,1)} %collective-permute-done.1), channel_id=1, source_target_pairs={{0,1},{1,0},{2,3},{3,2},{4,5},{5,4},{6,7},{7,6},{8,9},{9,8},{10,11... | collective-permute-start | bytes 1572872 | tf_op jit(solution)/shard_map/ppermute | solution.py:22
  100.9 61.7 %all-to-all-start = ((f32[64,16,384]{2,1,0:T(8,128)}), f32[64,16,384]{2,1,0:T(8,128)}, u32[]{:S(2)}, u32[]{:S(2)}) async-start(f32[64,16,384]{2,1,0:T(8,128)} %broadcast_in_dim.83), calls=%async_computation | async-start | bytes 3145728 | tf_op jit(solution)/shard_map/all_to_all | solution.py:27
  111.1 9.6 %collective-permute-start.5 = (bf16[2048,256]{1,0:T(8,128)(2,1)}, bf16[2048,256]{1,0:T(8,128)(2,1)}, u32[]{:S(2)}, u32[]{:S(2)}) collective-permute-start(bf16[2048,256]{1,0:T(8,128)(2,1)} %collective-permute-done.4), channel_id=1, source_target_pairs={{0,1},{1,0},{2,3},{3,2},{4,5},{5,4},{6,7},{7,6},{8,9},{9,8},{10,11... | collective-permute-start | bytes 3145736 | tf_op jit(solution)/shard_map/ppermute | solution.py:22
  173.6 2.3 %copy-start.8 = (f32[256,256]{1,0:T(8,128)S(1)}, f32[256,256]{1,0:T(8,128)}, u32[]{:S(2)}) copy-start(f32[256,256]{1,0:T(8,128)} %param.21) | copy-start | bytes 786436
  173.6 2.3 %copy-start.9 = (f32[256,256]{1,0:T(8,128)S(1)}, f32[256,256]{1,0:T(8,128)}, u32[]{:S(2)}) copy-start(f32[256,256]{1,0:T(8,128)} %fusion.56) | copy-start | bytes 786436
  (5 other events, 9.7 us)
where the time goes:
time: 182 us; the launch traced here: 180 us
  matrix products  49.3 us (27%)
  other arithmetic  46.7 us (26%)
  starting transfers between devices  27.4 us (15%)
  local copies, waits for them, and re-layouts  23.7 us (13%)
  waiting for transfers between devices  22.2 us (12%)
  blocking collectives  6.16 us (3%)
  between operations  4.33 us (2%)
    dot_general x12, matrix products, one_block(): jnp.dot(tile.astype(jnp.bfloat16), values, preferred_element_type=jnp.flo...  33.6 us
    ppermute x18, waiting for transfers between devices, from_partner(): lax.ppermute(shard, axis, [(i, i ^ 1 << stride) for i in range(lax.axis_s...  22.2 us
    ppermute x18, starting transfers between devices, from_partner(): lax.ppermute(shard, axis, [(i, i ^ 1 << stride) for i in range(lax.axis_s...  18.3 us
    reduce_sum x12, other arithmetic, one_block(): row_norm = jnp.sum(jnp.square(row_points.astype(jnp.float32)), axis=1)  12.6 us
    all_to_all x1, starting transfers between devices, sent_to_all(): lax.all_to_all(jnp.broadcast_to(shard[None], (peers, *shard.shape)), axis...  9.14 us
    convert_element_type x10, other arithmetic, shortened(): a.astype(jnp.bfloat16)  8.33 us
    gather x1, local copies, waits for them, and re-layouts, per_device(): rhs = jnp.take(charges, order[0], axis=0)  8 us
    all_to_all x1, blocking collectives, sent_to_all(): lax.all_to_all(jnp.broadcast_to(shard[None], (peers, *shard.shape)), axis...  6.16 us
  transfers between devices with their start and end apart: 19, of which 4 were waited for; matrix products, arithmetic and copies ran while one was open for 54% of the time, Pallas kernels for 0%

commit v1 on v0

v1 whole, which is shorter than its diff:
```python
import functools

import jax
import jax.numpy as jnp
from jax import lax
from jax.experimental import pallas as pl
from jax.experimental.pallas import tpu as pltpu
from jax.sharding import PartitionSpec as P

D = 128
NRHS = 256
RANK = 256
LEAF = 2048
AXIS = "leaf"
BF = jnp.bfloat16
F32 = jnp.float32
SCALE = 4.0 / D * 1.4426950408889634
CHUNKS = ((0, 1024), (1024, 1024))


def dot(a, b):
    return lax.dot_general(a, b, (((1,), (0,)), ((), ())), preferred_element_type=F32)


def dot_t(a, b):
    return lax.dot_general(a, b, (((1,), (1,)), ((), ())), preferred_element_type=F32)


def widened(x, left):
    wide = x.astype(F32)
    rest = 0.5 * jnp.sum(wide * wide, axis=1, keepdims=True)
    high = rest.astype(BF).astype(F32)
    rest = rest - high
    middle = rest.astype(BF).astype(F32)
    low = rest - middle
    lane = lax.broadcasted_iota(jnp.int32, (x.shape[0], 128), 1)
    first, ones = (0, 3) if left else (3, 0)
    extra = jnp.where(
        lane == first, -high, jnp.where(lane == first + 1, -middle, jnp.where(lane == first + 2, -low, 0.0))
    )
    extra = jnp.where((lane >= ones) & (lane < ones + 3), 1.0, extra)
    return jnp.concatenate([x.astype(BF), extra.astype(BF)], axis=1)


def gauss(left, right):
    return jnp.exp2(dot_t(left, right) * SCALE).astype(BF)


def call(body, outs, *args, name, scratch=(), smem=0, flops=0, aliases=None):
    specs = [
        pl.BlockSpec(memory_space=pltpu.SMEM if i < smem else pltpu.VMEM) for i in range(len(args))
    ]
    return pl.pallas_call(
        body,
        out_shape=[jax.ShapeDtypeStruct(s, d) for s, d in outs],
        in_specs=specs,
        out_specs=[pl.BlockSpec(memory_space=pltpu.VMEM)] * len(outs),
        scratch_shapes=list(scratch),
        input_output_aliases=aliases or {},
        name=name,
        cost_estimate=pl.CostEstimate(flops=flops, bytes_accessed=1 << 20, transcendentals=0),
        compiler_params=pltpu.CompilerParams(vmem_limit_bytes=44 << 20),
    )(*args)


def prep_body(meta, order, points, charges, bases, lift, proxy, own_w, rhs, far, keep, send, up):
    core = meta[0]
    own_w[...] = widened(points[...], True)
    tall = jnp.concatenate([order[...].astype(F32)] * 8, axis=0).T
    places = lax.broadcasted_iota(jnp.int32, (128, LEAF), 1).astype(F32)
    for b in range(LEAF // 128):
        hot = jnp.where(tall[:, b : b + 1] == places, 1.0, 0.0).astype(BF)
        rhs[b * 128 : (b + 1) * 128, :] = dot(hot, charges[...]).astype(BF)
    coef = lax.dot_general(rhs[...], bases[...], (((0,), (0,)), ((), ())), preferred_element_type=F32)
    coef = coef.astype(BF)
    far[0:RANK, :] = coef
    far[RANK:, 0:D] = proxy[0:128, :].astype(BF)
    far[RANK:, D:] = proxy[128:256, :].astype(BF)
    up[...] = dot(coef, lift[...].astype(BF))
    keep[...] = up[pl.ds(pl.multiple_of(core * 128, 128), 128), :]
    send[...] = up[pl.ds(pl.multiple_of((1 - core) * 128, 128), 128), :].astype(BF)


def halve_body(meta, keep, got, kept, send, total):
    u = meta[1]
    total[...] = keep[...] + got[...].astype(F32)
    kept[...] = total[pl.ds(pl.multiple_of(u * 64, 64), 64), :]
    send[...] = total[pl.ds(pl.multiple_of((1 - u) * 64, 64), 64), :].astype(BF)


def node_body(meta, kept, got, stat, send, lift):
    slot = meta[3]
    for j in range(4):
        at = pl.multiple_of((slot ^ j) * 64, 64)
        lift[pl.ds(at, 64), 0:128] = stat[j, 0:64, :]
        lift[pl.ds(at, 64), 128:256] = stat[j, 64:128, :]
    node = (kept[...] + got[...].astype(F32)).astype(BF)
    send[0:64, :] = node
    send[64:128, :] = dot(node, lift[...]).astype(BF)


def pair_body(mine, got, send):
    send[0:64, :] = mine[0:64, :]
    send[64:128, :] = got[0:64, :]
    send[128:192, :] = (mine[64:128, :].astype(F32) + got[64:128, :].astype(F32)).astype(BF)


def coupling_body(meta, nodes, tops, kernel_one, kernel_two, z_node, z_top):
    slot, part = meta[3], meta[4]
    for h in range(4):
        for j in range(4):
            at = (slot ^ (2 * (h % 2)) ^ j) * 64
            z_node[pl.ds(pl.multiple_of(h * 256 + at, 64), 64), :] = nodes[4 * h + j, 0:64, :]
    for r in range(8):
        for k in range(16):
            place = (k & 1) ^ (k & 2) ^ (6 * (k // 4 % 2)) ^ (8 * (k // 8)) ^ (8 * (r % 2))
            at = (part ^ place) * 16
            z_top[pl.ds(pl.multiple_of(r * 256 + at, 16), 16), :] = tops[16 * r + k, :, :]
    own = widened(z_node[0:256, :], False)
    for h in range(1, 4):
        kernel_one[(h - 1) * 256 : h * 256, :] = gauss(widened(z_node[h * 256 : (h + 1) * 256, :], True), own)
    own = widened(z_top[0:256, :], False)
    for r in range(1, 8):
        kernel_two[(r - 1) * 256 : r * 256, :] = gauss(widened(z_top[r * 256 : (r + 1) * 256, :], True), own)


def field_body(sibs_a, sibs_b, low, high, kernel_one, kernel_two, lift, out):
    field = dot(low[64:128, :], kernel_two[0:256, :])
    for r in range(2, 8):
        part = low[r * 64 : (r + 1) * 64, :] if r < 4 else high[(r - 4) * 64 : (r - 3) * 64, :]
        field += dot(part, kernel_two[(r - 1) * 256 : r * 256, :])
    total = dot_t(field.astype(BF), lift[...])
    total += dot(sibs_a[64:128, :], kernel_one[0:256, :])
    total += dot(sibs_b[0:64, :], kernel_one[256:512, :])
    total += dot(sibs_b[64:128, :], kernel_one[512:768, :])
    out[...] = total.astype(BF)


def join_body(meta, mine, got, out):
    u = meta[1]
    out[pl.ds(pl.multiple_of(u * 64, 64), 64), :] = mine[...]
    out[pl.ds(pl.multiple_of((1 - u) * 64, 64), 64), :] = got[...]


def near_tile(own_w, other_w, values, acc, first, rows, block=512):
    for r in range(0, rows, block):
        total = None if first else acc[r : r + block, :]
        for c in range(0, other_w.shape[0], 256):
            tile = gauss(own_w[r : r + block, :], other_w[c : c + 256, :])
            part = dot(tile, values[c : c + 256, :])
            total = part if total is None else total + part
        acc[r : r + block, :] = total


def own_body(own_w, points, rhs, acc, other_w):
    other_w[...] = widened(points[...], False)
    near_tile(own_w, other_w, rhs, acc, True, own_w.shape[0])


def chunk_body(own_w, pts_a, rhs_a, pts_b, rhs_b, acc_in, acc, other_w):
    n = rhs_a.shape[0]
    other_w[0:n, :] = widened(pts_a[...], False)
    other_w[n:, :] = widened(pts_b[...], False)
    for r in range(0, LEAF, 512):
        total = acc_in[r : r + 512, :]
        for values, base in ((rhs_a, 0), (rhs_b, n)):
            for c in range(0, n, 256):
                tile = gauss(own_w[r : r + 512, :], other_w[base + c : base + c + 256, :])
                total += dot(tile, values[c : c + 256, :])
        acc[r : r + 512, :] = total


def last_body(
    meta, own_w, pts_a, rhs_a, pts_b, rhs_b, acc_in, bases, far_one, far_two, proxy, lift, half, got,
    out, other_w, far, node,
):
    n = rhs_a.shape[0]
    core = meta[0]

    @pl.when(meta[2] == 1)
    def _():
        far[...] = far_one[...]

    @pl.when(meta[2] == 0)
    def _():
        far[...] = far_two[...]

    z_far = jnp.concatenate([far[RANK:, 0:D], far[RANK:, D:]], axis=0)
    kernel = gauss(widened(z_far, True), widened(proxy[...].astype(BF), False))
    node[pl.ds(pl.multiple_of(core * 128, 128), 128), :] = half[...]
    node[pl.ds(pl.multiple_of((1 - core) * 128, 128), 128), :] = got[...]
    field = dot(far[0:RANK, :], kernel) + dot_t(node[...], lift[...].astype(BF))
    field = field.astype(BF)
    other_w[0:n, :] = widened(pts_a[...], False)
    other_w[n:, :] = widened(pts_b[...], False)
    for r in range(0, LEAF, 512):
        total = acc_in[r : r + 512, :] + dot_t(bases[r : r + 512, :], field)
        for values, base in ((rhs_a, 0), (rhs_b, n)):
            for c in range(0, n, 256):
                tile = gauss(own_w[r : r + 512, :], other_w[base + c : base + c + 256, :])
                total += dot(tile, values[c : c + 256, :])
        out[r : r + 512, :] = total.astype(BF)


def swap(x, flip):
    n = lax.axis_size(AXIS)
    return lax.ppermute(x, AXIS, [(i, i ^ flip) for i in range(n)])


def per_device(
    points, charges, order, near, bases, lift_leaf, lift_node, proxy_leaf, proxy_node, proxy_top
):
    me = lax.axis_index(AXIS)
    slot = me % 4
    x = me // 2 % 4
    far_flip = (6 - slot - near[0, 0] % 4 - near[0, 1] % 4) ^ slot
    far_core = (far_flip == 1).astype(jnp.int32)
    meta = jnp.stack([me % 2, (x % 2) ^ (x // 2), far_core, slot, me % 16]).astype(jnp.int32)

    lift_rows = lift_node.astype(BF)
    zn, zt = proxy_node.astype(BF), proxy_top.astype(BF)
    stat = jnp.concatenate([lift_rows[:, :128], lift_rows[:, 128:], zn, zt], axis=0)[None]
    stat = jnp.concatenate([stat, swap(stat, 1)], axis=0)
    stat = jnp.concatenate([stat, swap(stat, 2)], axis=0)
    own_z = stat[:, 128:]
    own_z = jnp.concatenate([own_z, swap(own_z, 6)], axis=0)
    own_z = jnp.concatenate([own_z, swap(own_z, 8)], axis=0)
    nodes, tops = own_z[:, :64], own_z[:, 64:]
    for flip in (24, 32, 96):
        tops = jnp.concatenate([tops, swap(tops, flip)], axis=0)
    kernel_one, kernel_two = call(
        coupling_body, [((768, 256), BF), ((1792, 256), BF)], meta, nodes, tops,
        name="coupling", smem=1, flops=1 << 30,
        scratch=[pltpu.VMEM((1024, 128), BF), pltpu.VMEM((2048, 128), BF)],
    )

    pts_a = swap(points, 3)
    own_w, rhs, far_out, keep, send = call(
        prep_body,
        [((LEAF, 256), BF), ((LEAF, NRHS), BF), ((384, 256), BF), ((128, 256), F32), ((128, 256), BF)],
        meta, order.reshape(16, 128), points, charges, bases, lift_leaf, proxy_leaf,
        name="prep", smem=1, flops=5 << 30, scratch=[pltpu.VMEM((256, 256), F32)],
    )

    kept, send = call(
        halve_body, [((64, 256), F32), ((64, 256), BF)], meta, keep, swap(send, 1),
        name="halve", smem=1, scratch=[pltpu.VMEM((128, 256), F32)],
    )
    send_three, lift_all = call(
        node_body, [((128, 256), BF), ((256, 256), BF)], meta, kept, swap(send, 2), stat,
        name="node", smem=1,
    )
    send_four, = call(pair_body, [((192, 256), BF)], send_three, swap(send_three, 6), name="pair")
    got_four = swap(send_four, 8)
    top = (send_four[128:].astype(F32) + got_four[128:].astype(F32)).astype(BF)
    low = jnp.concatenate([top, swap(top, 24)], axis=0)
    low = jnp.concatenate([low, swap(low, 32)], axis=0)
    high = swap(low, 96)
    quarter, = call(
        field_body, [((64, 256), BF)], send_four, got_four, low, high, kernel_one, kernel_two, lift_all,
        name="field", flops=1 << 29,
    )
    half, = call(join_body, [((128, 256), BF)], meta, quarter, swap(quarter, 2), name="join", smem=1)
    other_half = swap(half, 1)

    chosen = jnp.where(far_core == 1, pts_a, points)
    pts_b = swap(chosen, 1)
    rhs_a = [swap(rhs[s : s + n], 3) for s, n in CHUNKS]
    rhs_b = [swap(jnp.where(far_core == 1, got, rhs[s : s + n]), 1) for got, (s, n) in zip(rhs_a, CHUNKS)]
    far_one, far_two = swap(far_out, 1), swap(far_out, 2)
    acc, = call(
        own_body, [((LEAF, NRHS), F32)], own_w, points, rhs, name="near_own", flops=6 << 30,
        scratch=[pltpu.VMEM((LEAF, 256), BF)],
    )
    (s, n) = CHUNKS[0]
    acc, = call(
        chunk_body, [((LEAF, NRHS), F32)], own_w, pts_a[s : s + n], rhs_a[0], pts_b[s : s + n], rhs_b[0], acc,
        name="near_chunk", flops=6 << 30, scratch=[pltpu.VMEM((2 * n, 256), BF)], aliases={5: 0},
    )
    (s, n) = CHUNKS[1]
    out, = call(
        last_body, [((LEAF, NRHS), BF)],
        meta, own_w, pts_a[s : s + n], rhs_a[1], pts_b[s : s + n], rhs_b[1], acc, bases, far_one, far_two,
        proxy_leaf, lift_leaf, half, other_half,
        name="near_last", smem=1, flops=6 << 30,
        scratch=[pltpu.VMEM((2 * n, 256), BF), pltpu.VMEM((384, 256), BF), pltpu.VMEM((256, 256), BF)],
    )
    return out


def solution(mesh):
    spec = P(AXIS, None)
    return jax.shard_map(
        per_device, mesh=mesh, in_specs=(spec,) * 10, out_specs=spec, check_vma=False
    )
```

time: 182 us -> 91.5 us (0.50)
  matrix products: 49.3 us -> 0 us
  other arithmetic: 46.7 us -> 6.62 us
  Pallas kernels: 0 us -> 25.2 us
  waiting for transfers between devices: 22.2 us -> 5.5 us
  local copies, waits for them, and re-layouts: 23.7 us -> 9.75 us
  starting transfers between devices: 27.4 us -> 39.7 us
  blocking collectives: 6.16 us -> 0 us
    dot_general x24 -> x0, matrix products: 49.3 us -> none  [the longest x12 33.6 us: one_block(): jnp.dot(tile.astype(jnp.bfloat16), values, preferred_element_type=jnp.flo...]
    pallas_call x0 -> x10, Pallas kernels: none -> 25.2 us  [call(): pl.pallas_call(body, out_shape=[jax.ShapeDtypeStruct(s, d) for s, d in ou...]
    ppermute x18 -> x24, starting transfers between devices: 18.3 us -> 39.7 us  [swap(): return lax.ppermute(x, AXIS, [(i, i ^ flip) for i in range(n)])]
    reduce_sum x22 -> x0, other arithmetic: 19.3 us -> none  [the longest x12 12.6 us: one_block(): row_norm = jnp.sum(jnp.square(row_points.astype(jnp.float32)), axis=1)]
    ppermute x18 -> x24, waiting for transfers between devices: 22.2 us -> 5.5 us  [swap(): return lax.ppermute(x, AXIS, [(i, i ^ flip) for i in range(n)])]
    all_to_all x1 -> x0, starting transfers between devices: 9.14 us -> none  [sent_to_all(): lax.all_to_all(jnp.broadcast_to(shard[None], (peers, *shard.shape)), axis...]
    convert_element_type x16 -> x4, other arithmetic: 11.3 us -> 2.31 us  [the longest x2 1.46 us: per_device(): zn, zt = (proxy_node.astype(BF), proxy_top.astype(BF))]
    select_n x6 -> x3, other arithmetic: 9 us -> 0.22 us  [the longest x2 0.17 us: per_device(): jnp.where(far_core == 1, got, rhs[s:s + n])]
  transfers between devices with their start and end apart: 19 -> 24, of which waited for: 4 -> 5; matrix products, arithmetic and copies ran while one was open for 54% -> 7% of each run, Pallas kernels for 0% -> 20%
where the time goes in v1:
time: 91.5 us; the launch traced here: 90.7 us
  starting transfers between devices  39.7 us (43%)
  Pallas kernels  25.2 us (28%)
  local copies, waits for them, and re-layouts  9.75 us (11%)
  other arithmetic  6.62 us (7%)
  waiting for transfers between devices  5.5 us (6%)
  between operations  3.98 us (4%)
    ppermute x24, starting transfers between devices, swap(): return lax.ppermute(x, AXIS, [(i, i ^ flip) for i in range(n)])  39.7 us
    pallas_call x10, Pallas kernels, call(): pl.pallas_call(body, out_shape=[jax.ShapeDtypeStruct(s, d) for s, d in ou...  25.2 us
    unnamed x28, local copies, waits for them, and re-layouts  7.42 us
    ppermute x24, waiting for transfers between devices, swap(): return lax.ppermute(x, AXIS, [(i, i ^ flip) for i in range(n)])  5.5 us
  transfers between devices with their start and end apart: 24, of which 5 were waited for; matrix products, arithmetic and copies ran while one was open for 7% of the time, Pallas kernels for 20%

profile of v1, /device:TPU:1, one launch (start us, length us, event | category | flops | bytes accessed | tf_op | source)
XLA Modules:
  0.0 90.7 jit_solution(11510841504843035909)
XLA Ops:
  1.5 0.8 convert_element_type.22
  2.3 1.5 %collective-permute-start.10 = (bf16[1,208,128]{2,1,0:T(8,128)(2,1)S(1)}, bf16[1,208,128]{2,1,0:T(8,128)(2,1)S(1)}, u32[]{:S(2)}, u32[]{:S(2)}) collective-permute-start(bf16[1,208,128]{2,1,0:T(8,128)(2,1)S(1)} %maximum_bitcast_fusion), channel_id=1, source_target_pairs={{0,1},{1,0},{2,3},{3,2},{4,5},{5,4},{6,7},{7,6},{8,9},{9,8},{10,11... | collective-permute-start | bytes 159752 | tf_op jit(solution)/shard_map/ppermute | solution.py:207
  3.8 1.3 %fusion.3 = (s32[1,1]{1,0:T(1,128)}, s32[1,1]{1,0:T(1,128)}) fusion(s32[1,2]{1,0:T(1,128)} %param.13), kind=kLoop, calls=%fused_computation.18 | loop fusion | bytes 16 | tf_op jit(solution)/shard_map/slice | solution.py:216
  8.9 1.4 %collective-permute-start.11 = (bf16[2,208,128]{2,1,0:T(8,128)(2,1)S(1)}, bf16[2,208,128]{2,1,0:T(8,128)(2,1)S(1)}, u32[]{:S(2)}, u32[]{:S(2)}) collective-permute-start(bf16[2,208,128]{2,1,0:T(8,128)(2,1)S(1)} %pad_maximum_fusion.7), channel_id=1, source_target_pairs={{0,2},{1,3},{2,0},{3,1},{4,6},{5,7},{6,4},{7,5},{8,10},{9,11},{10,... | collective-permute-start | bytes 319496 | tf_op jit(solution)/shard_map/ppermute | solution.py:207
  10.3 1.0 %copy-done = bf16[2048,128]{1,0:T(8,128)(2,1)S(1)} copy-done((bf16[2048,128]{1,0:T(8,128)(2,1)S(1)}, bf16[2048,128]{1,0:T(8,128)(2,1)}, u32[]{:S(2)}) %copy-start) | copy-done | bytes 524312
  11.3 1.2 %copy-done.2 = bf16[2048,256]{1,0:T(8,128)(2,1)S(1)} copy-done((bf16[2048,256]{1,0:T(8,128)(2,1)S(1)}, bf16[2048,256]{1,0:T(8,128)(2,1)}, u32[]{:S(2)}) %copy-start.2) | copy-done | bytes 1048600
  12.5 1.2 %copy-done.3 = bf16[2048,256]{1,0:T(8,128)(2,1)S(1)} copy-done((bf16[2048,256]{1,0:T(8,128)(2,1)S(1)}, bf16[2048,256]{1,0:T(8,128)(2,1)}, u32[]{:S(2)}) %copy-start.3) | copy-done | bytes 1048600
  13.8 0.9 %copy-done.5 = f32[256,256]{1,0:T(8,128)S(1)} copy-done((f32[256,256]{1,0:T(8,128)S(1)}, f32[256,256]{1,0:T(8,128)}, u32[]{:S(2)}) %copy-start.5) | copy-done | bytes 262168
  14.7 0.9 copy-done.7
  16.3 3.7 %prep.1 = (bf16[2048,256]{1,0:T(8,128)(2,1)S(1)}, bf16[2048,256]{1,0:T(8,128)(2,1)S(1)}, bf16[384,256]{1,0:T(8,128)(2,1)S(1)}, f32[128,256]{1,0:T(8,128)S(1)}, bf16[128,256]{1,0:T(8,128)(2,1)S(1)}) custom-call(s32[5]{0:T(128)S(1)} %stack.23.meta, s32[16,128]{1,0:T(8,128)S(1)} %bitcast.10, bf16[2048,128]{1,0:T(8,128)(2,1)S(1)} %copy-done, ...), custom_call_target="tpu_custom_call" | custom-call | flops 5368709120 | bytes 1048576 | tf_op jit(solution)/shard_map/prep/pallas_call | solution.py:53
  20.4 1.0 %collective-permute-done.8.got = bf16[128,256]{1,0:T(8,128)(2,1)S(1)} collective-permute-done((bf16[128,256]{1,0:T(8,128)(2,1)S(1)}, bf16[128,256]{1,0:T(8,128)(2,1)S(1)}, u32[]{:S(2)}, u32[]{:S(2)}) %collective-permute-start.8) | collective-permute-done | bytes 65568 | tf_op jit(solution)/shard_map/ppermute | solution.py:207
  22.2 2.6 %collective-permute-start.17 = (bf16[4,80,128]{2,1,0:T(8,128)(2,1)S(1)}, bf16[4,80,128]{2,1,0:T(8,128)(2,1)S(1)}, u32[]{:S(2)}, u32[]{:S(2)}) collective-permute-start(bf16[4,80,128]{2,1,0:T(8,128)(2,1)S(1)} %slice.70), channel_id=1, source_target_pairs={{0,6},{1,7},{2,4},{3,5},{4,2},{5,3},{6,0},{7,1},{8,14},{9,15},{10,... | collective-permute-start | bytes 245768 | tf_op jit(solution)/shard_map/ppermute | solution.py:207
  25.6 1.7 %collective-permute-start.12 = (bf16[128,256]{1,0:T(8,128)(2,1)S(1)}, bf16[128,256]{1,0:T(8,128)(2,1)S(1)}, u32[]{:S(2)}, u32[]{:S(2)}) collective-permute-start(bf16[128,256]{1,0:T(8,128)(2,1)S(1)} %get-tuple-element.23.mine), channel_id=1, source_target_pairs={{0,6},{1,7},{2,4},{3,5},{4,2},{5,3},{6,0},{7,1},{8,14},{9,15},{10,... | collective-permute-start | bytes 196616 | tf_op jit(solution)/shard_map/ppermute | solution.py:207
  27.3 1.9 %collective-permute-start = (bf16[2048,128]{1,0:T(8,128)(2,1)S(1)}, bf16[2048,128]{1,0:T(8,128)(2,1)S(1)}, u32[]{:S(2)}, u32[]{:S(2)}) collective-permute-start(bf16[2048,128]{1,0:T(8,128)(2,1)S(1)} %copy-done.1), channel_id=1, source_target_pairs={{0,3},{1,2},{2,1},{3,0},{4,7},{5,6},{6,5},{7,4},{8,11},{9,10},{10,... | collective-permute-start | bytes 1572872 | tf_op jit(solution)/shard_map/ppermute | solution.py:207
  30.1 1.5 %collective-permute-start.6 = (bf16[384,256]{1,0:T(8,128)(2,1)S(1)}, bf16[384,256]{1,0:T(8,128)(2,1)S(1)}, u32[]{:S(2)}, u32[]{:S(2)}) collective-permute-start(bf16[384,256]{1,0:T(8,128)(2,1)S(1)} %get-tuple-element.18), channel_id=1, source_target_pairs={{0,1},{1,0},{2,3},{3,2},{4,5},{5,4},{6,7},{7,6},{8,9},{9,8},{10,11... | collective-permute-start | bytes 589832 | tf_op jit(solution)/shard_map/ppermute | solution.py:207
  31.6 1.4 %collective-permute-start.13 = (bf16[192,256]{1,0:T(8,128)(2,1)S(1)}, bf16[192,256]{1,0:T(8,128)(2,1)S(1)}, u32[]{:S(2)}, u32[]{:S(2)}) collective-permute-start(bf16[192,256]{1,0:T(8,128)(2,1)S(1)} %pair.1.sibs_a), channel_id=1, source_target_pairs={{0,8},{1,9},{2,10},{3,11},{4,12},{5,13},{6,14},{7,15},{8,0},{9,1},... | collective-permute-start | bytes 294920 | tf_op jit(solution)/shard_map/ppermute | solution.py:207
  33.9 1.6 %collective-permute-done.13.sibs_b = bf16[192,256]{1,0:T(8,128)(2,1)S(1)} collective-permute-done((bf16[192,256]{1,0:T(8,128)(2,1)S(1)}, bf16[192,256]{1,0:T(8,128)(2,1)S(1)}, u32[]{:S(2)}, u32[]{:S(2)}) %collective-permute-start.13) | collective-permute-done | bytes 98336 | tf_op jit(solution)/shard_map/ppermute | solution.py:207
  35.5 3.0 %collective-permute-start.14 = (bf16[64,256]{1,0:T(8,128)(2,1)S(1)}, bf16[64,256]{1,0:T(8,128)(2,1)}, u32[]{:S(2)}, u32[]{:S(2)}) collective-permute-start(bf16[64,256]{1,0:T(8,128)(2,1)S(1)} %add_convert_fusion), channel_id=1, source_target_pairs={{0,24},{1,25},{2,26},{3,27},{4,28},{5,29},{6,30},{7,31},{8,16},{9,... | collective-permute-start | bytes 98312 | tf_op jit(solution)/shard_map/ppermute | solution.py:207
  38.5 4.9 %near_own.1.acc_in = f32[2048,256]{1,0:T(8,128)S(1)} custom-call(bf16[2048,256]{1,0:T(8,128)(2,1)S(1)} %get-tuple-element.16.own_w, bf16[2048,128]{1,0:T(8,128)(2,1)S(1)} %copy-done.1, bf16[2048,256]{1,0:T(8,128)(2,1)S(1)} %get-tuple-element.17.rhs), custom_call_target="tpu_custom_call" | custom-call | flops 6442450944 | bytes 1048576 | tf_op jit(solution)/shard_map/near_own/pallas_call | solution.py:53
  43.4 1.3 %copy-done.10 = f32[2048,256]{1,0:T(8,128)} copy-done((f32[2048,256]{1,0:T(8,128)}, f32[2048,256]{1,0:T(8,128)S(1)}, u32[]{:S(2)}) %copy-start.10) | copy-done | bytes 2097176
  45.5 1.6 %collective-permute-start.15 = (bf16[128,256]{1,0:T(8,128)(2,1)S(1)}, bf16[128,256]{1,0:T(8,128)(2,1)S(1)}, u32[]{:S(2)}, u32[]{:S(2)}) collective-permute-start(bf16[128,256]{1,0:T(8,128)(2,1)S(1)} %pad_maximum_fusion.9), channel_id=1, source_target_pairs={{0,32},{1,33},{2,34},{3,35},{4,36},{5,37},{6,38},{7,39},{8,40},{9,... | collective-permute-start | bytes 196616 | tf_op jit(solution)/shard_map/ppermute | solution.py:207
  47.2 1.0 %pad_maximum_fusion.1 = bf16[16,80,128]{2,1,0:T(8,128)(2,1)S(1)} fusion(bf16[8,80,128]{2,1,0:T(8,128)(2,1)} %collective-permute-done.18, bf16[4,80,128]{2,1,0:T(8,128)(2,1)S(1)} %collective-permute-done.17, bf16[4,80,128]{2,1,0:T(8,128)(2,1)S(1)} %slice.70), kind=kLoop, calls=%fused_computation.4 | loop fusion | flops 327680 | bytes 655360 | tf_op jit(solution)/shard_map/concatenate | solution.py:227
  49.9 3.7 %collective-permute-start.16 = (bf16[256,256]{1,0:T(8,128)(2,1)S(1)}, bf16[256,256]{1,0:T(8,128)(2,1)S(1)}, u32[]{:S(2)}, u32[]{:S(2)}) collective-permute-start(bf16[256,256]{1,0:T(8,128)(2,1)S(1)} %pad_maximum_fusion.5.low), channel_id=1, source_target_pairs={{0,96},{1,97},{2,98},{3,99},{4,100},{5,101},{6,102},{7,103},{8,104... | collective-permute-start | bytes 393224 | tf_op jit(solution)/shard_map/ppermute | solution.py:207
  53.8 3.6 %collective-permute-start.1 = (bf16[1024,256]{1,0:T(8,128)(2,1)S(1)}, bf16[1024,256]{1,0:T(8,128)(2,1)S(1)}, u32[]{:S(2)}, u32[]{:S(2)}) collective-permute-start(bf16[1024,256]{1,0:T(8,128)(2,1)S(1)} %get-tuple-element.28), channel_id=1, source_target_pairs={{0,3},{1,2},{2,1},{3,0},{4,7},{5,6},{6,5},{7,4},{8,11},{9,10},{10,... | collective-permute-start | bytes 1572872 | tf_op jit(solution)/shard_map/ppermute | solution.py:207
  57.5 3.7 %collective-permute-start.21 = (bf16[64,16,128]{2,1,0:T(8,128)(2,1)S(1)}, bf16[64,16,128]{2,1,0:T(8,128)(2,1)S(1)}, u32[]{:S(2)}, u32[]{:S(2)}) collective-permute-start(bf16[64,16,128]{2,1,0:T(8,128)(2,1)S(1)} %pad_maximum_fusion.2), channel_id=1, source_target_pairs={{0,96},{1,97},{2,98},{3,99},{4,100},{5,101},{6,102},{7,103},{8,104... | collective-permute-start | bytes 786440 | tf_op jit(solution)/shard_map/ppermute | solution.py:207
  61.3 4.1 %collective-permute-start.2 = (bf16[2048,128]{1,0:T(8,128)(2,1)S(1)}, bf16[2048,128]{1,0:T(8,128)(2,1)S(1)}, u32[]{:S(2)}, u32[]{:S(2)}) collective-permute-start(bf16[2048,128]{1,0:T(8,128)(2,1)S(1)} %broadcast_select_fusion.2), channel_id=1, source_target_pairs={{0,1},{1,0},{2,3},{3,2},{4,5},{5,4},{6,7},{7,6},{8,9},{9,8},{10,11... | collective-permute-start | bytes 1572872 | tf_op jit(solution)/shard_map/ppermute | solution.py:207
  65.4 4.9 %collective-permute-start.5 = (bf16[1024,256]{1,0:T(8,128)(2,1)S(1)}, bf16[1024,256]{1,0:T(8,128)(2,1)S(1)}, u32[]{:S(2)}, u32[]{:S(2)}) collective-permute-start(bf16[1024,256]{1,0:T(8,128)(2,1)S(1)} %get-tuple-element.27), channel_id=1, source_target_pairs={{0,1},{1,0},{2,3},{3,2},{4,5},{5,4},{6,7},{7,6},{8,9},{9,8},{10,11... | collective-permute-start | bytes 1572872 | tf_op jit(solution)/shard_map/ppermute | solution.py:207
  70.4 1.7 %coupling.1 = (bf16[768,256]{1,0:T(8,128)(2,1)S(1)}, bf16[1792,256]{1,0:T(8,128)(2,1)S(1)}) custom-call(s32[5]{0:T(128)S(1)} %stack.23.meta, bf16[16,64,128]{2,1,0:T(8,128)(2,1)S(1)} %slice.71.nodes, bf16[128,16,128]{2,1,0:T(8,128)(2,1)S(1)} %pad_maximum_fusion.tops), custom_call_target="tpu_custom_call" | custom-call | flops 1073741824 | bytes 1048576 | tf_op jit(solution)/shard_map/coupling/pallas_call | solution.py:53
  72.9 2.6 %collective-permute-done.22.got = bf16[64,256]{1,0:T(8,128)(2,1)S(1)} collective-permute-done((bf16[64,256]{1,0:T(8,128)(2,1)S(1)}, bf16[64,256]{1,0:T(8,128)(2,1)S(1)}, u32[]{:S(2)}, u32[]{:S(2)}) %collective-permute-start.22) | collective-permute-done | bytes 32800 | tf_op jit(solution)/shard_map/ppermute | solution.py:207
  76.2 1.5 %collective-permute-start.23 = (bf16[128,256]{1,0:T(8,128)(2,1)S(1)}, bf16[128,256]{1,0:T(8,128)(2,1)S(1)}, u32[]{:S(2)}, u32[]{:S(2)}) collective-permute-start(bf16[128,256]{1,0:T(8,128)(2,1)S(1)} %join.1.half), channel_id=1, source_target_pairs={{0,1},{1,0},{2,3},{3,2},{4,5},{5,4},{6,7},{7,6},{8,9},{9,8},{10,11... | collective-permute-start | bytes 196616 | tf_op jit(solution)/shard_map/ppermute | solution.py:207
  78.2 5.1 %near_chunk.1.acc_in = f32[2048,256]{1,0:T(8,128)S(1)} custom-call(bf16[2048,256]{1,0:T(8,128)(2,1)S(1)} %copy-done.13, bf16[1024,128]{1,0:T(8,128)(2,1)S(1)} %get-tuple-element.31.pts_a, bf16[1024,256]{1,0:T(8,128)(2,1)S(1)} %collective-permute-done.4.rhs_a, bf16[1024,128]{1,0:T(8,128)(2,1)S(1)} %get-tuple-element.29.pts_b, ...), custom_call_target="tpu_custom_call", output_to_operand_aliasing={{}: (5, {})} | custom-call | flops 6442450944 | bytes 1048576 | tf_op jit(solution)/shard_map/near_chunk/pallas_call | solution.py:53
  83.4 7.3 %near_last.1 = bf16[2048,256]{1,0:T(8,128)(2,1)} custom-call(s32[5]{0:T(128)S(1)} %stack.23.meta, bf16[2048,256]{1,0:T(8,128)(2,1)S(1)} %copy-done.13, bf16[1024,128]{1,0:T(8,128)(2,1)S(1)} %get-tuple-element.32.pts_a, bf16[1024,256]{1,0:T(8,128)(2,1)S(1)} %collective-permute-done.1.rhs_a, bf16[1024,128]{1,0:T(8,128)(2,1)S(1)} %get-tuple-element.30.pts_b, ...), custom_call_target="tpu_custom_call" | custom-call | flops 6442450944 | bytes 1048576 | tf_op jit(solution)/shard_map/near_last/pallas_call | solution.py:53
  (80 shorter events, 10.8 us)
Async XLA Ops:
  2.3 6.5 %collective-permute-start.10 = (bf16[1,208,128]{2,1,0:T(8,128)(2,1)S(1)}, bf16[1,208,128]{2,1,0:T(8,128)(2,1)S(1)}, u32[]{:S(2)}, u32[]{:S(2)}) collective-permute-start(bf16[1,208,128]{2,1,0:T(8,128)(2,1)S(1)} %maximum_bitcast_fusion), channel_id=1, source_target_pairs={{0,1},{1,0},{2,3},{3,2},{4,5},{5,4},{6,7},{7,6},{8,9},{9,8},{10,11... | collective-permute-start | bytes 159752 | tf_op jit(solution)/shard_map/ppermute | solution.py:207
  8.9 13.3 %collective-permute-start.11 = (bf16[2,208,128]{2,1,0:T(8,128)(2,1)S(1)}, bf16[2,208,128]{2,1,0:T(8,128)(2,1)S(1)}, u32[]{:S(2)}, u32[]{:S(2)}) collective-permute-start(bf16[2,208,128]{2,1,0:T(8,128)(2,1)S(1)} %pad_maximum_fusion.7), channel_id=1, source_target_pairs={{0,2},{1,3},{2,0},{3,1},{4,6},{5,7},{6,4},{7,5},{8,10},{9,11},{10,... | collective-permute-start | bytes 319496 | tf_op jit(solution)/shard_map/ppermute | solution.py:207
  16.3 11.0 %copy-start.1 = (bf16[2048,128]{1,0:T(8,128)(2,1)S(1)}, bf16[2048,128]{1,0:T(8,128)(2,1)}, u32[]{:S(2)}) copy-start(bf16[2048,128]{1,0:T(8,128)(2,1)} %points.3) | copy-start | bytes 1572868
  20.0 18.5 %copy-start.12 = (bf16[2048,256]{1,0:T(8,128)(2,1)}, bf16[2048,256]{1,0:T(8,128)(2,1)S(1)}, u32[]{:S(2)}) copy-start(bf16[2048,256]{1,0:T(8,128)(2,1)S(1)} %get-tuple-element.16.own_w) | copy-start | bytes 3145732
  20.0 1.3 %collective-permute-start.8 = (bf16[128,256]{1,0:T(8,128)(2,1)S(1)}, bf16[128,256]{1,0:T(8,128)(2,1)S(1)}, u32[]{:S(2)}, u32[]{:S(2)}) collective-permute-start(bf16[128,256]{1,0:T(8,128)(2,1)S(1)} %get-tuple-element.20), channel_id=1, source_target_pairs={{0,1},{1,0},{2,3},{3,2},{4,5},{5,4},{6,7},{7,6},{8,9},{9,8},{10,11... | collective-permute-start | bytes 196616 | tf_op jit(solution)/shard_map/ppermute | solution.py:207
  21.9 2.9 %collective-permute-start.9 = (bf16[64,256]{1,0:T(8,128)(2,1)S(1)}, bf16[64,256]{1,0:T(8,128)(2,1)S(1)}, u32[]{:S(2)}, u32[]{:S(2)}) collective-permute-start(bf16[64,256]{1,0:T(8,128)(2,1)S(1)} %get-tuple-element.22), channel_id=1, source_target_pairs={{0,2},{1,3},{2,0},{3,1},{4,6},{5,7},{6,4},{7,5},{8,10},{9,11},{10,... | collective-permute-start | bytes 98312 | tf_op jit(solution)/shard_map/ppermute | solution.py:207
  22.2 10.8 %collective-permute-start.17 = (bf16[4,80,128]{2,1,0:T(8,128)(2,1)S(1)}, bf16[4,80,128]{2,1,0:T(8,128)(2,1)S(1)}, u32[]{:S(2)}, u32[]{:S(2)}) collective-permute-start(bf16[4,80,128]{2,1,0:T(8,128)(2,1)S(1)} %slice.70), channel_id=1, source_target_pairs={{0,6},{1,7},{2,4},{3,5},{4,2},{5,3},{6,0},{7,1},{8,14},{9,15},{10,... | collective-permute-start | bytes 245768 | tf_op jit(solution)/shard_map/ppermute | solution.py:207
  25.6 6.0 %collective-permute-start.12 = (bf16[128,256]{1,0:T(8,128)(2,1)S(1)}, bf16[128,256]{1,0:T(8,128)(2,1)S(1)}, u32[]{:S(2)}, u32[]{:S(2)}) collective-permute-start(bf16[128,256]{1,0:T(8,128)(2,1)S(1)} %get-tuple-element.23.mine), channel_id=1, source_target_pairs={{0,6},{1,7},{2,4},{3,5},{4,2},{5,3},{6,0},{7,1},{8,14},{9,15},{10,... | collective-permute-start | bytes 196616 | tf_op jit(solution)/shard_map/ppermute | solution.py:207
  27.3 34.0 %collective-permute-start = (bf16[2048,128]{1,0:T(8,128)(2,1)S(1)}, bf16[2048,128]{1,0:T(8,128)(2,1)S(1)}, u32[]{:S(2)}, u32[]{:S(2)}) collective-permute-start(bf16[2048,128]{1,0:T(8,128)(2,1)S(1)} %copy-done.1), channel_id=1, source_target_pairs={{0,3},{1,2},{2,1},{3,0},{4,7},{5,6},{6,5},{7,4},{8,11},{9,10},{10,... | collective-permute-start | bytes 1572872 | tf_op jit(solution)/shard_map/ppermute | solution.py:207
  30.1 23.6 %collective-permute-start.4 = (bf16[1024,256]{1,0:T(8,128)(2,1)}, bf16[1024,256]{1,0:T(8,128)(2,1)S(1)}, u32[]{:S(2)}, u32[]{:S(2)}) collective-permute-start(bf16[1024,256]{1,0:T(8,128)(2,1)} %slice.53), channel_id=1, source_target_pairs={{0,3},{1,2},{2,1},{3,0},{4,7},{5,6},{6,5},{7,4},{8,11},{9,10},{10,... | collective-permute-start | bytes 1572872 | tf_op jit(solution)/shard_map/ppermute | solution.py:207
  30.1 53.3 %collective-permute-start.6 = (bf16[384,256]{1,0:T(8,128)(2,1)S(1)}, bf16[384,256]{1,0:T(8,128)(2,1)S(1)}, u32[]{:S(2)}, u32[]{:S(2)}) collective-permute-start(bf16[384,256]{1,0:T(8,128)(2,1)S(1)} %get-tuple-element.18), channel_id=1, source_target_pairs={{0,1},{1,0},{2,3},{3,2},{4,5},{5,4},{6,7},{7,6},{8,9},{9,8},{10,11... | collective-permute-start | bytes 589832 | tf_op jit(solution)/shard_map/ppermute | solution.py:207
  31.6 3.8 %collective-permute-start.13 = (bf16[192,256]{1,0:T(8,128)(2,1)S(1)}, bf16[192,256]{1,0:T(8,128)(2,1)S(1)}, u32[]{:S(2)}, u32[]{:S(2)}) collective-permute-start(bf16[192,256]{1,0:T(8,128)(2,1)S(1)} %pair.1.sibs_a), channel_id=1, source_target_pairs={{0,8},{1,9},{2,10},{3,11},{4,12},{5,13},{6,14},{7,15},{8,0},{9,1},... | collective-permute-start | bytes 294920 | tf_op jit(solution)/shard_map/ppermute | solution.py:207
  33.7 13.5 %collective-permute-start.18 = (bf16[8,80,128]{2,1,0:T(8,128)(2,1)}, bf16[8,80,128]{2,1,0:T(8,128)(2,1)}, u32[]{:S(2)}, u32[]{:S(2)}) collective-permute-start(bf16[8,80,128]{2,1,0:T(8,128)(2,1)} %pad_maximum_fusion.4), channel_id=1, source_target_pairs={{0,8},{1,9},{2,10},{3,11},{4,12},{5,13},{6,14},{7,15},{8,0},{9,1},... | collective-permute-start | bytes 491528 | tf_op jit(solution)/shard_map/ppermute | solution.py:207
  35.5 9.3 %collective-permute-start.14 = (bf16[64,256]{1,0:T(8,128)(2,1)S(1)}, bf16[64,256]{1,0:T(8,128)(2,1)}, u32[]{:S(2)}, u32[]{:S(2)}) collective-permute-start(bf16[64,256]{1,0:T(8,128)(2,1)S(1)} %add_convert_fusion), channel_id=1, source_target_pairs={{0,24},{1,25},{2,26},{3,27},{4,28},{5,29},{6,30},{7,31},{8,16},{9,... | collective-permute-start | bytes 98312 | tf_op jit(solution)/shard_map/ppermute | solution.py:207
  43.4 1.3 %copy-start.10 = (f32[2048,256]{1,0:T(8,128)}, f32[2048,256]{1,0:T(8,128)S(1)}, u32[]{:S(2)}) copy-start(f32[2048,256]{1,0:T(8,128)S(1)} %near_own.1.acc_in) | copy-start | bytes 6291460
  45.5 3.6 %collective-permute-start.15 = (bf16[128,256]{1,0:T(8,128)(2,1)S(1)}, bf16[128,256]{1,0:T(8,128)(2,1)S(1)}, u32[]{:S(2)}, u32[]{:S(2)}) collective-permute-start(bf16[128,256]{1,0:T(8,128)(2,1)S(1)} %pad_maximum_fusion.9), channel_id=1, source_target_pairs={{0,32},{1,33},{2,34},{3,35},{4,36},{5,37},{6,38},{7,39},{8,40},{9,... | collective-permute-start | bytes 196616 | tf_op jit(solution)/shard_map/ppermute | solution.py:207
  48.9 4.6 %collective-permute-start.19 = (bf16[16,16,128]{2,1,0:T(8,128)(2,1)S(1)}, bf16[16,16,128]{2,1,0:T(8,128)(2,1)S(1)}, u32[]{:S(2)}, u32[]{:S(2)}) collective-permute-start(bf16[16,16,128]{2,1,0:T(8,128)(2,1)S(1)} %pad_maximum_fusion.8), channel_id=1, source_target_pairs={{0,24},{1,25},{2,26},{3,27},{4,28},{5,29},{6,30},{7,31},{8,16},{9,... | collective-permute-start | bytes 196616 | tf_op jit(solution)/shard_map/ppermute | solution.py:207
  49.9 22.2 %collective-permute-start.16 = (bf16[256,256]{1,0:T(8,128)(2,1)S(1)}, bf16[256,256]{1,0:T(8,128)(2,1)S(1)}, u32[]{:S(2)}, u32[]{:S(2)}) collective-permute-start(bf16[256,256]{1,0:T(8,128)(2,1)S(1)} %pad_maximum_fusion.5.low), channel_id=1, source_target_pairs={{0,96},{1,97},{2,98},{3,99},{4,100},{5,101},{6,102},{7,103},{8,104... | collective-permute-start | bytes 393224 | tf_op jit(solution)/shard_map/ppermute | solution.py:207
  53.6 3.9 %collective-permute-start.20 = (bf16[32,16,128]{2,1,0:T(8,128)(2,1)S(1)}, bf16[32,16,128]{2,1,0:T(8,128)(2,1)S(1)}, u32[]{:S(2)}, u32[]{:S(2)}) collective-permute-start(bf16[32,16,128]{2,1,0:T(8,128)(2,1)S(1)} %pad_maximum_fusion.6), channel_id=1, source_target_pairs={{0,32},{1,33},{2,34},{3,35},{4,36},{5,37},{6,38},{7,39},{8,40},{9,... | collective-permute-start | bytes 393224 | tf_op jit(solution)/shard_map/ppermute | solution.py:207
  53.8 22.4 %collective-permute-start.1 = (bf16[1024,256]{1,0:T(8,128)(2,1)S(1)}, bf16[1024,256]{1,0:T(8,128)(2,1)S(1)}, u32[]{:S(2)}, u32[]{:S(2)}) collective-permute-start(bf16[1024,256]{1,0:T(8,128)(2,1)S(1)} %get-tuple-element.28), channel_id=1, source_target_pairs={{0,3},{1,2},{2,1},{3,0},{4,7},{5,6},{6,5},{7,4},{8,11},{9,10},{10,... | collective-permute-start | bytes 1572872 | tf_op jit(solution)/shard_map/ppermute | solution.py:207
  57.5 7.9 %collective-permute-start.21 = (bf16[64,16,128]{2,1,0:T(8,128)(2,1)S(1)}, bf16[64,16,128]{2,1,0:T(8,128)(2,1)S(1)}, u32[]{:S(2)}, u32[]{:S(2)}) collective-permute-start(bf16[64,16,128]{2,1,0:T(8,128)(2,1)S(1)} %pad_maximum_fusion.2), channel_id=1, source_target_pairs={{0,96},{1,97},{2,98},{3,99},{4,100},{5,101},{6,102},{7,103},{8,104... | collective-permute-start | bytes 786440 | tf_op jit(solution)/shard_map/ppermute | solution.py:207
  61.3 16.5 %collective-permute-start.2 = (bf16[2048,128]{1,0:T(8,128)(2,1)S(1)}, bf16[2048,128]{1,0:T(8,128)(2,1)S(1)}, u32[]{:S(2)}, u32[]{:S(2)}) collective-permute-start(bf16[2048,128]{1,0:T(8,128)(2,1)S(1)} %broadcast_select_fusion.2), channel_id=1, source_target_pairs={{0,1},{1,0},{2,3},{3,2},{4,5},{5,4},{6,7},{7,6},{8,9},{9,8},{10,11... | collective-permute-start | bytes 1572872 | tf_op jit(solution)/shard_map/ppermute | solution.py:207
  65.4 12.8 %collective-permute-start.5 = (bf16[1024,256]{1,0:T(8,128)(2,1)S(1)}, bf16[1024,256]{1,0:T(8,128)(2,1)S(1)}, u32[]{:S(2)}, u32[]{:S(2)}) collective-permute-start(bf16[1024,256]{1,0:T(8,128)(2,1)S(1)} %get-tuple-element.27), channel_id=1, source_target_pairs={{0,1},{1,0},{2,3},{3,2},{4,5},{5,4},{6,7},{7,6},{8,9},{9,8},{10,11... | collective-permute-start | bytes 1572872 | tf_op jit(solution)/shard_map/ppermute | solution.py:207
  72.7 5.5 %copy-start.11 = (f32[2048,256]{1,0:T(8,128)S(1)}, f32[2048,256]{1,0:T(8,128)}, u32[]{:S(2)}) copy-start(f32[2048,256]{1,0:T(8,128)} %copy-done.10) | copy-start | bytes 6291460
  72.7 5.5 %copy-start.13 = (bf16[2048,256]{1,0:T(8,128)(2,1)S(1)}, bf16[2048,256]{1,0:T(8,128)(2,1)}, u32[]{:S(2)}) copy-start(bf16[2048,256]{1,0:T(8,128)(2,1)} %copy-done.12) | copy-start | bytes 3145732
  72.7 2.8 %collective-permute-start.22 = (bf16[64,256]{1,0:T(8,128)(2,1)S(1)}, bf16[64,256]{1,0:T(8,128)(2,1)S(1)}, u32[]{:S(2)}, u32[]{:S(2)}) collective-permute-start(bf16[64,256]{1,0:T(8,128)(2,1)S(1)} %field.1.mine), channel_id=1, source_target_pairs={{0,2},{1,3},{2,0},{3,1},{4,6},{5,7},{6,4},{7,5},{8,10},{9,11},{10,... | collective-permute-start | bytes 98312 | tf_op jit(solution)/shard_map/ppermute | solution.py:207
  75.5 7.8 %collective-permute-start.7 = (bf16[384,256]{1,0:T(8,128)(2,1)S(1)}, bf16[384,256]{1,0:T(8,128)(2,1)S(1)}, u32[]{:S(2)}, u32[]{:S(2)}) collective-permute-start(bf16[384,256]{1,0:T(8,128)(2,1)S(1)} %get-tuple-element.18), channel_id=1, source_target_pairs={{0,2},{1,3},{2,0},{3,1},{4,6},{5,7},{6,4},{7,5},{8,10},{9,11},{10,... | collective-permute-start | bytes 589832 | tf_op jit(solution)/shard_map/ppermute | solution.py:207
  76.2 7.2 %collective-permute-start.23 = (bf16[128,256]{1,0:T(8,128)(2,1)S(1)}, bf16[128,256]{1,0:T(8,128)(2,1)S(1)}, u32[]{:S(2)}, u32[]{:S(2)}) collective-permute-start(bf16[128,256]{1,0:T(8,128)(2,1)S(1)} %join.1.half), channel_id=1, source_target_pairs={{0,1},{1,0},{2,3},{3,2},{4,5},{5,4},{6,7},{7,6},{8,9},{9,8},{10,11... | collective-permute-start | bytes 196616 | tf_op jit(solution)/shard_map/ppermute | solution.py:207
  77.8 5.6 %collective-permute-start.3 = (bf16[1024,256]{1,0:T(8,128)(2,1)S(1)}, bf16[1024,256]{1,0:T(8,128)(2,1)S(1)}, u32[]{:S(2)}, u32[]{:S(2)}) collective-permute-start(bf16[1024,256]{1,0:T(8,128)(2,1)S(1)} %broadcast_select_fusion.1), channel_id=1, source_target_pairs={{0,1},{1,0},{2,3},{3,2},{4,5},{5,4},{6,7},{7,6},{8,9},{9,8},{10,11... | collective-permute-start | bytes 1572872 | tf_op jit(solution)/shard_map/ppermute | solution.py:207
  78.2 5.2 %copy-start.4 = (bf16[2048,256]{1,0:T(8,128)(2,1)S(1)}, bf16[2048,256]{1,0:T(8,128)(2,1)}, u32[]{:S(2)}) copy-start(bf16[2048,256]{1,0:T(8,128)(2,1)} %bases.3) | copy-start | bytes 3145732
  78.2 5.2 %copy-start.6 = (f32[256,256]{1,0:T(8,128)S(1)}, f32[256,256]{1,0:T(8,128)}, u32[]{:S(2)}) copy-start(f32[256,256]{1,0:T(8,128)} %lift.3) | copy-start | bytes 786436
  78.2 5.2 %copy-start.8 = (f32[256,128]{1,0:T(8,128)S(1)}, f32[256,128]{1,0:T(8,128)}, u32[]{:S(2)}) copy-start(f32[256,128]{1,0:T(8,128)} %proxy.3) | copy-start | bytes 393220
  (6 other events, 6.0 us)

commit v2 on v1

v2 whole, which is shorter than its diff:
```python
import functools

import jax
import jax.numpy as jnp
from jax import lax
from jax.experimental import pallas as pl
from jax.experimental.pallas import tpu as pltpu
from jax.sharding import PartitionSpec as P

D = 128
NRHS = 256
RANK = 256
LEAF = 2048
AXIS = "leaf"
BF = jnp.bfloat16
F32 = jnp.float32
SCALE = 4.0 / D * 1.4426950408889634
FAR = 384
CHUNKS = ((0, 512), (512, 512), (1024, 512), (1536, 512))
BASES = (0, FAR, 0, 0)
HALF = LEAF // 2


def dot(a, b):
    return lax.dot_general(a, b, (((1,), (0,)), ((), ())), preferred_element_type=F32)


def dot_t(a, b):
    return lax.dot_general(a, b, (((1,), (1,)), ((), ())), preferred_element_type=F32)


def widened(x, left):
    wide = x.astype(F32)
    rest = 0.5 * jnp.sum(wide * wide, axis=1, keepdims=True)
    high = rest.astype(BF).astype(F32)
    rest = rest - high
    middle = rest.astype(BF).astype(F32)
    low = rest - middle
    lane = lax.broadcasted_iota(jnp.int32, (x.shape[0], 128), 1)
    first, ones = (0, 3) if left else (3, 0)
    extra = jnp.where(
        lane == first, -high, jnp.where(lane == first + 1, -middle, jnp.where(lane == first + 2, -low, 0.0))
    )
    extra = jnp.where((lane >= ones) & (lane < ones + 3), 1.0, extra)
    return jnp.concatenate([x.astype(BF), extra.astype(BF)], axis=1)


def gauss(left, right):
    return jnp.exp2(dot_t(left, right) * SCALE).astype(BF)


def call(body, outs, *args, name, scratch=(), smem=0, hbm=(), aliases=None, limit=24):
    def space(i):
        return pltpu.SMEM if i < smem else pltpu.HBM if i in hbm else pltpu.VMEM

    args = [
        pltpu.with_memory_space_constraint(arg, pltpu.HBM) if i in hbm else arg for i, arg in enumerate(args)
    ]
    return pl.pallas_call(
        body,
        out_shape=[jax.ShapeDtypeStruct(s, d) for s, d in outs],
        in_specs=[pl.BlockSpec(memory_space=space(i)) for i in range(len(args))],
        out_specs=[pl.BlockSpec(memory_space=pltpu.VMEM)] * len(outs),
        scratch_shapes=list(scratch),
        input_output_aliases=aliases or {},
        name=name,
        cost_estimate=pl.CostEstimate(flops=0, bytes_accessed=0, transcendentals=0),
        compiler_params=pltpu.CompilerParams(vmem_limit_bytes=limit << 20),
    )(*args)


def place():
    me = lax.axis_index(AXIS)
    x = lax.rem(lax.div(me, 2), 4)
    return lax.rem(me, 2), lax.rem(x, 2) ^ lax.div(x, 2), lax.rem(me, 4), lax.rem(me, 16)


def far_is_core(near):
    slot = place()[2]
    return ((6 - slot - lax.rem(near[0, 0], 4) - lax.rem(near[0, 1], 4)) ^ slot) == 1


def choose_body(skip, near, got, own, out):
    core = far_is_core(near)

    @pl.when(core)
    def _():
        out[skip:, :] = got[skip:, :]
        if skip:
            out[0:skip, :] = own[0:skip, :]

    @pl.when(jnp.logical_not(core))
    def _():
        out[skip:, :] = own[skip:, :]
        if skip:
            out[0:skip, :] = got[0:skip, :]


def fetched(pairs, sems):
    copies = [pltpu.make_async_copy(src, dst, sems.at[i]) for i, (src, dst) in enumerate(pairs)]
    for copy in copies:
        copy.start()
    return copies


def pack_body(lift_h, node_h, top_h, out, lift, node, top, sems):
    for copy in fetched(((lift_h, lift), (node_h, node), (top_h, top)), sems):
        copy.wait()
    out[0:64, :] = lift[:, 0:128].astype(BF)
    out[64:128, :] = lift[:, 128:256].astype(BF)
    out[128:192, :] = node[...].astype(BF)
    out[192:208, :] = top[...].astype(BF)


def cat_body(one, two, out):
    n = one.shape[0]
    out[0:n] = one[...]
    out[n:] = two[...]


def cat_z_body(a, b, c, d, out):
    for j, stat in enumerate((a, b, c, d)):
        out[j] = stat[128:, :]


def tops_body(z_a, z_b, out):
    out[0:8] = z_a[:, 64:, :]
    out[8:16] = z_b[:, 64:, :]


def prep_body(
    order, points_h, charges_h, bases_h, lift_h, proxy_h,
    own_l, own_r, buf_zero, buf_one, buf_two, buf_three, keep, send,
    points, charges, bases, lift, proxy, up, sems,
):
    core = place()[0]
    pairs = ((charges_h, charges), (points_h, points), (bases_h, bases), (lift_h, lift), (proxy_h, proxy))
    copies = fetched(pairs, sems)
    rows = [order[:, b * 128 : (b + 1) * 128] for b in range(LEAF // 128)]
    tall = jnp.concatenate(rows * (128 // len(rows)), axis=0).astype(F32).T
    places = lax.broadcasted_iota(jnp.int32, (128, LEAF), 1).astype(F32)
    copies[0].wait()
    coef = None
    for i, (buf, (start, n)) in enumerate(zip((buf_zero, buf_one, buf_two, buf_three), CHUNKS)):
        base = BASES[i]
        for b in range(n // 128):
            at = start // 128 + b
            hot = jnp.where(tall[:, at : at + 1] == places, 1.0, 0.0).astype(BF)
            buf[base + b * 128 : base + (b + 1) * 128, :] = dot(hot, charges[...]).astype(BF)
        if i == 0:
            copies[1].wait()
            copies[2].wait()
        part = lax.dot_general(
            buf[base : base + n, :], bases[start : start + n, :], (((0,), (0,)), ((), ())),
            preferred_element_type=F32,
        )
        coef = part if coef is None else coef + part
    copies[3].wait()
    copies[4].wait()
    coef = coef.astype(BF)
    buf_one[0:RANK, :] = coef
    buf_one[RANK:FAR, 0:D] = proxy[0:128, :].astype(BF)
    buf_one[RANK:FAR, D:] = proxy[128:256, :].astype(BF)
    up[...] = dot(coef, lift[...].astype(BF))
    keep[...] = up[pl.ds(pl.multiple_of(core * 128, 128), 128), :]
    send[...] = up[pl.ds(pl.multiple_of((1 - core) * 128, 128), 128), :].astype(BF)
    own_l[...] = widened(points[...], True)
    own_r[...] = widened(points[...], False)


def halve_body(keep, got, kept, send, total):
    u = place()[1]
    total[...] = keep[...] + got[...].astype(F32)
    kept[...] = total[pl.ds(pl.multiple_of(u * 64, 64), 64), :]
    send[...] = total[pl.ds(pl.multiple_of((1 - u) * 64, 64), 64), :].astype(BF)


def node_body(kept, got, stat_a, stat_b, stat_c, stat_d, send, lift):
    slot = place()[2]
    for j, stat in enumerate((stat_a, stat_b, stat_c, stat_d)):
        at = pl.multiple_of((slot ^ j) * 64, 64)
        lift[pl.ds(at, 64), 0:128] = stat[0:64, :]
        lift[pl.ds(at, 64), 128:256] = stat[64:128, :]
    node = (kept[...] + got[...].astype(F32)).astype(BF)
    send[0:64, :] = node
    send[64:128, :] = dot(node, lift[...]).astype(BF)


def pair_body(mine, got, send):
    send[0:64, :] = mine[0:64, :]
    send[64:128, :] = got[0:64, :]
    send[128:192, :] = (mine[64:128, :].astype(F32) + got[64:128, :].astype(F32)).astype(BF)


def top_body(mine, got, out):
    out[...] = (mine[128:192, :].astype(F32) + got[128:192, :].astype(F32)).astype(BF)


def node_coupling_body(nodes_a, nodes_b, out, z_node):
    slot = place()[2]
    for h in range(4):
        nodes = nodes_a if h < 2 else nodes_b
        for j in range(4):
            at = (slot ^ (2 * (h % 2)) ^ j) * 64
            z_node[pl.ds(pl.multiple_of(h * 256 + at, 64), 64), :] = nodes[4 * (h % 2) + j, 0:64, :]
    own = widened(z_node[0:256, :], False)
    for h in range(1, 4):
        out[(h - 1) * 256 : h * 256, :] = gauss(widened(z_node[h * 256 : (h + 1) * 256, :], True), own)


def top_coupling_body(tops_a, tops_b, out, z_top):
    part = place()[3]
    for r in range(8):
        tops = tops_a if r < 4 else tops_b
        for k in range(16):
            offset = (k & 1) ^ (k & 2) ^ (6 * (k // 4 % 2)) ^ (8 * (k // 8)) ^ (8 * (r % 2))
            at = (part ^ offset) * 16
            z_top[pl.ds(pl.multiple_of(r * 256 + at, 16), 16), :] = tops[16 * (r % 4) + k, :, :]
    own = widened(z_top[0:256, :], False)
    for r in range(1, 8):
        out[(r - 1) * 256 : r * 256, :] = gauss(widened(z_top[r * 256 : (r + 1) * 256, :], True), own)


def field_body(sibs_a, sibs_b, low, high, kernel_one, kernel_two, lift, out):
    field = dot(low[64:128, :], kernel_two[0:256, :])
    for r in range(2, 8):
        part = low[r * 64 : (r + 1) * 64, :] if r < 4 else high[(r - 4) * 64 : (r - 3) * 64, :]
        field += dot(part, kernel_two[(r - 1) * 256 : r * 256, :])
    total = dot_t(field.astype(BF), lift[...])
    total += dot(sibs_a[64:128, :], kernel_one[0:256, :])
    total += dot(sibs_b[0:64, :], kernel_one[256:512, :])
    total += dot(sibs_b[64:128, :], kernel_one[512:768, :])
    out[...] = total.astype(BF)


def join_body(mine, got, out):
    u = place()[1]
    out[pl.ds(pl.multiple_of(u * 64, 64), 64), :] = mine[...]
    out[pl.ds(pl.multiple_of((1 - u) * 64, 64), 64), :] = got[...]


def add_near(total, left, right, values, base, n):
    for c in range(0, n, 256):
        tile = gauss(left, right[c : c + 256, :])
        part = dot(tile, values[base + c : base + c + 256, :])
        total = part if total is None else total + part
    return total


def own_body(first, own_l, own_r, buf_zero, buf_one, buf_two, buf_three, acc):
    for r in range(0, HALF, 512):
        left = own_l[first + r : first + r + 512, :]
        total = None
        for values, (start, n), base in zip((buf_zero, buf_one, buf_two, buf_three), CHUNKS, BASES):
            total = add_near(total, left, own_r.at[start : start + n, :], values, base, n)
        acc[r : r + 512, :] = total


def chunk_body(i, own_l, pts_a, rhs_a, pts_b, rhs_b, in_a, in_b, acc_a, acc_b, right):
    (start, n), base = CHUNKS[i], BASES[i]
    right[0:n, :] = widened(pts_a[start : start + n, :], False)
    right[n:, :] = widened(pts_b[start : start + n, :], False)
    for r in range(0, LEAF, 512):
        acc_in, acc = (in_a, acc_a) if r < HALF else (in_b, acc_b)
        rows = slice(r % HALF, r % HALF + 512)
        left = own_l[r : r + 512, :]
        total = add_near(acc_in[rows, :], left, right.at[0:n, :], rhs_a, base, n)
        acc[rows, :] = add_near(total, left, right.at[n : 2 * n, :], rhs_b, base, n)


def last_body(
    own_l, pts_a, rhs_a, pts_b, rhs_b, acc_a, acc_b, bases, far, proxy, lift, half, got,
    out, right, node,
):
    start, n = CHUNKS[3]
    core = place()[0]
    z_far = jnp.concatenate([far[RANK:FAR, 0:D], far[RANK:FAR, D:]], axis=0)
    kernel = gauss(widened(z_far, True), widened(proxy[...].astype(BF), False))
    node[pl.ds(pl.multiple_of(core * 128, 128), 128), :] = half[...]
    node[pl.ds(pl.multiple_of((1 - core) * 128, 128), 128), :] = got[...]
    field = dot(far[0:RANK, :], kernel) + dot_t(node[...], lift[...].astype(BF))
    field = field.astype(BF)
    right[0:n, :] = widened(pts_a[start : start + n, :], False)
    right[n:, :] = widened(pts_b[start : start + n, :], False)
    for r in range(0, LEAF, 512):
        left = own_l[r : r + 512, :]
        acc = acc_a if r < HALF else acc_b
        total = acc[r % HALF : r % HALF + 512, :] + dot_t(bases[r : r + 512, :], field)
        total = add_near(total, left, right.at[0:n, :], rhs_a, 0, n)
        total = add_near(total, left, right.at[n : 2 * n, :], rhs_b, 0, n)
        out[r : r + 512, :] = total.astype(BF)


def after(x, token):
    return lax.optimization_barrier((x, token))[0]


def swap(x, flip):
    n = lax.axis_size(AXIS)
    return lax.ppermute(x, AXIS, [(i, i ^ flip) for i in range(n)])


def per_device(
    points, charges, order, near, bases, lift_leaf, lift_node, proxy_leaf, proxy_node, proxy_top
):
    vm, sem = pltpu.VMEM, pltpu.SemaphoreType.DMA

    def choose(got, own, skip=0):
        return call(
            functools.partial(choose_body, skip), [(own.shape, BF)], near, got, own, name="choose", smem=1
        )[0]

    def chunk(i, v):
        n = CHUNKS[i][1]
        return call(
            functools.partial(chunk_body, i), [((HALF, NRHS), F32)] * 2,
            v["own_l"], v["pts_a"], v["far_rows", i], v["pts_b"], v["near_rows", i], v["acc", 0], v["acc", 1],
            name="near_chunk", scratch=[vm((2 * n, 256), BF)], aliases={5: 0, 6: 1},
        )

    def own_half(i, v):
        return call(
            functools.partial(own_body, i * HALF), [((HALF, NRHS), F32)],
            v["own_l"], v["own_r"], *[v["buf", j] for j in range(4)], name="near_own",
        )[0]

    def cat(one, two):
        shape = (2 * one.shape[0], *one.shape[1:])
        return call(cat_body, [(shape, BF)], one, two, name="join_rows")[0]

    v = {}

    def finish(**new):
        v.update(new)
        keys = list(v)
        for key, value in zip(keys, lax.optimization_barrier([v[key] for key in keys])):
            v[key] = value

    stat, = call(
        pack_body, [((208, 128), BF)], lift_node, proxy_node, proxy_top, name="pack", hbm=(0, 1, 2),
        scratch=[vm((64, 256), F32), vm((64, 128), F32), vm((16, 128), F32), sem((3,))],
    )
    finish(stat=stat, order=order, points=points)

    stats = [v["stat"]] + [swap(v["stat"], k) for k in (1, 2, 3)]
    across_a = swap(v["points"][:HALF], 3)
    own_l, own_r, *bufs, keep, send = call(
        prep_body,
        [((LEAF, 256), BF), ((LEAF, 256), BF)]
        + [((base + n, 256), BF) for (_, n), base in zip(CHUNKS, BASES)]
        + [((128, 256), F32), ((128, 256), BF)],
        v["order"], points, charges, bases, lift_leaf, proxy_leaf,
        name="prep", hbm=(1, 2, 3, 4, 5),
        scratch=[
            vm((LEAF, D), BF), vm((LEAF, 256), BF), vm((LEAF, 256), BF), vm((256, 256), F32),
            vm((256, 128), F32), vm((256, 256), F32), sem((5,)),
        ],
    )
    v.update({("buf", i): buf for i, buf in enumerate(bufs)})
    finish(stats=tuple(stats), own_l=own_l, own_r=own_r, keep=keep, send=send)

    got = swap(v["send"], 1)
    z_a, = call(cat_z_body, [((4, 80, 128), BF)], *v["stats"], name="cat_z")
    z_b = swap(z_a, 6)
    finish(got=got, z_a=z_a)

    kept, send = call(
        halve_body, [((64, 256), F32), ((64, 256), BF)], v["keep"], v["got"],
        name="halve", scratch=[vm((128, 256), F32)],
    )
    got = swap(send, 2)
    v["acc", 0] = own_half(0, v)
    across_b = swap(after(v["points"], v["acc", 0])[HALF:], 3)
    finish(got=got, kept=kept, z_b=z_b, across_a=across_a)

    send, lift_all = call(
        node_body, [((128, 256), BF), ((256, 256), BF)], v["kept"], v["got"], *v["stats"], name="node",
    )
    got = swap(send, 6)
    z_c = cat(v["z_a"], v["z_b"])
    z_d = swap(z_c, 8)
    rows = [swap(v["buf", 0], 3)]
    v["acc", 1] = own_half(1, v)
    finish(got=got, send=send, lift_all=lift_all, z_c=z_c, z_d=z_d)

    send, = call(pair_body, [((192, 256), BF)], v["send"], v["got"], name="pair")
    got = swap(send, 8)
    t_a, = call(tops_body, [((16, 16, 128), BF)], v["z_c"], v["z_d"], name="tops")
    t_b = swap(t_a, 24)
    rows.append(swap(v["buf", 1], 3))
    kernel_one, = call(
        node_coupling_body, [((768, 256), BF)], v["z_c"], v["z_d"], name="node_coupling",
        scratch=[vm((1024, 128), BF)],
    )
    pts_a = jnp.concatenate([v["across_a"], across_b], axis=0)
    pts_b = swap(choose(pts_a, v["points"]), 1)
    finish(send_four=send, got_four=got, t_a=t_a, t_b=t_b, kernel_one=kernel_one, pts_a=pts_a)

    top, = call(top_body, [((64, 256), BF)], v["send_four"], v["got_four"], name="top")
    got = swap(top, 24)
    t_a = cat(v["t_a"], v["t_b"])
    t_b = swap(t_a, 32)
    rows.append(swap(v["buf", 2], 3))
    near_rows = [swap(choose(rows[0], v["buf", 0], BASES[0]), 1)]
    v["far_rows", 0] = rows[0]
    finish(got=got, low=top, t_a=t_a, t_b=t_b, pts_b=pts_b)

    low = cat(v["low"], v["got"])
    got = swap(low, 32)
    t_a = cat(v["t_a"], v["t_b"])
    t_b = swap(t_a, 96)
    rows.append(swap(v["buf", 3], 3))
    v["near_rows", 0] = near_rows[0]
    v["acc", 0], v["acc", 1] = chunk(0, v)
    finish(got=got, low=low, t_a=t_a, t_b=t_b)

    low = cat(v["low"], v["got"])
    got = swap(low, 96)
    kernel_two, = call(
        top_coupling_body, [((1792, 256), BF)], v["t_a"], v["t_b"], name="top_coupling",
        scratch=[vm((2048, 128), BF)],
    )
    near_rows.append(swap(choose(rows[1], v["buf", 1], BASES[1]), 1))
    v["far_rows", 1] = rows[1]
    finish(got=got, low=low, kernel_two=kernel_two)

    quarter, = call(
        field_body, [((64, 256), BF)], v["send_four"], v["got_four"], v["low"], v["got"],
        v["kernel_one"], v["kernel_two"], v["lift_all"], name="field",
    )
    got = swap(quarter, 2)
    v["near_rows", 1] = near_rows[1]
    v["acc", 0], v["acc", 1] = chunk(1, v)
    near_rows.append(swap(choose(rows[2], v["buf", 2], BASES[2]), 1))
    v["far_rows", 2] = rows[2]
    finish(got=got, quarter=quarter)

    half, = call(join_body, [((128, 256), BF)], v["quarter"], v["got"], name="join")
    got = swap(half, 1)
    v["near_rows", 2] = near_rows[2]
    v["acc", 0], v["acc", 1] = chunk(2, v)
    near_rows.append(swap(choose(rows[3], v["buf", 3], BASES[3]), 1))
    finish(got=got, half=half)

    n = CHUNKS[3][1]
    out, = call(
        last_body, [((LEAF, NRHS), BF)],
        v["own_l"], v["pts_a"], rows[3], v["pts_b"], near_rows[3], v["acc", 0], v["acc", 1], bases,
        v["near_rows", 1], proxy_leaf, lift_leaf, v["half"], v["got"],
        name="near_last", scratch=[vm((2 * n, 256), BF), vm((256, 256), BF)],
    )
    return out


def solution(mesh):
    spec = P(AXIS, None)
    return jax.shard_map(
        per_device, mesh=mesh, in_specs=(spec,) * 10, out_specs=spec, check_vma=False
    )
```

time: 91.5 us -> 79.1 us (0.86)
  local copies, waits for them, and re-layouts: 9.75 us -> 1.08 us
  other arithmetic: 6.62 us -> 0 us
  Pallas kernels: 25.2 us -> 30.1 us
  between operations: 3.98 us -> 0.35 us
  waiting for transfers between devices: 5.5 us -> 9.04 us
  starting transfers between devices: 39.7 us -> 38.4 us
    unnamed x28 -> x13, local copies, waits for them, and re-layouts: 7.42 us -> 0.06 us
    pallas_call x10 -> x28, Pallas kernels: 25.2 us -> 30.1 us  [call(): pl.pallas_call(body, out_shape=[jax.ShapeDtypeStruct(s, d) for s, d in ou...]
    ppermute x24 -> x28, waiting for transfers between devices: 5.5 us -> 9.04 us  [swap(): return lax.ppermute(x, AXIS, [(i, i ^ flip) for i in range(n)])]
    concatenate x9 -> x0, other arithmetic: 3.31 us -> none  [the longest x1 0.95 us: per_device(): own_z = jnp.concatenate([own_z, swap(own_z, 8)], axis=0)]
    convert_element_type x4 -> x0, other arithmetic: 2.31 us -> none  [the longest x2 1.46 us: per_device(): zn, zt = (proxy_node.astype(BF), proxy_top.astype(BF))]
    ppermute x24 -> x28, starting transfers between devices: 39.7 us -> 38.4 us  [swap(): return lax.ppermute(x, AXIS, [(i, i ^ flip) for i in range(n)])]
    slice x7 -> x2, local copies, waits for them, and re-layouts: 2.25 us -> 0.99 us  [the longest x1 0.97 us: per_device(): across_a = swap(v['points'][:HALF], 3)]
  transfers between devices with their start and end apart: 24 -> 28, of which waited for: 5 -> 7; matrix products, arithmetic and copies ran while one was open for 7% -> 0% of each run, Pallas kernels for 20% -> 30%
where the time goes in v2:
time: 79.1 us; the launch traced here: 78.9 us
  starting transfers between devices  38.4 us (49%)
  Pallas kernels  30.1 us (38%)
  waiting for transfers between devices  9.04 us (11%)
  local copies, waits for them, and re-layouts  1.08 us (1%)
    ppermute x28, starting transfers between devices, swap(): return lax.ppermute(x, AXIS, [(i, i ^ flip) for i in range(n)])  38.4 us
    pallas_call x28, Pallas kernels, call(): pl.pallas_call(body, out_shape=[jax.ShapeDtypeStruct(s, d) for s, d in ou...  30.1 us
    ppermute x28, waiting for transfers between devices, swap(): return lax.ppermute(x, AXIS, [(i, i ^ flip) for i in range(n)])  9.04 us
  transfers between devices with their start and end apart: 28, of which 7 were waited for; matrix products, arithmetic and copies ran while one was open for 0% of the time, Pallas kernels for 30%

profile of v2, /device:TPU:1, one launch (start us, length us, event | category | flops | bytes accessed | tf_op | source)
XLA Modules:
  0.0 78.9 jit_solution(6567822292053826326)
XLA Ops:
  0.9 1.0 %slice.6 = bf16[1024,128]{1,0:T(8,128)(2,1)S(1)} slice(bf16[2048,128]{1,0:T(8,128)(2,1)} %own), slice={[0:1024], [0:128]} | slice | bytes 524288 | tf_op jit(solution)/shard_map/slice | solution.py:346
  1.9 2.7 %collective-permute-start.6 = (bf16[1024,128]{1,0:T(8,128)(2,1)S(1)}, bf16[1024,128]{1,0:T(8,128)(2,1)S(1)}, u32[]{:S(2)}, u32[]{:S(2)}) collective-permute-start(bf16[1024,128]{1,0:T(8,128)(2,1)S(1)} %slice.6), channel_id=1, source_target_pairs={{0,3},{1,2},{2,1},{3,0},{4,7},{5,6},{6,5},{7,4},{8,11},{9,10},{10,... | collective-permute-start | bytes 786440 | tf_op jit(solution)/shard_map/ppermute | solution.py:300
  4.8 1.9 %collective-permute-start.2 = (bf16[208,128]{1,0:T(8,128)(2,1)S(1)}, bf16[208,128]{1,0:T(8,128)(2,1)S(1)}, u32[]{:S(2)}, u32[]{:S(2)}) collective-permute-start(bf16[208,128]{1,0:T(8,128)(2,1)S(1)} %pack.1.a.stat_a), channel_id=1, source_target_pairs={{0,3},{1,2},{2,1},{3,0},{4,7},{5,6},{6,5},{7,4},{8,11},{9,10},{10,... | collective-permute-start | bytes 159752 | tf_op jit(solution)/shard_map/ppermute | solution.py:300
  6.7 5.7 %prep.1 = (bf16[2048,256]{1,0:T(8,128)(2,1)S(1)}, bf16[2048,256]{1,0:T(8,128)(2,1)S(1)}, bf16[512,256]{1,0:T(8,128)(2,1)S(1)}, bf16[896,256]{1,0:T(8,128)(2,1)S(...) custom-call(s32[1,2048]{1,0:T(1,128)S(1)} %copy-done.5, ...), custom_call_target="tpu_custom_call" | custom-call | tf_op jit(solution)/shard_map/prep/pallas_call | solution.py:59
  12.6 1.1 %collective-permute-done.2.d.stat_d = bf16[208,128]{1,0:T(8,128)(2,1)S(1)} collective-permute-done((bf16[208,128]{1,0:T(8,128)(2,1)S(1)}, bf16[208,128]{1,0:T(8,128)(2,1)S(1)}, u32[]{:S(2)}, u32[]{:S(2)}) %collective-permute-start.2) | collective-permute-done | bytes 53280 | tf_op jit(solution)/shard_map/ppermute | solution.py:300
  14.1 2.7 %collective-permute-start.5 = (bf16[4,80,128]{2,1,0:T(8,128)(2,1)S(1)}, bf16[4,80,128]{2,1,0:T(8,128)(2,1)S(1)}, u32[]{:S(2)}, u32[]{:S(2)}) collective-permute-start(bf16[4,80,128]{2,1,0:T(8,128)(2,1)S(1)} %cat_z.1.one), channel_id=1, source_target_pairs={{0,6},{1,7},{2,4},{3,5},{4,2},{5,3},{6,0},{7,1},{8,14},{9,15},{10,... | collective-permute-start | bytes 245768 | tf_op jit(solution)/shard_map/ppermute | solution.py:300
  17.0 2.6 %near_own.2.in_a = f32[1024,256]{1,0:T(8,128)S(1)} custom-call(bf16[2048,256]{1,0:T(8,128)(2,1)S(1)} %get-tuple-element.317.own_l, bf16[2048,256]{1,0:T(8,128)(2,1)S(1)} %get-tuple-element.215.own_r, bf16[512,256]{1,0:T(8,128)(2,1)S(1)} %get-tuple-element.239.buf_zero.own, bf16[896,256]{1,0:T(8,128)(2,1)S(1)} %get-tuple-element.272.buf_one.own, ...), custom_call_target="tpu_custom_call" | custom-call | tf_op jit(solution)/shard_map/near_own/pallas_call | solution.py:59
  19.8 1.5 %collective-permute-start.8 = (bf16[8,80,128]{2,1,0:T(8,128)(2,1)S(1)}, bf16[8,80,128]{2,1,0:T(8,128)(2,1)S(1)}, u32[]{:S(2)}, u32[]{:S(2)}) collective-permute-start(bf16[8,80,128]{2,1,0:T(8,128)(2,1)S(1)} %join_rows.5.z_a.nodes_a), channel_id=1, source_target_pairs={{0,8},{1,9},{2,10},{3,11},{4,12},{5,13},{6,14},{7,15},{8,0},{9,1},... | collective-permute-start | bytes 491528 | tf_op jit(solution)/shard_map/ppermute | solution.py:300
  21.4 2.0 %collective-permute-start.11 = (bf16[1024,128]{1,0:T(8,128)(2,1)S(1)}, bf16[1024,128]{1,0:T(8,128)(2,1)S(1)}, u32[]{:S(2)}, u32[]{:S(2)}) collective-permute-start(bf16[1024,128]{1,0:T(8,128)(2,1)S(1)} %slice.7), channel_id=1, source_target_pairs={{0,3},{1,2},{2,1},{3,0},{4,7},{5,6},{6,5},{7,4},{8,11},{9,10},{10,... | collective-permute-start | bytes 786440 | tf_op jit(solution)/shard_map/ppermute | solution.py:300
  23.6 1.0 %collective-permute-start.7 = (bf16[128,256]{1,0:T(8,128)(2,1)S(1)}, bf16[128,256]{1,0:T(8,128)(2,1)S(1)}, u32[]{:S(2)}, u32[]{:S(2)}) collective-permute-start(bf16[128,256]{1,0:T(8,128)(2,1)S(1)} %get-tuple-element.230.mine), channel_id=1, source_target_pairs={{0,6},{1,7},{2,4},{3,5},{4,2},{5,3},{6,0},{7,1},{8,14},{9,15},{10,... | collective-permute-start | bytes 196616 | tf_op jit(solution)/shard_map/ppermute | solution.py:300
  24.6 2.6 %near_own.3.in_b = f32[1024,256]{1,0:T(8,128)S(1)} custom-call(bf16[2048,256]{1,0:T(8,128)(2,1)S(1)} %get-tuple-element.317.own_l, bf16[2048,256]{1,0:T(8,128)(2,1)S(1)} %get-tuple-element.215.own_r, bf16[512,256]{1,0:T(8,128)(2,1)S(1)} %get-tuple-element.239.buf_zero.own, bf16[896,256]{1,0:T(8,128)(2,1)S(1)} %get-tuple-element.272.buf_one.own, ...), custom_call_target="tpu_custom_call" | custom-call | tf_op jit(solution)/shard_map/near_own/pallas_call | solution.py:59
  27.3 1.7 %collective-permute-done.7.got = bf16[128,256]{1,0:T(8,128)(2,1)S(1)} collective-permute-done((bf16[128,256]{1,0:T(8,128)(2,1)S(1)}, bf16[128,256]{1,0:T(8,128)(2,1)S(1)}, u32[]{:S(2)}, u32[]{:S(2)}) %collective-permute-start.7) | collective-permute-done | bytes 65568 | tf_op jit(solution)/shard_map/ppermute | solution.py:300
  29.0 0.9 %collective-permute-done.11 = bf16[1024,128]{1,0:T(8,128)(2,1)S(1)} collective-permute-done((bf16[1024,128]{1,0:T(8,128)(2,1)S(1)}, bf16[1024,128]{1,0:T(8,128)(2,1)S(1)}, u32[]{:S(2)}, u32[]{:S(2)}) %collective-permute-start.11) | collective-permute-done | bytes 262176 | tf_op jit(solution)/shard_map/ppermute | solution.py:300
  30.6 1.1 %collective-permute-start.15 = (bf16[2048,128]{1,0:T(8,128)(2,1)S(1)}, bf16[2048,128]{1,0:T(8,128)(2,1)S(1)}, u32[]{:S(2)}, u32[]{:S(2)}) collective-permute-start(bf16[2048,128]{1,0:T(8,128)(2,1)S(1)} %choose.5), channel_id=1, source_target_pairs={{0,1},{1,0},{2,3},{3,2},{4,5},{5,4},{6,7},{7,6},{8,9},{9,8},{10,11... | collective-permute-start | bytes 1572872 | tf_op jit(solution)/shard_map/ppermute | solution.py:300
  31.7 1.0 %collective-permute-start.14 = (bf16[512,256]{1,0:T(8,128)(2,1)S(1)}, bf16[512,256]{1,0:T(8,128)(2,1)S(1)}, u32[]{:S(2)}, u32[]{:S(2)}) collective-permute-start(bf16[512,256]{1,0:T(8,128)(2,1)S(1)} %get-tuple-element.239.buf_zero.own), channel_id=1, source_target_pairs={{0,3},{1,2},{2,1},{3,0},{4,7},{5,6},{6,5},{7,4},{8,11},{9,10},{10,... | collective-permute-start | bytes 786440 | tf_op jit(solution)/shard_map/ppermute | solution.py:300
  33.0 2.7 %collective-permute-start.10 = (bf16[16,16,128]{2,1,0:T(8,128)(2,1)S(1)}, bf16[16,16,128]{2,1,0:T(8,128)(2,1)S(1)}, u32[]{:S(2)}, u32[]{:S(2)}) collective-permute-start(bf16[16,16,128]{2,1,0:T(8,128)(2,1)S(1)} %tops.1.one), channel_id=1, source_target_pairs={{0,24},{1,25},{2,26},{3,27},{4,28},{5,29},{6,30},{7,31},{8,16},{9,... | collective-permute-start | bytes 196616 | tf_op jit(solution)/shard_map/ppermute | solution.py:300
  35.7 1.4 %collective-permute-start.20 = (bf16[896,256]{1,0:T(8,128)(2,1)S(1)}, bf16[896,256]{1,0:T(8,128)(2,1)S(1)}, u32[]{:S(2)}, u32[]{:S(2)}) collective-permute-start(bf16[896,256]{1,0:T(8,128)(2,1)S(1)} %get-tuple-element.272.buf_one.own), channel_id=1, source_target_pairs={{0,3},{1,2},{2,1},{3,0},{4,7},{5,6},{6,5},{7,4},{8,11},{9,10},{10,... | collective-permute-start | bytes 1376264 | tf_op jit(solution)/shard_map/ppermute | solution.py:300
  37.6 1.7 %collective-permute-start.13 = (bf16[32,16,128]{2,1,0:T(8,128)(2,1)S(1)}, bf16[32,16,128]{2,1,0:T(8,128)(2,1)S(1)}, u32[]{:S(2)}, u32[]{:S(2)}) collective-permute-start(bf16[32,16,128]{2,1,0:T(8,128)(2,1)S(1)} %join_rows.6.one), channel_id=1, source_target_pairs={{0,32},{1,33},{2,34},{3,35},{4,36},{5,37},{6,38},{7,39},{8,40},{9,... | collective-permute-start | bytes 393224 | tf_op jit(solution)/shard_map/ppermute | solution.py:300
  39.3 2.5 %collective-permute-start.12 = (bf16[64,256]{1,0:T(8,128)(2,1)S(1)}, bf16[64,256]{1,0:T(8,128)(2,1)S(1)}, u32[]{:S(2)}, u32[]{:S(2)}) collective-permute-start(bf16[64,256]{1,0:T(8,128)(2,1)S(1)} %top.1.one), channel_id=1, source_target_pairs={{0,24},{1,25},{2,26},{3,27},{4,28},{5,29},{6,30},{7,31},{8,16},{9,... | collective-permute-start | bytes 98312 | tf_op jit(solution)/shard_map/ppermute | solution.py:300
  42.4 2.5 %collective-permute-start.17 = (bf16[512,256]{1,0:T(8,128)(2,1)S(1)}, bf16[512,256]{1,0:T(8,128)(2,1)S(1)}, u32[]{:S(2)}, u32[]{:S(2)}) collective-permute-start(bf16[512,256]{1,0:T(8,128)(2,1)S(1)} %choose.6), channel_id=1, source_target_pairs={{0,1},{1,0},{2,3},{3,2},{4,5},{5,4},{6,7},{7,6},{8,9},{9,8},{10,11... | collective-permute-start | bytes 786440 | tf_op jit(solution)/shard_map/ppermute | solution.py:300
  45.0 2.3 %collective-permute-start.18 = (bf16[64,16,128]{2,1,0:T(8,128)(2,1)S(1)}, bf16[64,16,128]{2,1,0:T(8,128)(2,1)S(1)}, u32[]{:S(2)}, u32[]{:S(2)}) collective-permute-start(bf16[64,16,128]{2,1,0:T(8,128)(2,1)S(1)} %join_rows.8.tops_a), channel_id=1, source_target_pairs={{0,96},{1,97},{2,98},{3,99},{4,100},{5,101},{6,102},{7,103},{8,104... | collective-permute-start | bytes 786440 | tf_op jit(solution)/shard_map/ppermute | solution.py:300
  48.0 2.9 %near_chunk.3 = (f32[1024,256]{1,0:T(8,128)S(1)}, f32[1024,256]{1,0:T(8,128)S(1)}) custom-call(bf16[2048,256]{1,0:T(8,128)(2,1)S(1)} %get-tuple-element.317.own_l, bf16[2048,128]{1,0:T(8,128)(2,1)S(1)} %constant_dynamic-update-slice_fusion.got.pts_a, ...), custom_call_target="tpu_custom_call", output_to_operand_aliasing={{0}: (5, {}), {1}: (6, {})} | custom-call | tf_op jit(solution)/shard_map/near_chunk/pallas_call | solution.py:59
  50.9 1.7 %collective-permute-done.18.tops_b = bf16[64,16,128]{2,1,0:T(8,128)(2,1)S(1)} collective-permute-done((bf16[64,16,128]{2,1,0:T(8,128)(2,1)S(1)}, bf16[64,16,128]{2,1,0:T(8,128)(2,1)S(1)}, u32[]{:S(2)}, u32[]{:S(2)}) %collective-permute-start.18) | collective-permute-done | bytes 262176 | tf_op jit(solution)/shard_map/ppermute | solution.py:300
  53.2 2.4 %collective-permute-start.22 = (bf16[896,256]{1,0:T(8,128)(2,1)S(1)}, bf16[896,256]{1,0:T(8,128)(2,1)S(1)}, u32[]{:S(2)}, u32[]{:S(2)}) collective-permute-start(bf16[896,256]{1,0:T(8,128)(2,1)S(1)} %choose.7), channel_id=1, source_target_pairs={{0,1},{1,0},{2,3},{3,2},{4,5},{5,4},{6,7},{7,6},{8,9},{9,8},{10,11... | collective-permute-start | bytes 1376264 | tf_op jit(solution)/shard_map/ppermute | solution.py:300
  56.1 1.3 %collective-permute-start.26 = (bf16[512,256]{1,0:T(8,128)(2,1)S(1)}, bf16[512,256]{1,0:T(8,128)(2,1)S(1)}, u32[]{:S(2)}, u32[]{:S(2)}) collective-permute-start(bf16[512,256]{1,0:T(8,128)(2,1)S(1)} %get-tuple-element.305.buf_three.own), channel_id=1, source_target_pairs={{0,3},{1,2},{2,1},{3,0},{4,7},{5,6},{6,5},{7,4},{8,11},{9,10},{10,... | collective-permute-start | bytes 786440 | tf_op jit(solution)/shard_map/ppermute | solution.py:300
  57.4 2.3 %collective-permute-start.19 = (bf16[256,256]{1,0:T(8,128)(2,1)S(1)}, bf16[256,256]{1,0:T(8,128)(2,1)S(1)}, u32[]{:S(2)}, u32[]{:S(2)}) collective-permute-start(bf16[256,256]{1,0:T(8,128)(2,1)S(1)} %join_rows.9.low), channel_id=1, source_target_pairs={{0,96},{1,97},{2,98},{3,99},{4,100},{5,101},{6,102},{7,103},{8,104... | collective-permute-start | bytes 393224 | tf_op jit(solution)/shard_map/ppermute | solution.py:300
  59.8 0.9 %top_coupling.1.kernel_two = bf16[1792,256]{1,0:T(8,128)(2,1)S(1)} custom-call(bf16[64,16,128]{2,1,0:T(8,128)(2,1)S(1)} %join_rows.8.tops_a, bf16[64,16,128]{2,1,0:T(8,128)(2,1)S(1)} %collective-permute-done.18.tops_b), custom_call_target="tpu_custom_call" | custom-call | tf_op jit(solution)/shard_map/top_coupling/pallas_call | solution.py:59
  60.7 3.1 %collective-permute-done.19.high = bf16[256,256]{1,0:T(8,128)(2,1)S(1)} collective-permute-done((bf16[256,256]{1,0:T(8,128)(2,1)S(1)}, bf16[256,256]{1,0:T(8,128)(2,1)S(1)}, u32[]{:S(2)}, u32[]{:S(2)}) %collective-permute-start.19) | collective-permute-done | bytes 131104 | tf_op jit(solution)/shard_map/ppermute | solution.py:300
  65.5 1.4 %collective-permute-start.25 = (bf16[512,256]{1,0:T(8,128)(2,1)S(1)}, bf16[512,256]{1,0:T(8,128)(2,1)S(1)}, u32[]{:S(2)}, u32[]{:S(2)}) collective-permute-start(bf16[512,256]{1,0:T(8,128)(2,1)S(1)} %choose.8), channel_id=1, source_target_pairs={{0,1},{1,0},{2,3},{3,2},{4,5},{5,4},{6,7},{7,6},{8,9},{9,8},{10,11... | collective-permute-start | bytes 786440 | tf_op jit(solution)/shard_map/ppermute | solution.py:300
  66.9 2.9 %near_chunk.4 = (f32[1024,256]{1,0:T(8,128)S(1)}, f32[1024,256]{1,0:T(8,128)S(1)}) custom-call(bf16[2048,256]{1,0:T(8,128)(2,1)S(1)} %get-tuple-element.317.own_l, bf16[2048,128]{1,0:T(8,128)(2,1)S(1)} %constant_dynamic-update-slice_fusion.got.pts_a, ...), custom_call_target="tpu_custom_call", output_to_operand_aliasing={{0}: (5, {}), {1}: (6, {})} | custom-call | tf_op jit(solution)/shard_map/near_chunk/pallas_call | solution.py:59
  71.5 2.9 %near_chunk.5 = (f32[1024,256]{1,0:T(8,128)S(1)}, f32[1024,256]{1,0:T(8,128)S(1)}) custom-call(bf16[2048,256]{1,0:T(8,128)(2,1)S(1)} %get-tuple-element.317.own_l, bf16[2048,128]{1,0:T(8,128)(2,1)S(1)} %constant_dynamic-update-slice_fusion.got.pts_a, ...), custom_call_target="tpu_custom_call", output_to_operand_aliasing={{0}: (5, {}), {1}: (6, {})} | custom-call | tf_op jit(solution)/shard_map/near_chunk/pallas_call | solution.py:59
  74.4 4.5 %near_last.1 = bf16[2048,256]{1,0:T(8,128)(2,1)} custom-call(bf16[2048,256]{1,0:T(8,128)(2,1)S(1)} %get-tuple-element.317.own_l, bf16[2048,128]{1,0:T(8,128)(2,1)S(1)} %constant_dynamic-update-slice_fusion.got.pts_a, bf16[512,256]{1,0:T(8,128)(2,1)S(1)} %collective-permute-done.26.got.rhs_a, bf16[2048,128]{1,0:T(8,128)(2,1)S(1)} %collective-permute-done.15.pts_b, ...), custom_call_target="tpu_custom_call" | custom-call | tf_op jit(solution)/shard_map/near_last/pallas_call | solution.py:59
  (68 shorter events, 9.4 us)
Async XLA Ops:
  0.9 5.8 %copy-start.5 = (s32[1,2048]{1,0:T(1,128)S(1)}, s32[1,2048]{1,0:T(1,128)}, u32[]{:S(2)}) copy-start(s32[1,2048]{1,0:T(1,128)} %order) | copy-start | bytes 24580
  1.9 17.9 %collective-permute-start.6 = (bf16[1024,128]{1,0:T(8,128)(2,1)S(1)}, bf16[1024,128]{1,0:T(8,128)(2,1)S(1)}, u32[]{:S(2)}, u32[]{:S(2)}) collective-permute-start(bf16[1024,128]{1,0:T(8,128)(2,1)S(1)} %slice.6), channel_id=1, source_target_pairs={{0,3},{1,2},{2,1},{3,0},{4,7},{5,6},{6,5},{7,4},{8,11},{9,10},{10,... | collective-permute-start | bytes 786440 | tf_op jit(solution)/shard_map/ppermute | solution.py:300
  4.6 7.8 %collective-permute-start = (bf16[208,128]{1,0:T(8,128)(2,1)S(1)}, bf16[208,128]{1,0:T(8,128)(2,1)S(1)}, u32[]{:S(2)}, u32[]{:S(2)}) collective-permute-start(bf16[208,128]{1,0:T(8,128)(2,1)S(1)} %pack.1.a.stat_a), channel_id=1, source_target_pairs={{0,1},{1,0},{2,3},{3,2},{4,5},{5,4},{6,7},{7,6},{8,9},{9,8},{10,11... | collective-permute-start | bytes 159752 | tf_op jit(solution)/shard_map/ppermute | solution.py:300
  4.6 8.0 %collective-permute-start.1 = (bf16[208,128]{1,0:T(8,128)(2,1)S(1)}, bf16[208,128]{1,0:T(8,128)(2,1)S(1)}, u32[]{:S(2)}, u32[]{:S(2)}) collective-permute-start(bf16[208,128]{1,0:T(8,128)(2,1)S(1)} %pack.1.a.stat_a), channel_id=1, source_target_pairs={{0,2},{1,3},{2,0},{3,1},{4,6},{5,7},{6,4},{7,5},{8,10},{9,11},{10,... | collective-permute-start | bytes 159752 | tf_op jit(solution)/shard_map/ppermute | solution.py:300
  4.8 9.0 %collective-permute-start.2 = (bf16[208,128]{1,0:T(8,128)(2,1)S(1)}, bf16[208,128]{1,0:T(8,128)(2,1)S(1)}, u32[]{:S(2)}, u32[]{:S(2)}) collective-permute-start(bf16[208,128]{1,0:T(8,128)(2,1)S(1)} %pack.1.a.stat_a), channel_id=1, source_target_pairs={{0,3},{1,2},{2,1},{3,0},{4,7},{5,6},{6,5},{7,4},{8,11},{9,10},{10,... | collective-permute-start | bytes 159752 | tf_op jit(solution)/shard_map/ppermute | solution.py:300
  13.7 3.1 %collective-permute-start.3 = (bf16[128,256]{1,0:T(8,128)(2,1)S(1)}, bf16[128,256]{1,0:T(8,128)(2,1)S(1)}, u32[]{:S(2)}, u32[]{:S(2)}) collective-permute-start(bf16[128,256]{1,0:T(8,128)(2,1)S(1)} %get-tuple-element.188), channel_id=1, source_target_pairs={{0,1},{1,0},{2,3},{3,2},{4,5},{5,4},{6,7},{7,6},{8,9},{9,8},{10,11... | collective-permute-start | bytes 196616 | tf_op jit(solution)/shard_map/ppermute | solution.py:300
  14.1 5.5 %collective-permute-start.5 = (bf16[4,80,128]{2,1,0:T(8,128)(2,1)S(1)}, bf16[4,80,128]{2,1,0:T(8,128)(2,1)S(1)}, u32[]{:S(2)}, u32[]{:S(2)}) collective-permute-start(bf16[4,80,128]{2,1,0:T(8,128)(2,1)S(1)} %cat_z.1.one), channel_id=1, source_target_pairs={{0,6},{1,7},{2,4},{3,5},{4,2},{5,3},{6,0},{7,1},{8,14},{9,15},{10,... | collective-permute-start | bytes 245768 | tf_op jit(solution)/shard_map/ppermute | solution.py:300
  16.8 4.5 %copy-start = (bf16[2048,128]{1,0:T(8,128)(2,1)S(1)}, bf16[2048,128]{1,0:T(8,128)(2,1)}, u32[]{:S(2)}) copy-start(bf16[2048,128]{1,0:T(8,128)(2,1)} %own) | copy-start | bytes 1572868
  16.9 3.0 %collective-permute-start.4 = (bf16[64,256]{1,0:T(8,128)(2,1)S(1)}, bf16[64,256]{1,0:T(8,128)(2,1)S(1)}, u32[]{:S(2)}, u32[]{:S(2)}) collective-permute-start(bf16[64,256]{1,0:T(8,128)(2,1)S(1)} %get-tuple-element.202), channel_id=1, source_target_pairs={{0,2},{1,3},{2,0},{3,1},{4,6},{5,7},{6,4},{7,5},{8,10},{9,11},{10,... | collective-permute-start | bytes 98312 | tf_op jit(solution)/shard_map/ppermute | solution.py:300
  19.8 9.2 %collective-permute-start.8 = (bf16[8,80,128]{2,1,0:T(8,128)(2,1)S(1)}, bf16[8,80,128]{2,1,0:T(8,128)(2,1)S(1)}, u32[]{:S(2)}, u32[]{:S(2)}) collective-permute-start(bf16[8,80,128]{2,1,0:T(8,128)(2,1)S(1)} %join_rows.5.z_a.nodes_a), channel_id=1, source_target_pairs={{0,8},{1,9},{2,10},{3,11},{4,12},{5,13},{6,14},{7,15},{8,0},{9,1},... | collective-permute-start | bytes 491528 | tf_op jit(solution)/shard_map/ppermute | solution.py:300
  21.4 8.6 %collective-permute-start.11 = (bf16[1024,128]{1,0:T(8,128)(2,1)S(1)}, bf16[1024,128]{1,0:T(8,128)(2,1)S(1)}, u32[]{:S(2)}, u32[]{:S(2)}) collective-permute-start(bf16[1024,128]{1,0:T(8,128)(2,1)S(1)} %slice.7), channel_id=1, source_target_pairs={{0,3},{1,2},{2,1},{3,0},{4,7},{5,6},{6,5},{7,4},{8,11},{9,10},{10,... | collective-permute-start | bytes 786440 | tf_op jit(solution)/shard_map/ppermute | solution.py:300
  23.6 5.4 %collective-permute-start.7 = (bf16[128,256]{1,0:T(8,128)(2,1)S(1)}, bf16[128,256]{1,0:T(8,128)(2,1)S(1)}, u32[]{:S(2)}, u32[]{:S(2)}) collective-permute-start(bf16[128,256]{1,0:T(8,128)(2,1)S(1)} %get-tuple-element.230.mine), channel_id=1, source_target_pairs={{0,6},{1,7},{2,4},{3,5},{4,2},{5,3},{6,0},{7,1},{8,14},{9,15},{10,... | collective-permute-start | bytes 196616 | tf_op jit(solution)/shard_map/ppermute | solution.py:300
  30.6 14.3 %collective-permute-start.15 = (bf16[2048,128]{1,0:T(8,128)(2,1)S(1)}, bf16[2048,128]{1,0:T(8,128)(2,1)S(1)}, u32[]{:S(2)}, u32[]{:S(2)}) collective-permute-start(bf16[2048,128]{1,0:T(8,128)(2,1)S(1)} %choose.5), channel_id=1, source_target_pairs={{0,1},{1,0},{2,3},{3,2},{4,5},{5,4},{6,7},{7,6},{8,9},{9,8},{10,11... | collective-permute-start | bytes 1572872 | tf_op jit(solution)/shard_map/ppermute | solution.py:300
  31.7 10.1 %collective-permute-start.14 = (bf16[512,256]{1,0:T(8,128)(2,1)S(1)}, bf16[512,256]{1,0:T(8,128)(2,1)S(1)}, u32[]{:S(2)}, u32[]{:S(2)}) collective-permute-start(bf16[512,256]{1,0:T(8,128)(2,1)S(1)} %get-tuple-element.239.buf_zero.own), channel_id=1, source_target_pairs={{0,3},{1,2},{2,1},{3,0},{4,7},{5,6},{6,5},{7,4},{8,11},{9,10},{10,... | collective-permute-start | bytes 786440 | tf_op jit(solution)/shard_map/ppermute | solution.py:300
  32.7 4.9 %collective-permute-start.9 = (bf16[192,256]{1,0:T(8,128)(2,1)S(1)}, bf16[192,256]{1,0:T(8,128)(2,1)S(1)}, u32[]{:S(2)}, u32[]{:S(2)}) collective-permute-start(bf16[192,256]{1,0:T(8,128)(2,1)S(1)} %pair.1.mine.sibs_a), channel_id=1, source_target_pairs={{0,8},{1,9},{2,10},{3,11},{4,12},{5,13},{6,14},{7,15},{8,0},{9,1},... | collective-permute-start | bytes 294920 | tf_op jit(solution)/shard_map/ppermute | solution.py:300
  33.0 4.6 %collective-permute-start.10 = (bf16[16,16,128]{2,1,0:T(8,128)(2,1)S(1)}, bf16[16,16,128]{2,1,0:T(8,128)(2,1)S(1)}, u32[]{:S(2)}, u32[]{:S(2)}) collective-permute-start(bf16[16,16,128]{2,1,0:T(8,128)(2,1)S(1)} %tops.1.one), channel_id=1, source_target_pairs={{0,24},{1,25},{2,26},{3,27},{4,28},{5,29},{6,30},{7,31},{8,16},{9,... | collective-permute-start | bytes 196616 | tf_op jit(solution)/shard_map/ppermute | solution.py:300
  35.7 16.9 %collective-permute-start.20 = (bf16[896,256]{1,0:T(8,128)(2,1)S(1)}, bf16[896,256]{1,0:T(8,128)(2,1)S(1)}, u32[]{:S(2)}, u32[]{:S(2)}) collective-permute-start(bf16[896,256]{1,0:T(8,128)(2,1)S(1)} %get-tuple-element.272.buf_one.own), channel_id=1, source_target_pairs={{0,3},{1,2},{2,1},{3,0},{4,7},{5,6},{6,5},{7,4},{8,11},{9,10},{10,... | collective-permute-start | bytes 1376264 | tf_op jit(solution)/shard_map/ppermute | solution.py:300
  37.6 7.3 %collective-permute-start.13 = (bf16[32,16,128]{2,1,0:T(8,128)(2,1)S(1)}, bf16[32,16,128]{2,1,0:T(8,128)(2,1)S(1)}, u32[]{:S(2)}, u32[]{:S(2)}) collective-permute-start(bf16[32,16,128]{2,1,0:T(8,128)(2,1)S(1)} %join_rows.6.one), channel_id=1, source_target_pairs={{0,32},{1,33},{2,34},{3,35},{4,36},{5,37},{6,38},{7,39},{8,40},{9,... | collective-permute-start | bytes 393224 | tf_op jit(solution)/shard_map/ppermute | solution.py:300
  39.3 5.6 %collective-permute-start.12 = (bf16[64,256]{1,0:T(8,128)(2,1)S(1)}, bf16[64,256]{1,0:T(8,128)(2,1)S(1)}, u32[]{:S(2)}, u32[]{:S(2)}) collective-permute-start(bf16[64,256]{1,0:T(8,128)(2,1)S(1)} %top.1.one), channel_id=1, source_target_pairs={{0,24},{1,25},{2,26},{3,27},{4,28},{5,29},{6,30},{7,31},{8,16},{9,... | collective-permute-start | bytes 98312 | tf_op jit(solution)/shard_map/ppermute | solution.py:300
  42.4 5.6 %collective-permute-start.17 = (bf16[512,256]{1,0:T(8,128)(2,1)S(1)}, bf16[512,256]{1,0:T(8,128)(2,1)S(1)}, u32[]{:S(2)}, u32[]{:S(2)}) collective-permute-start(bf16[512,256]{1,0:T(8,128)(2,1)S(1)} %choose.6), channel_id=1, source_target_pairs={{0,1},{1,0},{2,3},{3,2},{4,5},{5,4},{6,7},{7,6},{8,9},{9,8},{10,11... | collective-permute-start | bytes 786440 | tf_op jit(solution)/shard_map/ppermute | solution.py:300
  45.0 7.7 %collective-permute-start.18 = (bf16[64,16,128]{2,1,0:T(8,128)(2,1)S(1)}, bf16[64,16,128]{2,1,0:T(8,128)(2,1)S(1)}, u32[]{:S(2)}, u32[]{:S(2)}) collective-permute-start(bf16[64,16,128]{2,1,0:T(8,128)(2,1)S(1)} %join_rows.8.tops_a), channel_id=1, source_target_pairs={{0,96},{1,97},{2,98},{3,99},{4,100},{5,101},{6,102},{7,103},{8,104... | collective-permute-start | bytes 786440 | tf_op jit(solution)/shard_map/ppermute | solution.py:300
  47.3 3.6 %collective-permute-start.16 = (bf16[128,256]{1,0:T(8,128)(2,1)S(1)}, bf16[128,256]{1,0:T(8,128)(2,1)S(1)}, u32[]{:S(2)}, u32[]{:S(2)}) collective-permute-start(bf16[128,256]{1,0:T(8,128)(2,1)S(1)} %join_rows.7.one), channel_id=1, source_target_pairs={{0,32},{1,33},{2,34},{3,35},{4,36},{5,37},{6,38},{7,39},{8,40},{9,... | collective-permute-start | bytes 196616 | tf_op jit(solution)/shard_map/ppermute | solution.py:300
  53.2 13.7 %collective-permute-start.22 = (bf16[896,256]{1,0:T(8,128)(2,1)S(1)}, bf16[896,256]{1,0:T(8,128)(2,1)S(1)}, u32[]{:S(2)}, u32[]{:S(2)}) collective-permute-start(bf16[896,256]{1,0:T(8,128)(2,1)S(1)} %choose.7), channel_id=1, source_target_pairs={{0,1},{1,0},{2,3},{3,2},{4,5},{5,4},{6,7},{7,6},{8,9},{9,8},{10,11... | collective-permute-start | bytes 1376264 | tf_op jit(solution)/shard_map/ppermute | solution.py:300
  55.7 9.3 %collective-permute-start.23 = (bf16[512,256]{1,0:T(8,128)(2,1)S(1)}, bf16[512,256]{1,0:T(8,128)(2,1)S(1)}, u32[]{:S(2)}, u32[]{:S(2)}) collective-permute-start(bf16[512,256]{1,0:T(8,128)(2,1)S(1)} %get-tuple-element.288.buf_two.own), channel_id=1, source_target_pairs={{0,3},{1,2},{2,1},{3,0},{4,7},{5,6},{6,5},{7,4},{8,11},{9,10},{10,... | collective-permute-start | bytes 786440 | tf_op jit(solution)/shard_map/ppermute | solution.py:300
  56.1 13.7 %collective-permute-start.26 = (bf16[512,256]{1,0:T(8,128)(2,1)S(1)}, bf16[512,256]{1,0:T(8,128)(2,1)S(1)}, u32[]{:S(2)}, u32[]{:S(2)}) collective-permute-start(bf16[512,256]{1,0:T(8,128)(2,1)S(1)} %get-tuple-element.305.buf_three.own), channel_id=1, source_target_pairs={{0,3},{1,2},{2,1},{3,0},{4,7},{5,6},{6,5},{7,4},{8,11},{9,10},{10,... | collective-permute-start | bytes 786440 | tf_op jit(solution)/shard_map/ppermute | solution.py:300
  57.4 6.4 %collective-permute-start.19 = (bf16[256,256]{1,0:T(8,128)(2,1)S(1)}, bf16[256,256]{1,0:T(8,128)(2,1)S(1)}, u32[]{:S(2)}, u32[]{:S(2)}) collective-permute-start(bf16[256,256]{1,0:T(8,128)(2,1)S(1)} %join_rows.9.low), channel_id=1, source_target_pairs={{0,96},{1,97},{2,98},{3,99},{4,100},{5,101},{6,102},{7,103},{8,104... | collective-permute-start | bytes 393224 | tf_op jit(solution)/shard_map/ppermute | solution.py:300
  64.3 5.5 %collective-permute-start.21 = (bf16[64,256]{1,0:T(8,128)(2,1)S(1)}, bf16[64,256]{1,0:T(8,128)(2,1)S(1)}, u32[]{:S(2)}, u32[]{:S(2)}) collective-permute-start(bf16[64,256]{1,0:T(8,128)(2,1)S(1)} %field.1.mine), channel_id=1, source_target_pairs={{0,2},{1,3},{2,0},{3,1},{4,6},{5,7},{6,4},{7,5},{8,10},{9,11},{10,... | collective-permute-start | bytes 98312 | tf_op jit(solution)/shard_map/ppermute | solution.py:300
  65.5 6.0 %collective-permute-start.25 = (bf16[512,256]{1,0:T(8,128)(2,1)S(1)}, bf16[512,256]{1,0:T(8,128)(2,1)S(1)}, u32[]{:S(2)}, u32[]{:S(2)}) collective-permute-start(bf16[512,256]{1,0:T(8,128)(2,1)S(1)} %choose.8), channel_id=1, source_target_pairs={{0,1},{1,0},{2,3},{3,2},{4,5},{5,4},{6,7},{7,6},{8,9},{9,8},{10,11... | collective-permute-start | bytes 786440 | tf_op jit(solution)/shard_map/ppermute | solution.py:300
  70.4 4.0 %collective-permute-start.27 = (bf16[512,256]{1,0:T(8,128)(2,1)S(1)}, bf16[512,256]{1,0:T(8,128)(2,1)S(1)}, u32[]{:S(2)}, u32[]{:S(2)}) collective-permute-start(bf16[512,256]{1,0:T(8,128)(2,1)S(1)} %choose.9), channel_id=1, source_target_pairs={{0,1},{1,0},{2,3},{3,2},{4,5},{5,4},{6,7},{7,6},{8,9},{9,8},{10,11... | collective-permute-start | bytes 786440 | tf_op jit(solution)/shard_map/ppermute | solution.py:300
  71.4 3.1 %copy-start.1 = (bf16[2048,256]{1,0:T(8,128)(2,1)S(1)}, bf16[2048,256]{1,0:T(8,128)(2,1)}, u32[]{:S(2)}) copy-start(bf16[2048,256]{1,0:T(8,128)(2,1)} %bases.1) | copy-start | bytes 3145732
  71.4 3.1 %copy-start.2 = (f32[256,256]{1,0:T(8,128)S(1)}, f32[256,256]{1,0:T(8,128)}, u32[]{:S(2)}) copy-start(f32[256,256]{1,0:T(8,128)} %lift.1) | copy-start | bytes 786436
  71.4 3.0 %collective-permute-start.24 = (bf16[128,256]{1,0:T(8,128)(2,1)S(1)}, bf16[128,256]{1,0:T(8,128)(2,1)S(1)}, u32[]{:S(2)}, u32[]{:S(2)}) collective-permute-start(bf16[128,256]{1,0:T(8,128)(2,1)S(1)} %join.1.half), channel_id=1, source_target_pairs={{0,1},{1,0},{2,3},{3,2},{4,5},{5,4},{6,7},{7,6},{8,9},{9,8},{10,11... | collective-permute-start | bytes 196616 | tf_op jit(solution)/shard_map/ppermute | solution.py:300
  (2 other events, 4.0 us)

commit v3 on v2

v3 whole, which is shorter than its diff:
```python
import functools

import jax
import jax.numpy as jnp
from jax import lax
from jax.experimental import pallas as pl
from jax.experimental.pallas import tpu as pltpu
from jax.sharding import PartitionSpec as P

D = 128
NRHS = 256
RANK = 256
LEAF = 2048
AXIS = "leaf"
BF = jnp.bfloat16
F32 = jnp.float32
SCALE = 4.0 / D * 1.4426950408889634
FAR = 384
CHUNKS = ((0, 768), (768, 768), (1536, 512))
BASES = (0, FAR, 0)
HALF = LEAF // 2


def dot(a, b):
    return lax.dot_general(a, b, (((1,), (0,)), ((), ())), preferred_element_type=F32)


def dot_t(a, b):
    return lax.dot_general(a, b, (((1,), (1,)), ((), ())), preferred_element_type=F32)


def widened(x, left):
    wide = x.astype(F32)
    rest = 0.5 * jnp.sum(wide * wide, axis=1, keepdims=True)
    high = rest.astype(BF).astype(F32)
    rest = rest - high
    middle = rest.astype(BF).astype(F32)
    low = rest - middle
    lane = lax.broadcasted_iota(jnp.int32, (x.shape[0], 128), 1)
    first, ones = (0, 3) if left else (3, 0)
    extra = jnp.where(
        lane == first, -high, jnp.where(lane == first + 1, -middle, jnp.where(lane == first + 2, -low, 0.0))
    )
    extra = jnp.where((lane >= ones) & (lane < ones + 3), 1.0, extra)
    return jnp.concatenate([x.astype(BF), extra.astype(BF)], axis=1)


def gauss(left, right):
    return jnp.exp2(dot_t(left, right) * SCALE).astype(BF)


def call(body, outs, *args, name, scratch=(), smem=0, hbm=(), aliases=None, limit=24):
    def space(i):
        return pltpu.SMEM if i < smem else pltpu.HBM if i in hbm else pltpu.VMEM

    args = [
        pltpu.with_memory_space_constraint(arg, pltpu.HBM) if i in hbm else arg for i, arg in enumerate(args)
    ]
    return pl.pallas_call(
        body,
        out_shape=[jax.ShapeDtypeStruct(s, d) for s, d in outs],
        in_specs=[pl.BlockSpec(memory_space=space(i)) for i in range(len(args))],
        out_specs=[pl.BlockSpec(memory_space=pltpu.VMEM)] * len(outs),
        scratch_shapes=list(scratch),
        input_output_aliases=aliases or {},
        name=name,
        cost_estimate=pl.CostEstimate(flops=0, bytes_accessed=0, transcendentals=0),
        compiler_params=pltpu.CompilerParams(vmem_limit_bytes=limit << 20),
    )(*args)


def place():
    me = lax.axis_index(AXIS)
    x = lax.rem(lax.div(me, 2), 4)
    return lax.rem(me, 2), lax.rem(x, 2) ^ lax.div(x, 2), lax.rem(me, 4), lax.rem(me, 16)


def far_is_core(near):
    slot = place()[2]
    return ((6 - slot - lax.rem(near[0, 0], 4) - lax.rem(near[0, 1], 4)) ^ slot) == 1


def fetched(pairs, sems):
    copies = [pltpu.make_async_copy(src, dst, sems.at[i]) for i, (src, dst) in enumerate(pairs)]
    for copy in copies:
        copy.start()
    return copies


def prep_body(
    order_h, points_h, charges_h, bases_h, lift_h, proxy_h, lift_node_h, proxy_node_h, proxy_top_h,
    own_l, own_r, whole, buf_zero, buf_one, buf_two,
    keep, send, z_out, lift_low, proxy_wide,
    order, points, charges, bases, lift, proxy, lift_node, proxy_node, proxy_top, up, sems,
):
    core = place()[0]
    copies = fetched(
        (
            (order_h, order), (charges_h, charges), (points_h, points), (bases_h, bases), (lift_h, lift), (proxy_h, proxy),
            (lift_node_h, lift_node), (proxy_node_h, proxy_node), (proxy_top_h, proxy_top),
        ),
        sems,
    )
    copies[0].wait()
    rows = [order[:, b * 128 : (b + 1) * 128] for b in range(LEAF // 128)]
    tall = jnp.concatenate(rows * (128 // len(rows)), axis=0).astype(F32).T
    places = lax.broadcasted_iota(jnp.int32, (128, LEAF), 1).astype(F32)
    copies[1].wait()
    for b in range(LEAF // 128):
        hot = jnp.where(tall[:, b : b + 1] == places, 1.0, 0.0).astype(BF)
        whole[FAR + b * 128 : FAR + (b + 1) * 128, :] = dot(hot, charges[...]).astype(BF)
    for copy in copies[2:]:
        copy.wait()
    coef = lax.dot_general(
        whole[FAR:, :], bases[...], (((0,), (0,)), ((), ())), preferred_element_type=F32
    ).astype(BF)
    lift_low[...] = lift[...].astype(BF)
    proxy_wide[...] = widened(proxy[...].astype(BF), False)
    up[...] = dot(coef, lift_low[...])
    keep[...] = up[pl.ds(pl.multiple_of(core * 128, 128), 128), :]
    send[0:128, :] = up[pl.ds(pl.multiple_of((1 - core) * 128, 128), 128), :].astype(BF)
    send[128:192, :] = lift_node[...].astype(BF)
    z_out[0:32, 0:D] = proxy_node[0:32, :].astype(BF)
    z_out[0:32, D:] = proxy_node[32:64, :].astype(BF)
    z_out[32:40, 0:D] = proxy_top[0:8, :].astype(BF)
    z_out[32:40, D:] = proxy_top[8:16, :].astype(BF)
    whole[0:RANK, :] = coef
    whole[RANK:FAR, 0:D] = proxy[0:128, :].astype(BF)
    whole[RANK:FAR, D:] = proxy[128:256, :].astype(BF)
    for buf, (start, n), base in zip((buf_zero, buf_one, buf_two), CHUNKS, BASES):
        if base:
            buf[0:base, :] = whole[0:base, :]
        buf[base:, :] = whole[FAR + start : FAR + start + n, :]
    own_l[...] = widened(points[...], True)
    own_r[...] = widened(points[...], False)


def halve_body(keep, sent, got, z_own, kept, send, total):
    u = place()[1]
    total[...] = keep[...] + got[0:128, :].astype(F32)
    kept[...] = total[pl.ds(pl.multiple_of(u * 64, 64), 64), :]
    send[0:64, :] = total[pl.ds(pl.multiple_of((1 - u) * 64, 64), 64), :].astype(BF)
    send[64:128, :] = sent[128:192, :]
    send[128:192, :] = got[128:192, :]
    send[192:232, :] = z_own[...]


def node_body(kept, sent, got, send, lift):
    slot = place()[2]
    for j, (stat, row) in enumerate(((sent, 64), (sent, 128), (got, 64), (got, 128))):
        lift[pl.ds(pl.multiple_of((slot ^ j) * 64, 64), 64), :] = stat[row : row + 64, :]
    node = (kept[...] + got[0:64, :].astype(F32)).astype(BF)
    send[0:64, :] = node
    send[64:128, :] = dot(node, lift[...]).astype(BF)
    send[128:160, :] = sent[192:224, :]
    send[160:192, :] = got[192:224, :]
    send[192:200, :] = sent[224:232, :]
    send[200:208, :] = got[224:232, :]


def top_body(mine, got_x, got_y, got_xy, out, z_out):
    four = (mine, got_x, got_y, got_xy)
    out[0:64, :] = sum(part[64:128, :].astype(F32) for part in four).astype(BF)
    for h, part in enumerate(four):
        out[64 + 16 * h : 80 + 16 * h, :] = part[192:208, :]
        z_out[64 * h : 64 * h + 64, :] = part[128:192, :]


def more_body(mine, got_y, got_z, got_yz, out):
    for r, part in enumerate((mine, got_y, got_z, got_yz)):
        out[64 * r : 64 * r + 64, :] = part[0:64, :]
        out[256 + 64 * r : 320 + 64 * r, :] = part[64:128, :]


def node_coupling_body(z_own, z_got, out, z_node):
    slot = place()[2]
    for h in range(4):
        for core in range(2):
            for j in range(2):
                block = (z_got if core else z_own)[(2 * h + j) * 32 : (2 * h + j + 1) * 32, :]
                at = (slot ^ core ^ (2 * j) ^ (2 * (h % 2))) * 64
                z_node[pl.ds(pl.multiple_of(h * 256 + at, 64), 32), :] = block[:, 0:D]
                z_node[pl.ds(pl.multiple_of(h * 256 + at + 32, 32), 32), :] = block[:, D:]
    own = widened(z_node[0:256, :], False)
    for h in range(1, 4):
        out[(h - 1) * 256 : h * 256, :] = gauss(widened(z_node[h * 256 : (h + 1) * 256, :], True), own)


def field_body(
    sib_x, sib_y, sib_xy, low, high, low_core, high_core, kernel_one, lift, out, z_top
):
    part = place()[3]
    for r in range(8):
        for core in range(2):
            mine = ((low, high), (low_core, high_core))[core][r // 4]
            for k in range(8):
                offset = core ^ (2 * (k % 2)) ^ (6 * (k // 2 % 2)) ^ (8 * (k // 4)) ^ (8 * (r % 2))
                row = 256 + 64 * (r % 4) + 8 * k
                block = mine[row : row + 8, :].astype(F32)
                at = 256 * r + (part ^ offset) * 16
                z_top[pl.ds(pl.multiple_of(at, 16), 8), :] = block[:, 0:D]
                z_top[pl.ds(pl.multiple_of(at + 8, 8), 8), :] = block[:, D:]
    own = widened(z_top[0:256, :], False)
    field = None
    for r in range(1, 8):
        tile = gauss(widened(z_top[r * 256 : (r + 1) * 256, :], True), own)
        part = dot((low, high)[r // 4][64 * (r % 4) : 64 * (r % 4 + 1), :], tile)
        field = part if field is None else field + part
    total = dot_t(field.astype(BF), lift[...])
    for h, sib in enumerate((sib_x, sib_y, sib_xy)):
        total += dot(sib[0:64, :], kernel_one[256 * h : 256 * (h + 1), :])
    out[...] = total.astype(BF)


def join_body(mine, got, out):
    u = place()[1]
    out[pl.ds(pl.multiple_of(u * 64, 64), 64), :] = mine[...]
    out[pl.ds(pl.multiple_of((1 - u) * 64, 64), 64), :] = got[...]


def add_near(total, left, right, values, base, n):
    for c in range(0, n, 256):
        tile = gauss(left, right[c : c + 256, :])
        part = dot(tile, values[base + c : base + c + 256, :])
        total = part if total is None else total + part
    return total


def own_body(first, own_l, own_r, whole, *acc):
    for r in range(0, HALF, 512):
        total = acc[0][r : r + 512, :] if len(acc) > 1 else None
        left = own_l[first + r : first + r + 512, :]
        acc[-1][r : r + 512, :] = add_near(total, left, own_r, whole, FAR, LEAF)


def choose_body(skip, near, got, own, out):
    core = far_is_core(near)
    width = out.shape[1]

    @pl.when(core)
    def _():
        out[skip:, :] = got[skip:, :]
        if skip:
            out[0:skip, :] = own[0:skip, :]

    @pl.when(jnp.logical_not(core))
    def _():
        out[skip:, :] = own[skip:, 0:width]
        if skip:
            out[0:skip, :] = got[0:skip, :]


def chunk_body(i, own_l, pts_a, rows_a, pts_b, rows_b, in_a, in_b, acc_a, acc_b, right):
    (start, n), base = CHUNKS[i], BASES[i]
    right[0:n, :] = widened(pts_a[start : start + n, :], False)
    right[n : 2 * n, :] = widened(pts_b[start : start + n, :], False)
    for r in range(0, LEAF, 512):
        acc_in, acc = ((in_a, acc_a), (in_b, acc_b))[r // HALF]
        rows = slice(r % HALF, r % HALF + 512)
        left = own_l[r : r + 512, :]
        total = add_near(acc_in[rows, :], left, right.at[0:n, :], rows_a, base, n)
        acc[rows, :] = add_near(total, left, right.at[n : 2 * n, :], rows_b, base, n)


def far_body(rows, proxy, out):
    z_far = jnp.concatenate([rows[RANK:FAR, 0:D], rows[RANK:FAR, D:]], axis=0)
    out[...] = dot(rows[0:RANK, :], gauss(widened(z_far, True), proxy[...]))


def last_body(acc_a, acc_b, bases, far, lift, half, got, out, node):
    core = place()[0]
    node[pl.ds(pl.multiple_of(core * 128, 128), 128), :] = half[...]
    node[pl.ds(pl.multiple_of((1 - core) * 128, 128), 128), :] = got[...]
    field = (far[...] + dot_t(node[...], lift[...])).astype(BF)
    for r in range(0, LEAF, 512):
        acc = (acc_a, acc_b)[r // HALF]
        total = acc[r % HALF : r % HALF + 512, :] + dot_t(bases[r : r + 512, :], field)
        out[r : r + 512, :] = total.astype(BF)


def after(x, token):
    return lax.optimization_barrier((x, token))[0]


def swap(x, flip):
    n = lax.axis_size(AXIS)
    return lax.ppermute(x, AXIS, [(i, i ^ flip) for i in range(n)])


def per_device(
    points, charges, order, near, bases, lift_leaf, lift_node, proxy_leaf, proxy_node, proxy_top
):
    vm, sem = pltpu.VMEM, pltpu.SemaphoreType.DMA

    def chosen(got, own, skip=0):
        return call(
            functools.partial(choose_body, skip), [(got.shape, BF)], near, got, own, name="choose", smem=1
        )[0]

    def chunk(i):
        n = CHUNKS[i][1]
        v["acc", 0], v["acc", 1] = call(
            functools.partial(chunk_body, i), [((HALF, NRHS), F32)] * 2,
            v["own_l"], v["pts_a"], v["rows_a", i], v["pts_b"], v["rows_b", i], v["acc", 0], v["acc", 1],
            name="near_chunk", scratch=[vm((2 * n, 256), BF)], aliases={5: 0, 6: 1},
        )

    def own_half(i):
        v["acc", i], = call(
            functools.partial(own_body, i * HALF), [((HALF, NRHS), F32)],
            v["own_l"], v["own_r"], v["whole"], name="near_own",
        )

    v = {}

    def finish(new):
        v.update(new)
        keys = list(v)
        for key, value in zip(keys, lax.optimization_barrier([v[key] for key in keys])):
            v[key] = value

    pts_a = swap(points, 3)
    own_l, own_r, whole, *bufs, keep, send, z_own, lift_low, proxy_wide = call(
        prep_body,
        [((LEAF, 256), BF), ((LEAF, 256), BF), ((FAR + LEAF, 256), BF)]
        + [((base + n, 256), BF) for (_, n), base in zip(CHUNKS, BASES)]
        + [((128, 256), F32), ((192, 256), BF), ((40, 256), BF), ((256, 256), BF), ((256, 256), BF)],
        order, points, charges, bases, lift_leaf, proxy_leaf, lift_node, proxy_node, proxy_top,
        name="prep", hbm=tuple(range(9)),
        scratch=[
            vm((1, LEAF), jnp.int32), vm((LEAF, D), BF), vm((LEAF, 256), BF), vm((LEAF, 256), BF),
            vm((256, 256), F32), vm((256, 128), F32), vm((64, 256), F32), vm((64, 128), F32), vm((16, 128), F32),
            vm((256, 256), F32), sem((9,)),
        ],
    )
    v.update({("buf", i): buf for i, buf in enumerate(bufs)})
    finish(
        dict(
            own_l=own_l, own_r=own_r, whole=whole, keep=keep, send=send, z_own=z_own,
            lift_low=lift_low, proxy_wide=proxy_wide,
        )
    )

    got = swap(v["send"], 1)
    finish(dict(got=got))

    kept, send = call(
        halve_body, [((64, 256), F32), ((232, 256), BF)], v["keep"], v["send"], v["got"], v["z_own"],
        name="halve", scratch=[vm((128, 256), F32)],
    )
    got = swap(send, 2)
    own_half(0)
    own_half(1)
    finish(dict(got=got, kept=kept, send=send, pts_a=pts_a))

    send, lift_all = call(
        node_body, [((208, 256), BF), ((256, 256), BF)], v["kept"], v["send"], v["got"], name="node",
    )
    got = tuple(swap(send, k) for k in (6, 8, 14))
    rows_zero = swap(v["buf", 0], 3)
    v["pts_b"] = swap(chosen(v["pts_a"], v["own_l"]), 1)
    v["rows_a", 0] = rows_zero
    finish(dict(sibs=got, send=send, lift_all=lift_all))

    top, z_all = call(
        top_body, [((128, 256), BF), ((256, 256), BF)], v["send"], *v["sibs"], name="top"
    )
    got = tuple(swap(top, k) for k in (24, 32, 56))
    rows_one = swap(v["buf", 1], 3)
    v["rows_b", 0] = swap(chosen(v["rows_a", 0], v["buf", 0]), 1)
    chunk(0)
    finish(dict(got=got, low=top, z_all=z_all))

    low, = call(more_body, [((512, 256), BF)], v["low"], *v["got"], name="more")
    got = swap(low, 96)
    z_core = swap(v["z_all"], 1)
    low_core = swap(low, 1)
    rows_two = swap(v["buf", 2], 3)
    kernel_one, = call(
        node_coupling_body, [((768, 256), BF)], v["z_all"], z_core, name="node_coupling",
        scratch=[vm((1024, 128), BF)],
    )
    v["rows_a", 1] = rows_one
    finish(dict(got=got, low=low, low_core=low_core, kernel_one=kernel_one))

    high_core = swap(v["got"], 1)
    v["rows_b", 1] = swap(chosen(v["rows_a", 1], v["buf", 1], BASES[1]), 1)
    finish(dict(high_core=high_core))

    quarter, = call(
        field_body, [((64, 256), BF)], *v["sibs"], v["low"], v["got"], v["low_core"],
        v["high_core"], v["kernel_one"], v["lift_all"], name="field", scratch=[vm((2048, 128), F32)],
    )
    got = swap(quarter, 2)
    far, = call(far_body, [((256, 256), F32)], v["rows_b", 1], v["proxy_wide"], name="far")
    chunk(1)
    v["rows_a", 2] = rows_two
    finish(dict(got=got, quarter=quarter, far=far))

    half, = call(join_body, [((128, 256), BF)], v["quarter"], v["got"], name="join")
    v["rows_b", 2] = swap(chosen(v["rows_a", 2], v["buf", 2]), 1)
    got = swap(half, 1)
    chunk(2)
    out, = call(
        last_body, [((LEAF, NRHS), BF)],
        v["acc", 0], v["acc", 1], bases, v["far"], v["lift_low"], half, got,
        name="descent", scratch=[vm((256, 256), BF)],
    )
    return out


def solution(mesh):
    spec = P(AXIS, None)
    return jax.shard_map(
        per_device, mesh=mesh, in_specs=(spec,) * 10, out_specs=spec, check_vma=False
    )
```

time: 79.1 us -> 69.3 us (0.88)
  starting transfers between devices: 38.4 us -> 25 us
  waiting for transfers between devices: 9.04 us -> 15.8 us
  Pallas kernels: 30.1 us -> 28.2 us
  local copies, waits for them, and re-layouts: 1.08 us -> 0.01 us
    ppermute x28 -> x22, starting transfers between devices: 38.4 us -> 25 us  [swap(): return lax.ppermute(x, AXIS, [(i, i ^ flip) for i in range(n)])]
    ppermute x28 -> x22, waiting for transfers between devices: 9.04 us -> 15.8 us  [swap(): return lax.ppermute(x, AXIS, [(i, i ^ flip) for i in range(n)])]
    pallas_call x28 -> x19, Pallas kernels: 30.1 us -> 28.2 us  [call(): pl.pallas_call(body, out_shape=[jax.ShapeDtypeStruct(s, d) for s, d in ou...]
    slice x2 -> x0, local copies, waits for them, and re-layouts: 0.99 us -> none  [the longest x1 0.97 us: per_device(): across_a = swap(v['points'][:HALF], 3)]
  transfers between devices with their start and end apart: 28 -> 22, of which waited for: 7 -> 12; matrix products, arithmetic and copies ran while one was open for 0% -> 0% of each run, Pallas kernels for 30% -> 35%
where the time goes in v3:
time: 69.3 us; the launch traced here: 69.2 us
  Pallas kernels  28.2 us (41%)
  starting transfers between devices  25 us (36%)
  waiting for transfers between devices  15.8 us (23%)
    pallas_call x19, Pallas kernels, call(): pl.pallas_call(body, out_shape=[jax.ShapeDtypeStruct(s, d) for s, d in ou...  28.2 us
    ppermute x22, starting transfers between devices, swap(): return lax.ppermute(x, AXIS, [(i, i ^ flip) for i in range(n)])  25 us
    ppermute x22, waiting for transfers between devices, swap(): return lax.ppermute(x, AXIS, [(i, i ^ flip) for i in range(n)])  15.8 us
  transfers between devices with their start and end apart: 22, of which 12 were waited for; matrix products, arithmetic and copies ran while one was open for 0% of the time, Pallas kernels for 35%

profile of v3, /device:TPU:1, one launch (start us, length us, event | category | flops | bytes accessed | tf_op | source)
XLA Modules:
  0.0 69.2 jit_solution(7124291032797682715)
XLA Ops:
  0.0 2.6 %collective-permute-start.2 = (bf16[2048,128]{1,0:T(8,128)(2,1)}, bf16[2048,128]{1,0:T(8,128)(2,1)S(1)}, u32[]{:S(2)}, u32[]{:S(2)}) collective-permute-start(bf16[2048,128]{1,0:T(8,128)(2,1)} %points_h.1), channel_id=1, source_target_pairs={{0,3},{1,2},{2,1},{3,0},{4,7},{5,6},{6,5},{7,4},{8,11},{9,10},{10,... | collective-permute-start | bytes 1572872 | tf_op jit(solution)/shard_map/ppermute | solution.py:287
  2.6 5.4 %prep.1 = (bf16[2048,256]{1,0:T(8,128)(2,1)S(1)}, bf16[2048,256]{1,0:T(8,128)(2,1)S(1)}, bf16[2432,256]{1,0:T(8,128)(2,1)S(1)}, bf16[768,256]{1,0:T(8,128)(2,1)S...) custom-call(s32[1,2048]{1,0:T(1,128)} %order_h.1, ...), custom_call_target="tpu_custom_call" | custom-call | tf_op jit(solution)/shard_map/prep/pallas_call | solution.py:59
  8.1 1.3 %collective-permute-done.got = bf16[192,256]{1,0:T(8,128)(2,1)S(1)} collective-permute-done((bf16[192,256]{1,0:T(8,128)(2,1)S(1)}, bf16[192,256]{1,0:T(8,128)(2,1)S(1)}, u32[]{:S(2)}, u32[]{:S(2)}) %collective-permute-start) | collective-permute-done | bytes 98336 | tf_op jit(solution)/shard_map/ppermute | solution.py:287
  9.7 2.6 %near_own.2.in_a = f32[1024,256]{1,0:T(8,128)S(1)} custom-call(bf16[2048,256]{1,0:T(8,128)(2,1)S(1)} %get-tuple-element.272.own_l.own, bf16[2048,256]{1,0:T(8,128)(2,1)S(1)} %get-tuple-element.171.own_r, bf16[2432,256]{1,0:T(8,128)(2,1)S(1)} %get-tuple-element.172.whole), custom_call_target="tpu_custom_call" | custom-call | tf_op jit(solution)/shard_map/near_own/pallas_call | solution.py:59
  12.3 2.6 %near_own.3.in_b = f32[1024,256]{1,0:T(8,128)S(1)} custom-call(bf16[2048,256]{1,0:T(8,128)(2,1)S(1)} %get-tuple-element.272.own_l.own, bf16[2048,256]{1,0:T(8,128)(2,1)S(1)} %get-tuple-element.171.own_r, bf16[2432,256]{1,0:T(8,128)(2,1)S(1)} %get-tuple-element.172.whole), custom_call_target="tpu_custom_call" | custom-call | tf_op jit(solution)/shard_map/near_own/pallas_call | solution.py:59
  15.0 2.9 %collective-permute-done.1.got = bf16[232,256]{1,0:T(8,128)(2,1)S(1)} collective-permute-done((bf16[232,256]{1,0:T(8,128)(2,1)S(1)}, bf16[232,256]{1,0:T(8,128)(2,1)S(1)}, u32[]{:S(2)}, u32[]{:S(2)}) %collective-permute-start.1) | collective-permute-done | bytes 118816 | tf_op jit(solution)/shard_map/ppermute | solution.py:287
  19.1 1.3 %collective-permute-start.4 = (bf16[768,256]{1,0:T(8,128)(2,1)S(1)}, bf16[768,256]{1,0:T(8,128)(2,1)S(1)}, u32[]{:S(2)}, u32[]{:S(2)}) collective-permute-start(bf16[768,256]{1,0:T(8,128)(2,1)S(1)} %get-tuple-element.195.own), channel_id=1, source_target_pairs={{0,3},{1,2},{2,1},{3,0},{4,7},{5,6},{6,5},{7,4},{8,11},{9,10},{10,... | collective-permute-start | bytes 1179656 | tf_op jit(solution)/shard_map/ppermute | solution.py:287
  20.6 1.8 %collective-permute-start.5 = (bf16[208,256]{1,0:T(8,128)(2,1)S(1)}, bf16[208,256]{1,0:T(8,128)(2,1)S(1)}, u32[]{:S(2)}, u32[]{:S(2)}) collective-permute-start(bf16[208,256]{1,0:T(8,128)(2,1)S(1)} %get-tuple-element.199.mine), channel_id=1, source_target_pairs={{0,6},{1,7},{2,4},{3,5},{4,2},{5,3},{6,0},{7,1},{8,14},{9,15},{10,... | collective-permute-start | bytes 319496 | tf_op jit(solution)/shard_map/ppermute | solution.py:287
  22.4 1.4 %collective-permute-start.6 = (bf16[208,256]{1,0:T(8,128)(2,1)S(1)}, bf16[208,256]{1,0:T(8,128)(2,1)S(1)}, u32[]{:S(2)}, u32[]{:S(2)}) collective-permute-start(bf16[208,256]{1,0:T(8,128)(2,1)S(1)} %get-tuple-element.199.mine), channel_id=1, source_target_pairs={{0,8},{1,9},{2,10},{3,11},{4,12},{5,13},{6,14},{7,15},{8,0},{9,1},... | collective-permute-start | bytes 319496 | tf_op jit(solution)/shard_map/ppermute | solution.py:287
  23.7 0.7 %collective-permute-start.7 = (bf16[208,256]{1,0:T(8,128)(2,1)S(1)}, bf16[208,256]{1,0:T(8,128)(2,1)S(1)}, u32[]{:S(2)}, u32[]{:S(2)}) collective-permute-start(bf16[208,256]{1,0:T(8,128)(2,1)S(1)} %get-tuple-element.199.mine), channel_id=1, source_target_pairs={{0,14},{1,15},{2,12},{3,13},{4,10},{5,11},{6,8},{7,9},{8,6},{9,7},... | collective-permute-start | bytes 319496 | tf_op jit(solution)/shard_map/ppermute | solution.py:287
  24.5 1.5 %collective-permute-done.5.got_x.sib_x = bf16[208,256]{1,0:T(8,128)(2,1)S(1)} collective-permute-done((bf16[208,256]{1,0:T(8,128)(2,1)S(1)}, bf16[208,256]{1,0:T(8,128)(2,1)S(1)}, u32[]{:S(2)}, u32[]{:S(2)}) %collective-permute-start.5) | collective-permute-done | bytes 106528 | tf_op jit(solution)/shard_map/ppermute | solution.py:287
  26.2 3.2 %collective-permute-done.7.got_xy.sib_xy = bf16[208,256]{1,0:T(8,128)(2,1)S(1)} collective-permute-done((bf16[208,256]{1,0:T(8,128)(2,1)S(1)}, bf16[208,256]{1,0:T(8,128)(2,1)S(1)}, u32[]{:S(2)}, u32[]{:S(2)}) %collective-permute-start.7) | collective-permute-done | bytes 106528 | tf_op jit(solution)/shard_map/ppermute | solution.py:287
  29.4 0.9 %collective-permute-done.4.got.rows_a = bf16[768,256]{1,0:T(8,128)(2,1)S(1)} collective-permute-done((bf16[768,256]{1,0:T(8,128)(2,1)S(1)}, bf16[768,256]{1,0:T(8,128)(2,1)S(1)}, u32[]{:S(2)}, u32[]{:S(2)}) %collective-permute-start.4) | collective-permute-done | bytes 393248 | tf_op jit(solution)/shard_map/ppermute | solution.py:287
  30.9 1.5 %collective-permute-start.11 = (bf16[768,256]{1,0:T(8,128)(2,1)S(1)}, bf16[768,256]{1,0:T(8,128)(2,1)S(1)}, u32[]{:S(2)}, u32[]{:S(2)}) collective-permute-start(bf16[768,256]{1,0:T(8,128)(2,1)S(1)} %choose.5), channel_id=1, source_target_pairs={{0,1},{1,0},{2,3},{3,2},{4,5},{5,4},{6,7},{7,6},{8,9},{9,8},{10,11... | collective-permute-start | bytes 1179656 | tf_op jit(solution)/shard_map/ppermute | solution.py:287
  32.5 2.8 %collective-permute-start.8 = (bf16[128,256]{1,0:T(8,128)(2,1)S(1)}, bf16[128,256]{1,0:T(8,128)(2,1)S(1)}, u32[]{:S(2)}, u32[]{:S(2)}) collective-permute-start(bf16[128,256]{1,0:T(8,128)(2,1)S(1)} %get-tuple-element.220.mine), channel_id=1, source_target_pairs={{0,24},{1,25},{2,26},{3,27},{4,28},{5,29},{6,30},{7,31},{8,16},{9,... | collective-permute-start | bytes 196616 | tf_op jit(solution)/shard_map/ppermute | solution.py:287
  35.4 1.6 %collective-permute-start.9 = (bf16[128,256]{1,0:T(8,128)(2,1)S(1)}, bf16[128,256]{1,0:T(8,128)(2,1)S(1)}, u32[]{:S(2)}, u32[]{:S(2)}) collective-permute-start(bf16[128,256]{1,0:T(8,128)(2,1)S(1)} %get-tuple-element.220.mine), channel_id=1, source_target_pairs={{0,32},{1,33},{2,34},{3,35},{4,36},{5,37},{6,38},{7,39},{8,40},{9,... | collective-permute-start | bytes 196616 | tf_op jit(solution)/shard_map/ppermute | solution.py:287
  37.0 4.0 %near_chunk.3 = (f32[1024,256]{1,0:T(8,128)S(1)}, f32[1024,256]{1,0:T(8,128)S(1)}) custom-call(bf16[2048,256]{1,0:T(8,128)(2,1)S(1)} %get-tuple-element.272.own_l.own, bf16[2048,128]{1,0:T(8,128)(2,1)S(1)} %collective-permute-done.2.got.pts_a, bf16[768,256]{1,0:T(8,128)(2,1)S(1)} %collective-permute-done.4.got.rows_a, ...), custom_call_target="tpu_custom_call", output_to_operand_aliasing={{0}: (5, {}), {1}: (6, {})} | custom-call | tf_op jit(solution)/shard_map/near_chunk/pallas_call | solution.py:59
  41.0 1.2 %collective-permute-done.10.got_yz = bf16[128,256]{1,0:T(8,128)(2,1)S(1)} collective-permute-done((bf16[128,256]{1,0:T(8,128)(2,1)S(1)}, bf16[128,256]{1,0:T(8,128)(2,1)S(1)}, u32[]{:S(2)}, u32[]{:S(2)}) %collective-permute-start.10) | collective-permute-done | bytes 65568 | tf_op jit(solution)/shard_map/ppermute | solution.py:287
  42.2 2.3 %collective-permute-start.12 = (bf16[512,256]{1,0:T(8,128)(2,1)S(1)}, bf16[512,256]{1,0:T(8,128)(2,1)S(1)}, u32[]{:S(2)}, u32[]{:S(2)}) collective-permute-start(bf16[512,256]{1,0:T(8,128)(2,1)S(1)} %more.1.low), channel_id=1, source_target_pairs={{0,96},{1,97},{2,98},{3,99},{4,100},{5,101},{6,102},{7,103},{8,104... | collective-permute-start | bytes 786440 | tf_op jit(solution)/shard_map/ppermute | solution.py:287
  44.6 2.1 %collective-permute-start.14 = (bf16[512,256]{1,0:T(8,128)(2,1)S(1)}, bf16[512,256]{1,0:T(8,128)(2,1)S(1)}, u32[]{:S(2)}, u32[]{:S(2)}) collective-permute-start(bf16[512,256]{1,0:T(8,128)(2,1)S(1)} %more.1.low), channel_id=1, source_target_pairs={{0,1},{1,0},{2,3},{3,2},{4,5},{5,4},{6,7},{7,6},{8,9},{9,8},{10,11... | collective-permute-start | bytes 786440 | tf_op jit(solution)/shard_map/ppermute | solution.py:287
  46.7 1.3 %collective-permute-done.15.z_got = bf16[256,256]{1,0:T(8,128)(2,1)S(1)} collective-permute-done((bf16[256,256]{1,0:T(8,128)(2,1)S(1)}, bf16[256,256]{1,0:T(8,128)(2,1)S(1)}, u32[]{:S(2)}, u32[]{:S(2)}) %collective-permute-start.15) | collective-permute-done | bytes 131104 | tf_op jit(solution)/shard_map/ppermute | solution.py:287
  48.6 0.9 %collective-permute-done.12.high = bf16[512,256]{1,0:T(8,128)(2,1)S(1)} collective-permute-done((bf16[512,256]{1,0:T(8,128)(2,1)S(1)}, bf16[512,256]{1,0:T(8,128)(2,1)S(1)}, u32[]{:S(2)}, u32[]{:S(2)}) %collective-permute-start.12) | collective-permute-done | bytes 262176 | tf_op jit(solution)/shard_map/ppermute | solution.py:287
  50.1 2.9 %collective-permute-start.16 = (bf16[1152,256]{1,0:T(8,128)(2,1)S(1)}, bf16[1152,256]{1,0:T(8,128)(2,1)S(1)}, u32[]{:S(2)}, u32[]{:S(2)}) collective-permute-start(bf16[1152,256]{1,0:T(8,128)(2,1)S(1)} %choose.6), channel_id=1, source_target_pairs={{0,1},{1,0},{2,3},{3,2},{4,5},{5,4},{6,7},{7,6},{8,9},{9,8},{10,11... | collective-permute-start | bytes 1769480 | tf_op jit(solution)/shard_map/ppermute | solution.py:287
  53.0 1.0 %collective-permute-start.19 = (bf16[512,256]{1,0:T(8,128)(2,1)S(1)}, bf16[512,256]{1,0:T(8,128)(2,1)S(1)}, u32[]{:S(2)}, u32[]{:S(2)}) collective-permute-start(bf16[512,256]{1,0:T(8,128)(2,1)S(1)} %get-tuple-element.276.own), channel_id=1, source_target_pairs={{0,3},{1,2},{2,1},{3,0},{4,7},{5,6},{6,5},{7,4},{8,11},{9,10},{10,... | collective-permute-start | bytes 786440 | tf_op jit(solution)/shard_map/ppermute | solution.py:287
  54.0 1.0 %collective-permute-done.17.high_core = bf16[512,256]{1,0:T(8,128)(2,1)S(1)} collective-permute-done((bf16[512,256]{1,0:T(8,128)(2,1)S(1)}, bf16[512,256]{1,0:T(8,128)(2,1)S(1)}, u32[]{:S(2)}, u32[]{:S(2)}) %collective-permute-start.17) | collective-permute-done | bytes 262176 | tf_op jit(solution)/shard_map/ppermute | solution.py:287
  55.0 1.4 %field.1.mine = bf16[64,256]{1,0:T(8,128)(2,1)S(1)} custom-call(bf16[208,256]{1,0:T(8,128)(2,1)S(1)} %collective-permute-done.5.got_x.sib_x, bf16[208,256]{1,0:T(8,128)(2,1)S(1)} %collective-permute-done.6.got_y.sib_y, bf16[208,256]{1,0:T(8,128)(2,1)S(1)} %collective-permute-done.7.got_xy.sib_xy, bf16[512,256]{1,0:T(8,128)(2,1)S(1)} %more.1.low, ...), custom_call_target="tpu_custom_call" | custom-call | tf_op jit(solution)/shard_map/field/pallas_call | solution.py:59
  56.3 0.9 %collective-permute-start.18 = (bf16[64,256]{1,0:T(8,128)(2,1)S(1)}, bf16[64,256]{1,0:T(8,128)(2,1)S(1)}, u32[]{:S(2)}, u32[]{:S(2)}) collective-permute-start(bf16[64,256]{1,0:T(8,128)(2,1)S(1)} %field.1.mine), channel_id=1, source_target_pairs={{0,2},{1,3},{2,0},{3,1},{4,6},{5,7},{6,4},{7,5},{8,10},{9,11},{10,... | collective-permute-start | bytes 98312 | tf_op jit(solution)/shard_map/ppermute | solution.py:287
  57.8 4.0 %near_chunk.4 = (f32[1024,256]{1,0:T(8,128)S(1)}, f32[1024,256]{1,0:T(8,128)S(1)}) custom-call(bf16[2048,256]{1,0:T(8,128)(2,1)S(1)} %get-tuple-element.272.own_l.own, bf16[2048,128]{1,0:T(8,128)(2,1)S(1)} %collective-permute-done.2.got.pts_a, ...), custom_call_target="tpu_custom_call", output_to_operand_aliasing={{0}: (5, {}), {1}: (6, {})} | custom-call | tf_op jit(solution)/shard_map/near_chunk/pallas_call | solution.py:59
  62.7 0.7 %collective-permute-start.20 = (bf16[512,256]{1,0:T(8,128)(2,1)S(1)}, bf16[512,256]{1,0:T(8,128)(2,1)S(1)}, u32[]{:S(2)}, u32[]{:S(2)}) collective-permute-start(bf16[512,256]{1,0:T(8,128)(2,1)S(1)} %choose.7), channel_id=1, source_target_pairs={{0,1},{1,0},{2,3},{3,2},{4,5},{5,4},{6,7},{7,6},{8,9},{9,8},{10,11... | collective-permute-start | bytes 786440 | tf_op jit(solution)/shard_map/ppermute | solution.py:287
  63.6 1.0 %collective-permute-done.20.rows_b = bf16[512,256]{1,0:T(8,128)(2,1)S(1)} collective-permute-done((bf16[512,256]{1,0:T(8,128)(2,1)S(1)}, bf16[512,256]{1,0:T(8,128)(2,1)S(1)}, u32[]{:S(2)}, u32[]{:S(2)}) %collective-permute-start.20) | collective-permute-done | bytes 262176 | tf_op jit(solution)/shard_map/ppermute | solution.py:287
  64.6 2.9 %near_chunk.5 = (f32[1024,256]{1,0:T(8,128)S(1)}, f32[1024,256]{1,0:T(8,128)S(1)}) custom-call(bf16[2048,256]{1,0:T(8,128)(2,1)S(1)} %get-tuple-element.272.own_l.own, bf16[2048,128]{1,0:T(8,128)(2,1)S(1)} %collective-permute-done.2.got.pts_a, bf16[512,256]{1,0:T(8,128)(2,1)S(1)} %collective-permute-done.19.got.rows_a, ...), custom_call_target="tpu_custom_call", output_to_operand_aliasing={{0}: (5, {}), {1}: (6, {})} | custom-call | tf_op jit(solution)/shard_map/near_chunk/pallas_call | solution.py:59
  67.5 1.7 %descent.1 = bf16[2048,256]{1,0:T(8,128)(2,1)} custom-call(f32[1024,256]{1,0:T(8,128)S(1)} %get-tuple-element.279.acc_a, f32[1024,256]{1,0:T(8,128)S(1)} %get-tuple-element.280.acc_b, bf16[2048,256]{1,0:T(8,128)(2,1)S(1)} %copy-done, f32[256,256]{1,0:T(8,128)S(1)} %far.1, bf16[256,256]{1,0:T(8,128)(2,1)S(1)} %get-tuple-element.282.lift, ...), custom_call_target="tpu_custom_call" | custom-call | tf_op jit(solution)/shard_map/descent/pallas_call | solution.py:59
  (35 shorter events, 5.5 us)
Async XLA Ops:
  0.0 17.9 %collective-permute-start.2 = (bf16[2048,128]{1,0:T(8,128)(2,1)}, bf16[2048,128]{1,0:T(8,128)(2,1)S(1)}, u32[]{:S(2)}, u32[]{:S(2)}) collective-permute-start(bf16[2048,128]{1,0:T(8,128)(2,1)} %points_h.1), channel_id=1, source_target_pairs={{0,3},{1,2},{2,1},{3,0},{4,7},{5,6},{6,5},{7,4},{8,11},{9,10},{10,... | collective-permute-start | bytes 1572872 | tf_op jit(solution)/shard_map/ppermute | solution.py:287
  8.0 1.4 %collective-permute-start = (bf16[192,256]{1,0:T(8,128)(2,1)S(1)}, bf16[192,256]{1,0:T(8,128)(2,1)S(1)}, u32[]{:S(2)}, u32[]{:S(2)}) collective-permute-start(bf16[192,256]{1,0:T(8,128)(2,1)S(1)} %get-tuple-element.174.sent), channel_id=1, source_target_pairs={{0,1},{1,0},{2,3},{3,2},{4,5},{5,4},{6,7},{7,6},{8,9},{9,8},{10,11... | collective-permute-start | bytes 294920 | tf_op jit(solution)/shard_map/ppermute | solution.py:287
  9.4 8.5 %collective-permute-start.1 = (bf16[232,256]{1,0:T(8,128)(2,1)S(1)}, bf16[232,256]{1,0:T(8,128)(2,1)S(1)}, u32[]{:S(2)}, u32[]{:S(2)}) collective-permute-start(bf16[232,256]{1,0:T(8,128)(2,1)S(1)} %get-tuple-element.186.sent), channel_id=1, source_target_pairs={{0,2},{1,3},{2,0},{3,1},{4,6},{5,7},{6,4},{7,5},{8,10},{9,11},{10,... | collective-permute-start | bytes 356360 | tf_op jit(solution)/shard_map/ppermute | solution.py:287
  12.3 5.6 %copy-start.1 = (s32[1,2]{1,0:T(1,128)S(1)}, s32[1,2]{1,0:T(1,128)}, u32[]{:S(2)}) copy-start(s32[1,2]{1,0:T(1,128)} %near.7) | copy-start | bytes 28
  18.5 11.7 %collective-permute-start.3 = (bf16[2048,128]{1,0:T(8,128)(2,1)S(1)}, bf16[2048,128]{1,0:T(8,128)(2,1)S(1)}, u32[]{:S(2)}, u32[]{:S(2)}) collective-permute-start(bf16[2048,128]{1,0:T(8,128)(2,1)S(1)} %choose.4), channel_id=1, source_target_pairs={{0,1},{1,0},{2,3},{3,2},{4,5},{5,4},{6,7},{7,6},{8,9},{9,8},{10,11... | collective-permute-start | bytes 1572872 | tf_op jit(solution)/shard_map/ppermute | solution.py:287
  19.1 11.1 %collective-permute-start.4 = (bf16[768,256]{1,0:T(8,128)(2,1)S(1)}, bf16[768,256]{1,0:T(8,128)(2,1)S(1)}, u32[]{:S(2)}, u32[]{:S(2)}) collective-permute-start(bf16[768,256]{1,0:T(8,128)(2,1)S(1)} %get-tuple-element.195.own), channel_id=1, source_target_pairs={{0,3},{1,2},{2,1},{3,0},{4,7},{5,6},{6,5},{7,4},{8,11},{9,10},{10,... | collective-permute-start | bytes 1179656 | tf_op jit(solution)/shard_map/ppermute | solution.py:287
  20.6 5.3 %collective-permute-start.5 = (bf16[208,256]{1,0:T(8,128)(2,1)S(1)}, bf16[208,256]{1,0:T(8,128)(2,1)S(1)}, u32[]{:S(2)}, u32[]{:S(2)}) collective-permute-start(bf16[208,256]{1,0:T(8,128)(2,1)S(1)} %get-tuple-element.199.mine), channel_id=1, source_target_pairs={{0,6},{1,7},{2,4},{3,5},{4,2},{5,3},{6,0},{7,1},{8,14},{9,15},{10,... | collective-permute-start | bytes 319496 | tf_op jit(solution)/shard_map/ppermute | solution.py:287
  22.4 3.9 %collective-permute-start.6 = (bf16[208,256]{1,0:T(8,128)(2,1)S(1)}, bf16[208,256]{1,0:T(8,128)(2,1)S(1)}, u32[]{:S(2)}, u32[]{:S(2)}) collective-permute-start(bf16[208,256]{1,0:T(8,128)(2,1)S(1)} %get-tuple-element.199.mine), channel_id=1, source_target_pairs={{0,8},{1,9},{2,10},{3,11},{4,12},{5,13},{6,14},{7,15},{8,0},{9,1},... | collective-permute-start | bytes 319496 | tf_op jit(solution)/shard_map/ppermute | solution.py:287
  23.7 5.7 %collective-permute-start.7 = (bf16[208,256]{1,0:T(8,128)(2,1)S(1)}, bf16[208,256]{1,0:T(8,128)(2,1)S(1)}, u32[]{:S(2)}, u32[]{:S(2)}) collective-permute-start(bf16[208,256]{1,0:T(8,128)(2,1)S(1)} %get-tuple-element.199.mine), channel_id=1, source_target_pairs={{0,14},{1,15},{2,12},{3,13},{4,10},{5,11},{6,8},{7,9},{8,6},{9,7},... | collective-permute-start | bytes 319496 | tf_op jit(solution)/shard_map/ppermute | solution.py:287
  30.9 6.1 %collective-permute-start.11 = (bf16[768,256]{1,0:T(8,128)(2,1)S(1)}, bf16[768,256]{1,0:T(8,128)(2,1)S(1)}, u32[]{:S(2)}, u32[]{:S(2)}) collective-permute-start(bf16[768,256]{1,0:T(8,128)(2,1)S(1)} %choose.5), channel_id=1, source_target_pairs={{0,1},{1,0},{2,3},{3,2},{4,5},{5,4},{6,7},{7,6},{8,9},{9,8},{10,11... | collective-permute-start | bytes 1179656 | tf_op jit(solution)/shard_map/ppermute | solution.py:287
  32.4 16.2 %collective-permute-start.13 = (bf16[1152,256]{1,0:T(8,128)(2,1)S(1)}, bf16[1152,256]{1,0:T(8,128)(2,1)S(1)}, u32[]{:S(2)}, u32[]{:S(2)}) collective-permute-start(bf16[1152,256]{1,0:T(8,128)(2,1)S(1)} %get-tuple-element.233.own), channel_id=1, source_target_pairs={{0,3},{1,2},{2,1},{3,0},{4,7},{5,6},{6,5},{7,4},{8,11},{9,10},{10,... | collective-permute-start | bytes 1769480 | tf_op jit(solution)/shard_map/ppermute | solution.py:287
  32.5 8.5 %collective-permute-start.8 = (bf16[128,256]{1,0:T(8,128)(2,1)S(1)}, bf16[128,256]{1,0:T(8,128)(2,1)S(1)}, u32[]{:S(2)}, u32[]{:S(2)}) collective-permute-start(bf16[128,256]{1,0:T(8,128)(2,1)S(1)} %get-tuple-element.220.mine), channel_id=1, source_target_pairs={{0,24},{1,25},{2,26},{3,27},{4,28},{5,29},{6,30},{7,31},{8,16},{9,... | collective-permute-start | bytes 196616 | tf_op jit(solution)/shard_map/ppermute | solution.py:287
  35.4 5.7 %collective-permute-start.9 = (bf16[128,256]{1,0:T(8,128)(2,1)S(1)}, bf16[128,256]{1,0:T(8,128)(2,1)S(1)}, u32[]{:S(2)}, u32[]{:S(2)}) collective-permute-start(bf16[128,256]{1,0:T(8,128)(2,1)S(1)} %get-tuple-element.220.mine), channel_id=1, source_target_pairs={{0,32},{1,33},{2,34},{3,35},{4,36},{5,37},{6,38},{7,39},{8,40},{9,... | collective-permute-start | bytes 196616 | tf_op jit(solution)/shard_map/ppermute | solution.py:287
  37.0 5.2 %collective-permute-start.10 = (bf16[128,256]{1,0:T(8,128)(2,1)S(1)}, bf16[128,256]{1,0:T(8,128)(2,1)S(1)}, u32[]{:S(2)}, u32[]{:S(2)}) collective-permute-start(bf16[128,256]{1,0:T(8,128)(2,1)S(1)} %get-tuple-element.220.mine), channel_id=1, source_target_pairs={{0,56},{1,57},{2,58},{3,59},{4,60},{5,61},{6,62},{7,63},{8,48},{9,... | collective-permute-start | bytes 196616 | tf_op jit(solution)/shard_map/ppermute | solution.py:287
  42.2 7.2 %collective-permute-start.12 = (bf16[512,256]{1,0:T(8,128)(2,1)S(1)}, bf16[512,256]{1,0:T(8,128)(2,1)S(1)}, u32[]{:S(2)}, u32[]{:S(2)}) collective-permute-start(bf16[512,256]{1,0:T(8,128)(2,1)S(1)} %more.1.low), channel_id=1, source_target_pairs={{0,96},{1,97},{2,98},{3,99},{4,100},{5,101},{6,102},{7,103},{8,104... | collective-permute-start | bytes 786440 | tf_op jit(solution)/shard_map/ppermute | solution.py:287
  44.6 4.9 %collective-permute-start.14 = (bf16[512,256]{1,0:T(8,128)(2,1)S(1)}, bf16[512,256]{1,0:T(8,128)(2,1)S(1)}, u32[]{:S(2)}, u32[]{:S(2)}) collective-permute-start(bf16[512,256]{1,0:T(8,128)(2,1)S(1)} %more.1.low), channel_id=1, source_target_pairs={{0,1},{1,0},{2,3},{3,2},{4,5},{5,4},{6,7},{7,6},{8,9},{9,8},{10,11... | collective-permute-start | bytes 786440 | tf_op jit(solution)/shard_map/ppermute | solution.py:287
  46.7 1.3 %collective-permute-start.15 = (bf16[256,256]{1,0:T(8,128)(2,1)S(1)}, bf16[256,256]{1,0:T(8,128)(2,1)S(1)}, u32[]{:S(2)}, u32[]{:S(2)}) collective-permute-start(bf16[256,256]{1,0:T(8,128)(2,1)S(1)} %get-tuple-element.232.z_own), channel_id=1, source_target_pairs={{0,1},{1,0},{2,3},{3,2},{4,5},{5,4},{6,7},{7,6},{8,9},{9,8},{10,11... | collective-permute-start | bytes 393224 | tf_op jit(solution)/shard_map/ppermute | solution.py:287
  50.1 4.9 %collective-permute-start.16 = (bf16[1152,256]{1,0:T(8,128)(2,1)S(1)}, bf16[1152,256]{1,0:T(8,128)(2,1)S(1)}, u32[]{:S(2)}, u32[]{:S(2)}) collective-permute-start(bf16[1152,256]{1,0:T(8,128)(2,1)S(1)} %choose.6), channel_id=1, source_target_pairs={{0,1},{1,0},{2,3},{3,2},{4,5},{5,4},{6,7},{7,6},{8,9},{9,8},{10,11... | collective-permute-start | bytes 1769480 | tf_op jit(solution)/shard_map/ppermute | solution.py:287
  52.9 2.0 %collective-permute-start.17 = (bf16[512,256]{1,0:T(8,128)(2,1)S(1)}, bf16[512,256]{1,0:T(8,128)(2,1)S(1)}, u32[]{:S(2)}, u32[]{:S(2)}) collective-permute-start(bf16[512,256]{1,0:T(8,128)(2,1)S(1)} %collective-permute-done.12.high), channel_id=1, source_target_pairs={{0,1},{1,0},{2,3},{3,2},{4,5},{5,4},{6,7},{7,6},{8,9},{9,8},{10,11... | collective-permute-start | bytes 786440 | tf_op jit(solution)/shard_map/ppermute | solution.py:287
  53.0 8.7 %collective-permute-start.19 = (bf16[512,256]{1,0:T(8,128)(2,1)S(1)}, bf16[512,256]{1,0:T(8,128)(2,1)S(1)}, u32[]{:S(2)}, u32[]{:S(2)}) collective-permute-start(bf16[512,256]{1,0:T(8,128)(2,1)S(1)} %get-tuple-element.276.own), channel_id=1, source_target_pairs={{0,3},{1,2},{2,1},{3,0},{4,7},{5,6},{6,5},{7,4},{8,11},{9,10},{10,... | collective-permute-start | bytes 786440 | tf_op jit(solution)/shard_map/ppermute | solution.py:287
  56.3 5.8 %collective-permute-start.18 = (bf16[64,256]{1,0:T(8,128)(2,1)S(1)}, bf16[64,256]{1,0:T(8,128)(2,1)S(1)}, u32[]{:S(2)}, u32[]{:S(2)}) collective-permute-start(bf16[64,256]{1,0:T(8,128)(2,1)S(1)} %field.1.mine), channel_id=1, source_target_pairs={{0,2},{1,3},{2,0},{3,1},{4,6},{5,7},{6,4},{7,5},{8,10},{9,11},{10,... | collective-permute-start | bytes 98312 | tf_op jit(solution)/shard_map/ppermute | solution.py:287
  62.7 1.9 %collective-permute-start.20 = (bf16[512,256]{1,0:T(8,128)(2,1)S(1)}, bf16[512,256]{1,0:T(8,128)(2,1)S(1)}, u32[]{:S(2)}, u32[]{:S(2)}) collective-permute-start(bf16[512,256]{1,0:T(8,128)(2,1)S(1)} %choose.7), channel_id=1, source_target_pairs={{0,1},{1,0},{2,3},{3,2},{4,5},{5,4},{6,7},{7,6},{8,9},{9,8},{10,11... | collective-permute-start | bytes 786440 | tf_op jit(solution)/shard_map/ppermute | solution.py:287
  63.4 4.0 %copy-start = (bf16[2048,256]{1,0:T(8,128)(2,1)S(1)}, bf16[2048,256]{1,0:T(8,128)(2,1)}, u32[]{:S(2)}) copy-start(bf16[2048,256]{1,0:T(8,128)(2,1)} %bases.1) | copy-start | bytes 3145732
  63.4 4.0 %collective-permute-start.21 = (bf16[128,256]{1,0:T(8,128)(2,1)S(1)}, bf16[128,256]{1,0:T(8,128)(2,1)S(1)}, u32[]{:S(2)}, u32[]{:S(2)}) collective-permute-start(bf16[128,256]{1,0:T(8,128)(2,1)S(1)} %join.1.half), channel_id=1, source_target_pairs={{0,1},{1,0},{2,3},{3,2},{4,5},{5,4},{6,7},{7,6},{8,9},{9,8},{10,11... | collective-permute-start | bytes 196616 | tf_op jit(solution)/shard_map/ppermute | solution.py:287

commit v4 on v3

--- a/solution.py
+++ b/solution.py
@@ -17,7 +17,7 @@
 SCALE = 4.0 / D * 1.4426950408889634
 FAR = 384
 CHUNKS = ((0, 768), (768, 768), (1536, 512))
-BASES = (0, FAR, 0)
+BASES = (FAR, 0, 0)
 HALF = LEAF // 2
 
 
@@ -49,7 +49,7 @@
     return jnp.exp2(dot_t(left, right) * SCALE).astype(BF)
 
 
-def call(body, outs, *args, name, scratch=(), smem=0, hbm=(), aliases=None, limit=24):
+def call(body, outs, *args, name, scratch=(), smem=0, hbm=(), aliases=None, out_space=pltpu.VMEM):
     def space(i):
         return pltpu.SMEM if i < smem else pltpu.HBM if i in hbm else pltpu.VMEM
 
@@ -60,12 +60,12 @@
         body,
         out_shape=[jax.ShapeDtypeStruct(s, d) for s, d in outs],
         in_specs=[pl.BlockSpec(memory_space=space(i)) for i in range(len(args))],
-        out_specs=[pl.BlockSpec(memory_space=pltpu.VMEM)] * len(outs),
+        out_specs=[pl.BlockSpec(memory_space=out_space)] * len(outs),
         scratch_shapes=list(scratch),
         input_output_aliases=aliases or {},
         name=name,
         cost_estimate=pl.CostEstimate(flops=0, bytes_accessed=0, transcendentals=0),
-        compiler_params=pltpu.CompilerParams(vmem_limit_bytes=limit << 20),
+        compiler_params=pltpu.CompilerParams(vmem_limit_bytes=24 << 20),
     )(*args)
 
 
@@ -158,18 +158,20 @@
     send[200:208, :] = got[224:232, :]
 
 
-def top_body(mine, got_x, got_y, got_xy, out, z_out):
+def top_body(mine, got_x, got_y, got_xy, out, z_out, t_out):
     four = (mine, got_x, got_y, got_xy)
     out[0:64, :] = sum(part[64:128, :].astype(F32) for part in four).astype(BF)
     for h, part in enumerate(four):
         out[64 + 16 * h : 80 + 16 * h, :] = part[192:208, :]
+        t_out[16 * h : 16 * h + 16, :] = part[192:208, :]
         z_out[64 * h : 64 * h + 64, :] = part[128:192, :]
 
 
-def more_body(mine, got_y, got_z, got_yz, out):
+def more_body(mine, got_y, got_z, got_yz, z_all, out, side):
     for r, part in enumerate((mine, got_y, got_z, got_yz)):
         out[64 * r : 64 * r + 64, :] = part[0:64, :]
-        out[256 + 64 * r : 320 + 64 * r, :] = part[64:128, :]
+        side[64 * r : 64 * r + 64, :] = part[64:128, :]
+    side[256:, :] = z_all[...]
 
 
 def node_coupling_body(z_own, z_got, out, z_node):
@@ -177,7 +179,8 @@
     for h in range(4):
         for core in range(2):
             for j in range(2):
-                block = (z_got if core else z_own)[(2 * h + j) * 32 : (2 * h + j + 1) * 32, :]
+                row = (256 if core else 0) + (2 * h + j) * 32
+                block = (z_got if core else z_own)[row : row + 32, :]
                 at = (slot ^ core ^ (2 * j) ^ (2 * (h % 2))) * 64
                 z_node[pl.ds(pl.multiple_of(h * 256 + at, 64), 32), :] = block[:, 0:D]
                 z_node[pl.ds(pl.multiple_of(h * 256 + at + 32, 32), 32), :] = block[:, D:]
@@ -186,27 +189,32 @@
         out[(h - 1) * 256 : h * 256, :] = gauss(widened(z_node[h * 256 : (h + 1) * 256, :], True), own)
 
 
-def field_body(
-    sib_x, sib_y, sib_xy, low, high, low_core, high_core, kernel_one, lift, out, z_top
-):
+def top_coupling_body(low, side, side_core, across, across_core, own_field, send, z_top):
     part = place()[3]
-    for r in range(8):
+    for r in range(5):
         for core in range(2):
-            mine = ((low, high), (low_core, high_core))[core][r // 4]
             for k in range(8):
                 offset = core ^ (2 * (k % 2)) ^ (6 * (k // 2 % 2)) ^ (8 * (k // 4)) ^ (8 * (r % 2))
-                row = 256 + 64 * (r % 4) + 8 * k
-                block = mine[row : row + 8, :].astype(F32)
+                rows, first = ((across, across_core), 0) if r == 4 else ((side, side_core), 64 * r)
+                block = rows[core][first + 8 * k : first + 8 * k + 8, :].astype(F32)
                 at = 256 * r + (part ^ offset) * 16
                 z_top[pl.ds(pl.multiple_of(at, 16), 8), :] = block[:, 0:D]
                 z_top[pl.ds(pl.multiple_of(at + 8, 8), 8), :] = block[:, D:]
     own = widened(z_top[0:256, :], False)
-    field = None
-    for r in range(1, 8):
-        tile = gauss(widened(z_top[r * 256 : (r + 1) * 256, :], True), own)
-        part = dot((low, high)[r // 4][64 * (r % 4) : 64 * (r % 4 + 1), :], tile)
-        field = part if field is None else field + part
-    total = dot_t(field.astype(BF), lift[...])
+    other = widened(z_top[1024:1280, :], False)
+    sums = [None, None]
+    for r in range(4):
+        left = widened(z_top[r * 256 : (r + 1) * 256, :], True)
+        for i, right in enumerate((own, other)):
+            if r or i:
+                term = dot(low[64 * r : 64 * r + 64, :], gauss(left, right))
+                sums[i] = term if sums[i] is None else sums[i] + term
+    own_field[...] = sums[0]
+    send[...] = sums[1].astype(BF)
+
+
+def field_body(sib_x, sib_y, sib_xy, own_field, got, kernel_one, lift, out):
+    total = dot_t((own_field[...] + got[...].astype(F32)).astype(BF), lift[...])
     for h, sib in enumerate((sib_x, sib_y, sib_xy)):
         total += dot(sib[0:64, :], kernel_one[256 * h : 256 * (h + 1), :])
     out[...] = total.astype(BF)
@@ -267,15 +275,21 @@
     out[...] = dot(rows[0:RANK, :], gauss(widened(z_far, True), proxy[...]))
 
 
-def last_body(acc_a, acc_b, bases, far, lift, half, got, out, node):
+def last_body(in_a, in_b, bases, far, lift, half, got, out_h, node, out, sems):
     core = place()[0]
     node[pl.ds(pl.multiple_of(core * 128, 128), 128), :] = half[...]
     node[pl.ds(pl.multiple_of((1 - core) * 128, 128), 128), :] = got[...]
     field = (far[...] + dot_t(node[...], lift[...])).astype(BF)
-    for r in range(0, LEAF, 512):
-        acc = (acc_a, acc_b)[r // HALF]
-        total = acc[r % HALF : r % HALF + 512, :] + dot_t(bases[r : r + 512, :], field)
-        out[r : r + 512, :] = total.astype(BF)
+    copies = []
+    for r in range(0, LEAF, 256):
+        total = (in_a, in_b)[r // HALF][r % HALF : r % HALF + 256, :] + dot_t(bases[r : r + 256, :], field)
+        out[r : r + 256, :] = total.astype(BF)
+        copies.append(
+            pltpu.make_async_copy(out.at[r : r + 256, :], out_h.at[r : r + 256, :], sems.at[r // 256])
+        )
+        copies[-1].start()
+    for copy in copies:
+        copy.wait()
 
 
 def after(x, token):
@@ -349,6 +363,7 @@
         name="halve", scratch=[vm((128, 256), F32)],
     )
     got = swap(send, 2)
+    rows_zero = swap(v["buf", 0], 3)
     own_half(0)
     own_half(1)
     finish(dict(got=got, kept=kept, send=send, pts_a=pts_a))
@@ -357,54 +372,61 @@
         node_body, [((208, 256), BF), ((256, 256), BF)], v["kept"], v["send"], v["got"], name="node",
     )
     got = tuple(swap(send, k) for k in (6, 8, 14))
-    rows_zero = swap(v["buf", 0], 3)
     v["pts_b"] = swap(chosen(v["pts_a"], v["own_l"]), 1)
     v["rows_a", 0] = rows_zero
     finish(dict(sibs=got, send=send, lift_all=lift_all))
 
-    top, z_all = call(
-        top_body, [((128, 256), BF), ((256, 256), BF)], v["send"], *v["sibs"], name="top"
+    top, z_all, t_own = call(
+        top_body, [((128, 256), BF), ((256, 256), BF), ((64, 256), BF)], v["send"], *v["sibs"], name="top"
     )
     got = tuple(swap(top, k) for k in (24, 32, 56))
     rows_one = swap(v["buf", 1], 3)
-    v["rows_b", 0] = swap(chosen(v["rows_a", 0], v["buf", 0]), 1)
+    v["rows_b", 0] = swap(chosen(v["rows_a", 0], v["buf", 0], FAR), 1)
     chunk(0)
-    finish(dict(got=got, low=top, z_all=z_all))
-
-    low, = call(more_body, [((512, 256), BF)], v["low"], *v["got"], name="more")
-    got = swap(low, 96)
-    z_core = swap(v["z_all"], 1)
-    low_core = swap(low, 1)
+    finish(dict(got=got, low=top, z_all=z_all, t_own=t_own))
+
+    across = swap(v["t_own"], 96)
+    low, side = call(
+        more_body, [((256, 256), BF), ((512, 256), BF)], v["low"], *v["got"], v["z_all"], name="more"
+    )
+    side_core = swap(side, 1)
     rows_two = swap(v["buf", 2], 3)
+    far, = call(far_body, [((256, 256), F32)], v["rows_b", 0], v["proxy_wide"], name="far")
+    v["rows_a", 1] = rows_one
+    finish(dict(low=low, side=side, side_core=side_core, far=far, across=across))
+
+    across_core = swap(v["across"], 1)
+    rows_b_one = swap(chosen(v["rows_a", 1], v["buf", 1]), 1)
     kernel_one, = call(
-        node_coupling_body, [((768, 256), BF)], v["z_all"], z_core, name="node_coupling",
+        node_coupling_body, [((768, 256), BF)], v["z_all"], v["side_core"], name="node_coupling",
         scratch=[vm((1024, 128), BF)],
     )
-    v["rows_a", 1] = rows_one
-    finish(dict(got=got, low=low, low_core=low_core, kernel_one=kernel_one))
-
-    high_core = swap(v["got"], 1)
-    v["rows_b", 1] = swap(chosen(v["rows_a", 1], v["buf", 1], BASES[1]), 1)
-    finish(dict(high_core=high_core))
-
-    quarter, = call(
-        field_body, [((64, 256), BF)], *v["sibs"], v["low"], v["got"], v["low_core"],
-        v["high_core"], v["kernel_one"], v["lift_all"], name="field", scratch=[vm((2048, 128), F32)],
-    )
-    got = swap(quarter, 2)
-    far, = call(far_body, [((256, 256), F32)], v["rows_b", 1], v["proxy_wide"], name="far")
+    finish(dict(across_core=across_core, kernel_one=kernel_one))
+
+    own_field, send = call(
+        top_coupling_body, [((64, 256), F32), ((64, 256), BF)], v["low"], v["side"], v["side_core"],
+        v["across"], v["across_core"], name="top_coupling", scratch=[vm((1280, 128), F32)],
+    )
+    got = swap(send, 96)
+    v["rows_b", 1] = rows_b_one
     chunk(1)
     v["rows_a", 2] = rows_two
-    finish(dict(got=got, quarter=quarter, far=far))
+    finish(dict(got=got, own_field=own_field))
+
+    quarter, = call(
+        field_body, [((64, 256), BF)], *v["sibs"], v["own_field"], v["got"], v["kernel_one"], v["lift_all"],
+        name="field",
+    )
+    got = swap(quarter, 2)
+    v["rows_b", 2] = swap(chosen(v["rows_a", 2], v["buf", 2]), 1)
+    chunk(2)
+    finish(dict(got=got, quarter=quarter))
 
     half, = call(join_body, [((128, 256), BF)], v["quarter"], v["got"], name="join")
-    v["rows_b", 2] = swap(chosen(v["rows_a", 2], v["buf", 2]), 1)
-    got = swap(half, 1)
-    chunk(2)
     out, = call(
         last_body, [((LEAF, NRHS), BF)],
-        v["acc", 0], v["acc", 1], bases, v["far"], v["lift_low"], half, got,
-        name="descent", scratch=[vm((256, 256), BF)],
+        v["acc", 0], v["acc", 1], bases, v["far"], v["lift_low"], half, swap(half, 1),
+        name="descent", out_space=pl.ANY, scratch=[vm((256, 256), BF), vm((LEAF, NRHS), BF), sem((8,))],
     )
     return out
 

time: 69.3 us -> 68 us (0.981)
  waiting for transfers between devices: 15.8 us -> 12 us
  starting transfers between devices: 25 us -> 27.5 us
    ppermute x22, waiting for transfers between devices: 15.8 us -> 12 us  [swap(): return lax.ppermute(x, AXIS, [(i, i ^ flip) for i in range(n)])]
    ppermute x22, starting transfers between devices: 25 us -> 27.5 us  [swap(): return lax.ppermute(x, AXIS, [(i, i ^ flip) for i in range(n)])]
    pallas_call x19 -> x20, Pallas kernels: 28.2 us -> 27.9 us  [call(): pl.pallas_call(body, out_shape=[jax.ShapeDtypeStruct(s, d) for s, d in ou...]
  transfers between devices with their start and end apart: 22 -> 22, of which waited for: 12 -> 9; matrix products, arithmetic and copies ran while one was open for 0% -> 0% of each run, Pallas kernels for 35% -> 36%
where the time goes in v4:
time: 68 us; the launch traced here: 67.9 us
  Pallas kernels  27.9 us (41%)
  starting transfers between devices  27.5 us (40%)
  waiting for transfers between devices  12 us (18%)
    pallas_call x20, Pallas kernels, call(): pl.pallas_call(body, out_shape=[jax.ShapeDtypeStruct(s, d) for s, d in ou...  27.9 us
    ppermute x22, starting transfers between devices, swap(): return lax.ppermute(x, AXIS, [(i, i ^ flip) for i in range(n)])  27.5 us
    ppermute x22, waiting for transfers between devices, swap(): return lax.ppermute(x, AXIS, [(i, i ^ flip) for i in range(n)])  12 us
  transfers between devices with their start and end apart: 22, of which 9 were waited for; matrix products, arithmetic and copies ran while one was open for 0% of the time, Pallas kernels for 36%

profile of v4, /device:TPU:1, one launch (start us, length us, event | category | flops | bytes accessed | tf_op | source)
XLA Modules:
  0.0 67.9 jit_solution(2056967115605737174)
XLA Ops:
  0.0 2.6 %collective-permute-start.2 = (bf16[2048,128]{1,0:T(8,128)(2,1)}, bf16[2048,128]{1,0:T(8,128)(2,1)S(1)}, u32[]{:S(2)}, u32[]{:S(2)}) collective-permute-start(bf16[2048,128]{1,0:T(8,128)(2,1)} %points_h.1), channel_id=1, source_target_pairs={{0,3},{1,2},{2,1},{3,0},{4,7},{5,6},{6,5},{7,4},{8,11},{9,10},{10,... | collective-permute-start | bytes 1572872 | tf_op jit(solution)/shard_map/ppermute | solution.py:301
  2.6 5.4 %prep.1 = (bf16[2048,256]{1,0:T(8,128)(2,1)S(1)}, bf16[2048,256]{1,0:T(8,128)(2,1)S(1)}, bf16[2432,256]{1,0:T(8,128)(2,1)S(1)}, bf16[1152,256]{1,0:T(8,128)(2,1)...) custom-call(s32[1,2048]{1,0:T(1,128)} %order_h.1, ...), custom_call_target="tpu_custom_call" | custom-call | tf_op jit(solution)/shard_map/prep/pallas_call | solution.py:59
  8.1 1.3 %collective-permute-done.got = bf16[192,256]{1,0:T(8,128)(2,1)S(1)} collective-permute-done((bf16[192,256]{1,0:T(8,128)(2,1)S(1)}, bf16[192,256]{1,0:T(8,128)(2,1)S(1)}, u32[]{:S(2)}, u32[]{:S(2)}) %collective-permute-start) | collective-permute-done | bytes 98336 | tf_op jit(solution)/shard_map/ppermute | solution.py:301
  9.7 1.6 %collective-permute-start.4 = (bf16[1152,256]{1,0:T(8,128)(2,1)S(1)}, bf16[1152,256]{1,0:T(8,128)(2,1)S(1)}, u32[]{:S(2)}, u32[]{:S(2)}) collective-permute-start(bf16[1152,256]{1,0:T(8,128)(2,1)S(1)} %get-tuple-element.214.own), channel_id=1, source_target_pairs={{0,3},{1,2},{2,1},{3,0},{4,7},{5,6},{6,5},{7,4},{8,11},{9,10},{10,... | collective-permute-start | bytes 1769480 | tf_op jit(solution)/shard_map/ppermute | solution.py:301
  11.3 2.6 %near_own.3.in_b = f32[1024,256]{1,0:T(8,128)S(1)} custom-call(bf16[2048,256]{1,0:T(8,128)(2,1)S(1)} %get-tuple-element.300.own_l.own, bf16[2048,256]{1,0:T(8,128)(2,1)S(1)} %get-tuple-element.190.own_r, bf16[2432,256]{1,0:T(8,128)(2,1)S(1)} %get-tuple-element.191.whole), custom_call_target="tpu_custom_call" | custom-call | tf_op jit(solution)/shard_map/near_own/pallas_call | solution.py:59
  13.9 2.6 %near_own.2.in_a = f32[1024,256]{1,0:T(8,128)S(1)} custom-call(bf16[2048,256]{1,0:T(8,128)(2,1)S(1)} %get-tuple-element.300.own_l.own, bf16[2048,256]{1,0:T(8,128)(2,1)S(1)} %get-tuple-element.190.own_r, bf16[2432,256]{1,0:T(8,128)(2,1)S(1)} %get-tuple-element.191.whole), custom_call_target="tpu_custom_call" | custom-call | tf_op jit(solution)/shard_map/near_own/pallas_call | solution.py:59
  16.6 1.3 %collective-permute-done.1.got = bf16[232,256]{1,0:T(8,128)(2,1)S(1)} collective-permute-done((bf16[232,256]{1,0:T(8,128)(2,1)S(1)}, bf16[232,256]{1,0:T(8,128)(2,1)S(1)}, u32[]{:S(2)}, u32[]{:S(2)}) %collective-permute-start.1) | collective-permute-done | bytes 118816 | tf_op jit(solution)/shard_map/ppermute | solution.py:301
  17.9 0.6 choose.4
  18.5 0.7 %collective-permute-start.3 = (bf16[2048,128]{1,0:T(8,128)(2,1)S(1)}, bf16[2048,128]{1,0:T(8,128)(2,1)S(1)}, u32[]{:S(2)}, u32[]{:S(2)}) collective-permute-start(bf16[2048,128]{1,0:T(8,128)(2,1)S(1)} %choose.4), channel_id=1, source_target_pairs={{0,1},{1,0},{2,3},{3,2},{4,5},{5,4},{6,7},{7,6},{8,9},{9,8},{10,11... | collective-permute-start | bytes 1572872 | tf_op jit(solution)/shard_map/ppermute | solution.py:301
  19.4 2.5 %collective-permute-start.5 = (bf16[208,256]{1,0:T(8,128)(2,1)S(1)}, bf16[208,256]{1,0:T(8,128)(2,1)S(1)}, u32[]{:S(2)}, u32[]{:S(2)}) collective-permute-start(bf16[208,256]{1,0:T(8,128)(2,1)S(1)} %get-tuple-element.218.mine), channel_id=1, source_target_pairs={{0,6},{1,7},{2,4},{3,5},{4,2},{5,3},{6,0},{7,1},{8,14},{9,15},{10,... | collective-permute-start | bytes 319496 | tf_op jit(solution)/shard_map/ppermute | solution.py:301
  21.9 1.2 %collective-permute-start.6 = (bf16[208,256]{1,0:T(8,128)(2,1)S(1)}, bf16[208,256]{1,0:T(8,128)(2,1)S(1)}, u32[]{:S(2)}, u32[]{:S(2)}) collective-permute-start(bf16[208,256]{1,0:T(8,128)(2,1)S(1)} %get-tuple-element.218.mine), channel_id=1, source_target_pairs={{0,8},{1,9},{2,10},{3,11},{4,12},{5,13},{6,14},{7,15},{8,0},{9,1},... | collective-permute-start | bytes 319496 | tf_op jit(solution)/shard_map/ppermute | solution.py:301
  23.3 1.9 %collective-permute-done.5.got_x.sib_x = bf16[208,256]{1,0:T(8,128)(2,1)S(1)} collective-permute-done((bf16[208,256]{1,0:T(8,128)(2,1)S(1)}, bf16[208,256]{1,0:T(8,128)(2,1)S(1)}, u32[]{:S(2)}, u32[]{:S(2)}) %collective-permute-start.5) | collective-permute-done | bytes 106528 | tf_op jit(solution)/shard_map/ppermute | solution.py:301
  25.2 0.9 %collective-permute-done.6.got_y.sib_y = bf16[208,256]{1,0:T(8,128)(2,1)S(1)} collective-permute-done((bf16[208,256]{1,0:T(8,128)(2,1)S(1)}, bf16[208,256]{1,0:T(8,128)(2,1)S(1)}, u32[]{:S(2)}, u32[]{:S(2)}) %collective-permute-start.6) | collective-permute-done | bytes 106528 | tf_op jit(solution)/shard_map/ppermute | solution.py:301
  26.1 3.0 %collective-permute-done.7.got_xy.sib_xy = bf16[208,256]{1,0:T(8,128)(2,1)S(1)} collective-permute-done((bf16[208,256]{1,0:T(8,128)(2,1)S(1)}, bf16[208,256]{1,0:T(8,128)(2,1)S(1)}, u32[]{:S(2)}, u32[]{:S(2)}) %collective-permute-start.7) | collective-permute-done | bytes 106528 | tf_op jit(solution)/shard_map/ppermute | solution.py:301
  29.1 1.4 %collective-permute-done.4.got.rows_a = bf16[1152,256]{1,0:T(8,128)(2,1)S(1)} collective-permute-done((bf16[1152,256]{1,0:T(8,128)(2,1)S(1)}, bf16[1152,256]{1,0:T(8,128)(2,1)S(1)}, u32[]{:S(2)}, u32[]{:S(2)}) %collective-permute-start.4) | collective-permute-done | bytes 589856 | tf_op jit(solution)/shard_map/ppermute | solution.py:301
  30.5 0.6 choose.5
  31.1 0.7 collective-permute-start.11
  31.8 1.4 %collective-permute-start.12 = (bf16[768,256]{1,0:T(8,128)(2,1)S(1)}, bf16[768,256]{1,0:T(8,128)(2,1)S(1)}, u32[]{:S(2)}, u32[]{:S(2)}) collective-permute-start(bf16[768,256]{1,0:T(8,128)(2,1)S(1)} %get-tuple-element.257.own), channel_id=1, source_target_pairs={{0,3},{1,2},{2,1},{3,0},{4,7},{5,6},{6,5},{7,4},{8,11},{9,10},{10,... | collective-permute-start | bytes 1179656 | tf_op jit(solution)/shard_map/ppermute | solution.py:301
  33.2 4.2 %collective-permute-start.10 = (bf16[128,256]{1,0:T(8,128)(2,1)S(1)}, bf16[128,256]{1,0:T(8,128)(2,1)S(1)}, u32[]{:S(2)}, u32[]{:S(2)}) collective-permute-start(bf16[128,256]{1,0:T(8,128)(2,1)S(1)} %get-tuple-element.252.mine), channel_id=1, source_target_pairs={{0,56},{1,57},{2,58},{3,59},{4,60},{5,61},{6,62},{7,63},{8,48},{9,... | collective-permute-start | bytes 196616 | tf_op jit(solution)/shard_map/ppermute | solution.py:301
  37.8 4.0 %near_chunk.3 = (f32[1024,256]{1,0:T(8,128)S(1)}, f32[1024,256]{1,0:T(8,128)S(1)}) custom-call(bf16[2048,256]{1,0:T(8,128)(2,1)S(1)} %get-tuple-element.300.own_l.own, bf16[2048,128]{1,0:T(8,128)(2,1)S(1)} %collective-permute-done.2.got.pts_a, bf16[1152,256]{1,0:T(8,128)(2,1)S(1)} %collective-permute-done.4.got.rows_a, ...), custom_call_target="tpu_custom_call", output_to_operand_aliasing={{0}: (5, {}), {1}: (6, {})} | custom-call | tf_op jit(solution)/shard_map/near_chunk/pallas_call | solution.py:59
  41.9 1.8 %collective-permute-start.13 = (bf16[512,256]{1,0:T(8,128)(2,1)S(1)}, bf16[512,256]{1,0:T(8,128)(2,1)S(1)}, u32[]{:S(2)}, u32[]{:S(2)}) collective-permute-start(bf16[512,256]{1,0:T(8,128)(2,1)S(1)} %get-tuple-element.280.side), channel_id=1, source_target_pairs={{0,1},{1,0},{2,3},{3,2},{4,5},{5,4},{6,7},{7,6},{8,9},{9,8},{10,11... | collective-permute-start | bytes 786440 | tf_op jit(solution)/shard_map/ppermute | solution.py:301
  43.6 2.7 %collective-permute-start.14 = (bf16[64,256]{1,0:T(8,128)(2,1)S(1)}, bf16[64,256]{1,0:T(8,128)(2,1)S(1)}, u32[]{:S(2)}, u32[]{:S(2)}) collective-permute-start(bf16[64,256]{1,0:T(8,128)(2,1)S(1)} %get-tuple-element.255), channel_id=1, source_target_pairs={{0,96},{1,97},{2,98},{3,99},{4,100},{5,101},{6,102},{7,103},{8,104... | collective-permute-start | bytes 98312 | tf_op jit(solution)/shard_map/ppermute | solution.py:301
  46.8 0.8 %collective-permute-done.14.across = bf16[64,256]{1,0:T(8,128)(2,1)S(1)} collective-permute-done((bf16[64,256]{1,0:T(8,128)(2,1)S(1)}, bf16[64,256]{1,0:T(8,128)(2,1)S(1)}, u32[]{:S(2)}, u32[]{:S(2)}) %collective-permute-start.14) | collective-permute-done | bytes 32800 | tf_op jit(solution)/shard_map/ppermute | solution.py:301
  48.2 1.3 %collective-permute-start.17 = (bf16[768,256]{1,0:T(8,128)(2,1)S(1)}, bf16[768,256]{1,0:T(8,128)(2,1)S(1)}, u32[]{:S(2)}, u32[]{:S(2)}) collective-permute-start(bf16[768,256]{1,0:T(8,128)(2,1)S(1)} %choose.6), channel_id=1, source_target_pairs={{0,1},{1,0},{2,3},{3,2},{4,5},{5,4},{6,7},{7,6},{8,9},{9,8},{10,11... | collective-permute-start | bytes 1179656 | tf_op jit(solution)/shard_map/ppermute | solution.py:301
  51.0 1.1 %top_coupling.1 = (f32[64,256]{1,0:T(8,128)S(1)}, bf16[64,256]{1,0:T(8,128)(2,1)S(1)}) custom-call(bf16[256,256]{1,0:T(8,128)(2,1)S(1)} %get-tuple-element.279.low, bf16[512,256]{1,0:T(8,128)(2,1)S(1)} %get-tuple-element.280.side, bf16[512,256]{1,0:T(8,128)(2,1)S(1)} %collective-permute-done.13.z_got.side_core, ...), custom_call_target="tpu_custom_call" | custom-call | tf_op jit(solution)/shard_map/top_coupling/pallas_call | solution.py:59
  52.1 3.0 %collective-permute-start.16 = (bf16[64,256]{1,0:T(8,128)(2,1)S(1)}, bf16[64,256]{1,0:T(8,128)(2,1)S(1)}, u32[]{:S(2)}, u32[]{:S(2)}) collective-permute-start(bf16[64,256]{1,0:T(8,128)(2,1)S(1)} %get-tuple-element.284), channel_id=1, source_target_pairs={{0,96},{1,97},{2,98},{3,99},{4,100},{5,101},{6,102},{7,103},{8,104... | collective-permute-start | bytes 98312 | tf_op jit(solution)/shard_map/ppermute | solution.py:301
  55.1 4.0 %near_chunk.4 = (f32[1024,256]{1,0:T(8,128)S(1)}, f32[1024,256]{1,0:T(8,128)S(1)}) custom-call(bf16[2048,256]{1,0:T(8,128)(2,1)S(1)} %get-tuple-element.300.own_l.own, bf16[2048,128]{1,0:T(8,128)(2,1)S(1)} %collective-permute-done.2.got.pts_a, bf16[768,256]{1,0:T(8,128)(2,1)S(1)} %collective-permute-done.12.got.rows_a, ...), custom_call_target="tpu_custom_call", output_to_operand_aliasing={{0}: (5, {}), {1}: (6, {})} | custom-call | tf_op jit(solution)/shard_map/near_chunk/pallas_call | solution.py:59
  59.7 0.7 %collective-permute-start.20 = (bf16[512,256]{1,0:T(8,128)(2,1)S(1)}, bf16[512,256]{1,0:T(8,128)(2,1)S(1)}, u32[]{:S(2)}, u32[]{:S(2)}) collective-permute-start(bf16[512,256]{1,0:T(8,128)(2,1)S(1)} %choose.7), channel_id=1, source_target_pairs={{0,1},{1,0},{2,3},{3,2},{4,5},{5,4},{6,7},{7,6},{8,9},{9,8},{10,11... | collective-permute-start | bytes 786440 | tf_op jit(solution)/shard_map/ppermute | solution.py:301
  60.6 1.3 %collective-permute-start.19 = (bf16[64,256]{1,0:T(8,128)(2,1)S(1)}, bf16[64,256]{1,0:T(8,128)(2,1)S(1)}, u32[]{:S(2)}, u32[]{:S(2)}) collective-permute-start(bf16[64,256]{1,0:T(8,128)(2,1)S(1)} %field.1.mine), channel_id=1, source_target_pairs={{0,2},{1,3},{2,0},{3,1},{4,6},{5,7},{6,4},{7,5},{8,10},{9,11},{10,... | collective-permute-start | bytes 98312 | tf_op jit(solution)/shard_map/ppermute | solution.py:301
  62.0 2.9 %near_chunk.5 = (f32[1024,256]{1,0:T(8,128)S(1)}, f32[1024,256]{1,0:T(8,128)S(1)}) custom-call(bf16[2048,256]{1,0:T(8,128)(2,1)S(1)} %get-tuple-element.300.own_l.own, bf16[2048,128]{1,0:T(8,128)(2,1)S(1)} %collective-permute-done.2.got.pts_a, bf16[512,256]{1,0:T(8,128)(2,1)S(1)} %collective-permute-done.18.got.rows_a, ...), custom_call_target="tpu_custom_call", output_to_operand_aliasing={{0}: (5, {}), {1}: (6, {})} | custom-call | tf_op jit(solution)/shard_map/near_chunk/pallas_call | solution.py:59
  65.3 1.0 %collective-permute-done.21.got = bf16[128,256]{1,0:T(8,128)(2,1)S(1)} collective-permute-done((bf16[128,256]{1,0:T(8,128)(2,1)S(1)}, bf16[128,256]{1,0:T(8,128)(2,1)S(1)}, u32[]{:S(2)}, u32[]{:S(2)}) %collective-permute-start.21) | collective-permute-done | bytes 65568 | tf_op jit(solution)/shard_map/ppermute | solution.py:301
  66.2 1.5 %descent.1 = bf16[2048,256]{1,0:T(8,128)(2,1)} custom-call(f32[1024,256]{1,0:T(8,128)S(1)} %get-tuple-element.317.in_a, f32[1024,256]{1,0:T(8,128)S(1)} %get-tuple-element.318.in_b, bf16[2048,256]{1,0:T(8,128)(2,1)S(1)} %copy-done, f32[256,256]{1,0:T(8,128)S(1)} %far.1, bf16[256,256]{1,0:T(8,128)(2,1)S(1)} %get-tuple-element.320.lift, ...), custom_call_target="tpu_custom_call" | custom-call | tf_op jit(solution)/shard_map/descent/pallas_call | solution.py:59
  (36 shorter events, 4.9 us)
Async XLA Ops:
  0.0 17.9 %collective-permute-start.2 = (bf16[2048,128]{1,0:T(8,128)(2,1)}, bf16[2048,128]{1,0:T(8,128)(2,1)S(1)}, u32[]{:S(2)}, u32[]{:S(2)}) collective-permute-start(bf16[2048,128]{1,0:T(8,128)(2,1)} %points_h.1), channel_id=1, source_target_pairs={{0,3},{1,2},{2,1},{3,0},{4,7},{5,6},{6,5},{7,4},{8,11},{9,10},{10,... | collective-permute-start | bytes 1572872 | tf_op jit(solution)/shard_map/ppermute | solution.py:301
  8.0 1.4 %collective-permute-start = (bf16[192,256]{1,0:T(8,128)(2,1)S(1)}, bf16[192,256]{1,0:T(8,128)(2,1)S(1)}, u32[]{:S(2)}, u32[]{:S(2)}) collective-permute-start(bf16[192,256]{1,0:T(8,128)(2,1)S(1)} %get-tuple-element.193.sent), channel_id=1, source_target_pairs={{0,1},{1,0},{2,3},{3,2},{4,5},{5,4},{6,7},{7,6},{8,9},{9,8},{10,11... | collective-permute-start | bytes 294920 | tf_op jit(solution)/shard_map/ppermute | solution.py:301
  9.4 8.5 %collective-permute-start.1 = (bf16[232,256]{1,0:T(8,128)(2,1)S(1)}, bf16[232,256]{1,0:T(8,128)(2,1)S(1)}, u32[]{:S(2)}, u32[]{:S(2)}) collective-permute-start(bf16[232,256]{1,0:T(8,128)(2,1)S(1)} %get-tuple-element.205.sent), channel_id=1, source_target_pairs={{0,2},{1,3},{2,0},{3,1},{4,6},{5,7},{6,4},{7,5},{8,10},{9,11},{10,... | collective-permute-start | bytes 356360 | tf_op jit(solution)/shard_map/ppermute | solution.py:301
  9.7 20.8 %collective-permute-start.4 = (bf16[1152,256]{1,0:T(8,128)(2,1)S(1)}, bf16[1152,256]{1,0:T(8,128)(2,1)S(1)}, u32[]{:S(2)}, u32[]{:S(2)}) collective-permute-start(bf16[1152,256]{1,0:T(8,128)(2,1)S(1)} %get-tuple-element.214.own), channel_id=1, source_target_pairs={{0,3},{1,2},{2,1},{3,0},{4,7},{5,6},{6,5},{7,4},{8,11},{9,10},{10,... | collective-permute-start | bytes 1769480 | tf_op jit(solution)/shard_map/ppermute | solution.py:301
  13.9 3.9 %copy-start.1 = (s32[1,2]{1,0:T(1,128)S(1)}, s32[1,2]{1,0:T(1,128)}, u32[]{:S(2)}) copy-start(s32[1,2]{1,0:T(1,128)} %near.7) | copy-start | bytes 28
  18.5 12.0 %collective-permute-start.3 = (bf16[2048,128]{1,0:T(8,128)(2,1)S(1)}, bf16[2048,128]{1,0:T(8,128)(2,1)S(1)}, u32[]{:S(2)}, u32[]{:S(2)}) collective-permute-start(bf16[2048,128]{1,0:T(8,128)(2,1)S(1)} %choose.4), channel_id=1, source_target_pairs={{0,1},{1,0},{2,3},{3,2},{4,5},{5,4},{6,7},{7,6},{8,9},{9,8},{10,11... | collective-permute-start | bytes 1572872 | tf_op jit(solution)/shard_map/ppermute | solution.py:301
  19.4 5.8 %collective-permute-start.5 = (bf16[208,256]{1,0:T(8,128)(2,1)S(1)}, bf16[208,256]{1,0:T(8,128)(2,1)S(1)}, u32[]{:S(2)}, u32[]{:S(2)}) collective-permute-start(bf16[208,256]{1,0:T(8,128)(2,1)S(1)} %get-tuple-element.218.mine), channel_id=1, source_target_pairs={{0,6},{1,7},{2,4},{3,5},{4,2},{5,3},{6,0},{7,1},{8,14},{9,15},{10,... | collective-permute-start | bytes 319496 | tf_op jit(solution)/shard_map/ppermute | solution.py:301
  21.9 4.2 %collective-permute-start.6 = (bf16[208,256]{1,0:T(8,128)(2,1)S(1)}, bf16[208,256]{1,0:T(8,128)(2,1)S(1)}, u32[]{:S(2)}, u32[]{:S(2)}) collective-permute-start(bf16[208,256]{1,0:T(8,128)(2,1)S(1)} %get-tuple-element.218.mine), channel_id=1, source_target_pairs={{0,8},{1,9},{2,10},{3,11},{4,12},{5,13},{6,14},{7,15},{8,0},{9,1},... | collective-permute-start | bytes 319496 | tf_op jit(solution)/shard_map/ppermute | solution.py:301
  23.2 6.0 %collective-permute-start.7 = (bf16[208,256]{1,0:T(8,128)(2,1)S(1)}, bf16[208,256]{1,0:T(8,128)(2,1)S(1)}, u32[]{:S(2)}, u32[]{:S(2)}) collective-permute-start(bf16[208,256]{1,0:T(8,128)(2,1)S(1)} %get-tuple-element.218.mine), channel_id=1, source_target_pairs={{0,14},{1,15},{2,12},{3,13},{4,10},{5,11},{6,8},{7,9},{8,6},{9,7},... | collective-permute-start | bytes 319496 | tf_op jit(solution)/shard_map/ppermute | solution.py:301
  31.1 6.7 %collective-permute-start.11 = (bf16[1152,256]{1,0:T(8,128)(2,1)S(1)}, bf16[1152,256]{1,0:T(8,128)(2,1)S(1)}, u32[]{:S(2)}, u32[]{:S(2)}) collective-permute-start(bf16[1152,256]{1,0:T(8,128)(2,1)S(1)} %choose.5), channel_id=1, source_target_pairs={{0,1},{1,0},{2,3},{3,2},{4,5},{5,4},{6,7},{7,6},{8,9},{9,8},{10,11... | collective-permute-start | bytes 1769480 | tf_op jit(solution)/shard_map/ppermute | solution.py:301
  31.8 15.0 %collective-permute-start.12 = (bf16[768,256]{1,0:T(8,128)(2,1)S(1)}, bf16[768,256]{1,0:T(8,128)(2,1)S(1)}, u32[]{:S(2)}, u32[]{:S(2)}) collective-permute-start(bf16[768,256]{1,0:T(8,128)(2,1)S(1)} %get-tuple-element.257.own), channel_id=1, source_target_pairs={{0,3},{1,2},{2,1},{3,0},{4,7},{5,6},{6,5},{7,4},{8,11},{9,10},{10,... | collective-permute-start | bytes 1179656 | tf_op jit(solution)/shard_map/ppermute | solution.py:301
  33.2 8.6 %collective-permute-start.10 = (bf16[128,256]{1,0:T(8,128)(2,1)S(1)}, bf16[128,256]{1,0:T(8,128)(2,1)S(1)}, u32[]{:S(2)}, u32[]{:S(2)}) collective-permute-start(bf16[128,256]{1,0:T(8,128)(2,1)S(1)} %get-tuple-element.252.mine), channel_id=1, source_target_pairs={{0,56},{1,57},{2,58},{3,59},{4,60},{5,61},{6,62},{7,63},{8,48},{9,... | collective-permute-start | bytes 196616 | tf_op jit(solution)/shard_map/ppermute | solution.py:301
  37.4 4.4 %collective-permute-start.8 = (bf16[128,256]{1,0:T(8,128)(2,1)S(1)}, bf16[128,256]{1,0:T(8,128)(2,1)S(1)}, u32[]{:S(2)}, u32[]{:S(2)}) collective-permute-start(bf16[128,256]{1,0:T(8,128)(2,1)S(1)} %get-tuple-element.252.mine), channel_id=1, source_target_pairs={{0,24},{1,25},{2,26},{3,27},{4,28},{5,29},{6,30},{7,31},{8,16},{9,... | collective-permute-start | bytes 196616 | tf_op jit(solution)/shard_map/ppermute | solution.py:301
  37.4 4.4 %collective-permute-start.9 = (bf16[128,256]{1,0:T(8,128)(2,1)S(1)}, bf16[128,256]{1,0:T(8,128)(2,1)S(1)}, u32[]{:S(2)}, u32[]{:S(2)}) collective-permute-start(bf16[128,256]{1,0:T(8,128)(2,1)S(1)} %get-tuple-element.252.mine), channel_id=1, source_target_pairs={{0,32},{1,33},{2,34},{3,35},{4,36},{5,37},{6,38},{7,39},{8,40},{9,... | collective-permute-start | bytes 196616 | tf_op jit(solution)/shard_map/ppermute | solution.py:301
  41.9 5.8 %collective-permute-start.13 = (bf16[512,256]{1,0:T(8,128)(2,1)S(1)}, bf16[512,256]{1,0:T(8,128)(2,1)S(1)}, u32[]{:S(2)}, u32[]{:S(2)}) collective-permute-start(bf16[512,256]{1,0:T(8,128)(2,1)S(1)} %get-tuple-element.280.side), channel_id=1, source_target_pairs={{0,1},{1,0},{2,3},{3,2},{4,5},{5,4},{6,7},{7,6},{8,9},{9,8},{10,11... | collective-permute-start | bytes 786440 | tf_op jit(solution)/shard_map/ppermute | solution.py:301
  43.6 4.0 %collective-permute-start.14 = (bf16[64,256]{1,0:T(8,128)(2,1)S(1)}, bf16[64,256]{1,0:T(8,128)(2,1)S(1)}, u32[]{:S(2)}, u32[]{:S(2)}) collective-permute-start(bf16[64,256]{1,0:T(8,128)(2,1)S(1)} %get-tuple-element.255), channel_id=1, source_target_pairs={{0,96},{1,97},{2,98},{3,99},{4,100},{5,101},{6,102},{7,103},{8,104... | collective-permute-start | bytes 98312 | tf_op jit(solution)/shard_map/ppermute | solution.py:301
  48.2 6.8 %collective-permute-start.17 = (bf16[768,256]{1,0:T(8,128)(2,1)S(1)}, bf16[768,256]{1,0:T(8,128)(2,1)S(1)}, u32[]{:S(2)}, u32[]{:S(2)}) collective-permute-start(bf16[768,256]{1,0:T(8,128)(2,1)S(1)} %choose.6), channel_id=1, source_target_pairs={{0,1},{1,0},{2,3},{3,2},{4,5},{5,4},{6,7},{7,6},{8,9},{9,8},{10,11... | collective-permute-start | bytes 1179656 | tf_op jit(solution)/shard_map/ppermute | solution.py:301
  49.5 9.5 %collective-permute-start.18 = (bf16[512,256]{1,0:T(8,128)(2,1)S(1)}, bf16[512,256]{1,0:T(8,128)(2,1)S(1)}, u32[]{:S(2)}, u32[]{:S(2)}) collective-permute-start(bf16[512,256]{1,0:T(8,128)(2,1)S(1)} %get-tuple-element.299.own), channel_id=1, source_target_pairs={{0,3},{1,2},{2,1},{3,0},{4,7},{5,6},{6,5},{7,4},{8,11},{9,10},{10,... | collective-permute-start | bytes 786440 | tf_op jit(solution)/shard_map/ppermute | solution.py:301
  49.7 1.3 %collective-permute-start.15 = (bf16[64,256]{1,0:T(8,128)(2,1)S(1)}, bf16[64,256]{1,0:T(8,128)(2,1)S(1)}, u32[]{:S(2)}, u32[]{:S(2)}) collective-permute-start(bf16[64,256]{1,0:T(8,128)(2,1)S(1)} %collective-permute-done.14.across), channel_id=1, source_target_pairs={{0,1},{1,0},{2,3},{3,2},{4,5},{5,4},{6,7},{7,6},{8,9},{9,8},{10,11... | collective-permute-start | bytes 98312 | tf_op jit(solution)/shard_map/ppermute | solution.py:301
  52.1 7.0 %collective-permute-start.16 = (bf16[64,256]{1,0:T(8,128)(2,1)S(1)}, bf16[64,256]{1,0:T(8,128)(2,1)S(1)}, u32[]{:S(2)}, u32[]{:S(2)}) collective-permute-start(bf16[64,256]{1,0:T(8,128)(2,1)S(1)} %get-tuple-element.284), channel_id=1, source_target_pairs={{0,96},{1,97},{2,98},{3,99},{4,100},{5,101},{6,102},{7,103},{8,104... | collective-permute-start | bytes 98312 | tf_op jit(solution)/shard_map/ppermute | solution.py:301
  59.7 2.3 %collective-permute-start.20 = (bf16[512,256]{1,0:T(8,128)(2,1)S(1)}, bf16[512,256]{1,0:T(8,128)(2,1)S(1)}, u32[]{:S(2)}, u32[]{:S(2)}) collective-permute-start(bf16[512,256]{1,0:T(8,128)(2,1)S(1)} %choose.7), channel_id=1, source_target_pairs={{0,1},{1,0},{2,3},{3,2},{4,5},{5,4},{6,7},{7,6},{8,9},{9,8},{10,11... | collective-permute-start | bytes 786440 | tf_op jit(solution)/shard_map/ppermute | solution.py:301
  60.6 5.6 %copy-start = (bf16[2048,256]{1,0:T(8,128)(2,1)S(1)}, bf16[2048,256]{1,0:T(8,128)(2,1)}, u32[]{:S(2)}) copy-start(bf16[2048,256]{1,0:T(8,128)(2,1)} %bases.1) | copy-start | bytes 3145732
  60.6 4.2 %collective-permute-start.19 = (bf16[64,256]{1,0:T(8,128)(2,1)S(1)}, bf16[64,256]{1,0:T(8,128)(2,1)S(1)}, u32[]{:S(2)}, u32[]{:S(2)}) collective-permute-start(bf16[64,256]{1,0:T(8,128)(2,1)S(1)} %field.1.mine), channel_id=1, source_target_pairs={{0,2},{1,3},{2,0},{3,1},{4,6},{5,7},{6,4},{7,5},{8,10},{9,11},{10,... | collective-permute-start | bytes 98312 | tf_op jit(solution)/shard_map/ppermute | solution.py:301
  64.9 1.3 %collective-permute-start.21 = (bf16[128,256]{1,0:T(8,128)(2,1)S(1)}, bf16[128,256]{1,0:T(8,128)(2,1)S(1)}, u32[]{:S(2)}, u32[]{:S(2)}) collective-permute-start(bf16[128,256]{1,0:T(8,128)(2,1)S(1)} %join.1.half), channel_id=1, source_target_pairs={{0,1},{1,0},{2,3},{3,2},{4,5},{5,4},{6,7},{7,6},{8,9},{9,8},{10,11... | collective-permute-start | bytes 196616 | tf_op jit(solution)/shard_map/ppermute | solution.py:301

commit v5 on v4

--- a/solution.py
+++ b/solution.py
@@ -385,7 +385,7 @@
     chunk(0)
     finish(dict(got=got, low=top, z_all=z_all, t_own=t_own))
 
-    across = swap(v["t_own"], 96)
+    across, across_core = swap(v["t_own"], 96), swap(v["t_own"], 97)
     low, side = call(
         more_body, [((256, 256), BF), ((512, 256), BF)], v["low"], *v["got"], v["z_all"], name="more"
     )
@@ -393,25 +393,21 @@
     rows_two = swap(v["buf", 2], 3)
     far, = call(far_body, [((256, 256), F32)], v["rows_b", 0], v["proxy_wide"], name="far")
     v["rows_a", 1] = rows_one
-    finish(dict(low=low, side=side, side_core=side_core, far=far, across=across))
-
-    across_core = swap(v["across"], 1)
-    rows_b_one = swap(chosen(v["rows_a", 1], v["buf", 1]), 1)
+    finish(dict(low=low, side=side, side_core=side_core, far=far, across=across, across_core=across_core))
+
+    own_field, send = call(
+        top_coupling_body, [((64, 256), F32), ((64, 256), BF)], v["low"], v["side"], v["side_core"],
+        v["across"], v["across_core"], name="top_coupling", scratch=[vm((1280, 128), F32)],
+    )
+    got = swap(send, 96)
+    v["rows_b", 1] = swap(chosen(v["rows_a", 1], v["buf", 1]), 1)
     kernel_one, = call(
         node_coupling_body, [((768, 256), BF)], v["z_all"], v["side_core"], name="node_coupling",
         scratch=[vm((1024, 128), BF)],
     )
-    finish(dict(across_core=across_core, kernel_one=kernel_one))
-
-    own_field, send = call(
-        top_coupling_body, [((64, 256), F32), ((64, 256), BF)], v["low"], v["side"], v["side_core"],
-        v["across"], v["across_core"], name="top_coupling", scratch=[vm((1280, 128), F32)],
-    )
-    got = swap(send, 96)
-    v["rows_b", 1] = rows_b_one
     chunk(1)
     v["rows_a", 2] = rows_two
-    finish(dict(got=got, own_field=own_field))
+    finish(dict(got=got, own_field=own_field, kernel_one=kernel_one))
 
     quarter, = call(
         field_body, [((64, 256), BF)], *v["sibs"], v["own_field"], v["got"], v["kernel_one"], v["lift_all"],

time: 68 us -> 68.3 us (level)
  waiting for transfers between devices: 12 us -> 16.8 us
  starting transfers between devices: 27.5 us -> 23 us
    ppermute x22, waiting for transfers between devices: 12 us -> 16.8 us  [swap(): return lax.ppermute(x, AXIS, [(i, i ^ flip) for i in range(n)])]
    ppermute x22, starting transfers between devices: 27.5 us -> 23 us  [swap(): return lax.ppermute(x, AXIS, [(i, i ^ flip) for i in range(n)])]
  transfers between devices with their start and end apart: 22 -> 22, of which waited for: 9 -> 11; matrix products, arithmetic and copies ran while one was open for 0% -> 0% of each run, Pallas kernels for 36% -> 36%
where the time goes in v5:
time: 68.3 us; the launch traced here: 68.1 us
  Pallas kernels  27.9 us (41%)
  starting transfers between devices  23 us (34%)
  waiting for transfers between devices  16.8 us (25%)
    pallas_call x20, Pallas kernels, call(): pl.pallas_call(body, out_shape=[jax.ShapeDtypeStruct(s, d) for s, d in ou...  27.9 us
    ppermute x22, starting transfers between devices, swap(): return lax.ppermute(x, AXIS, [(i, i ^ flip) for i in range(n)])  23 us
    ppermute x22, waiting for transfers between devices, swap(): return lax.ppermute(x, AXIS, [(i, i ^ flip) for i in range(n)])  16.8 us
  transfers between devices with their start and end apart: 22, of which 11 were waited for; matrix products, arithmetic and copies ran while one was open for 0% of the time, Pallas kernels for 36%

profile of v5, /device:TPU:1, one launch (start us, length us, event | category | flops | bytes accessed | tf_op | source)
XLA Modules:
  0.0 68.1 jit_solution(417171029826798462)
XLA Ops:
  0.0 2.6 %collective-permute-start.2 = (bf16[2048,128]{1,0:T(8,128)(2,1)}, bf16[2048,128]{1,0:T(8,128)(2,1)S(1)}, u32[]{:S(2)}, u32[]{:S(2)}) collective-permute-start(bf16[2048,128]{1,0:T(8,128)(2,1)} %points_h.1), channel_id=1, source_target_pairs={{0,3},{1,2},{2,1},{3,0},{4,7},{5,6},{6,5},{7,4},{8,11},{9,10},{10,... | collective-permute-start | bytes 1572872 | tf_op jit(solution)/shard_map/ppermute | solution.py:301
  2.6 5.4 %prep.1 = (bf16[2048,256]{1,0:T(8,128)(2,1)S(1)}, bf16[2048,256]{1,0:T(8,128)(2,1)S(1)}, bf16[2432,256]{1,0:T(8,128)(2,1)S(1)}, bf16[1152,256]{1,0:T(8,128)(2,1)...) custom-call(s32[1,2048]{1,0:T(1,128)} %order_h.1, ...), custom_call_target="tpu_custom_call" | custom-call | tf_op jit(solution)/shard_map/prep/pallas_call | solution.py:59
  8.1 1.3 %collective-permute-done.got = bf16[192,256]{1,0:T(8,128)(2,1)S(1)} collective-permute-done((bf16[192,256]{1,0:T(8,128)(2,1)S(1)}, bf16[192,256]{1,0:T(8,128)(2,1)S(1)}, u32[]{:S(2)}, u32[]{:S(2)}) %collective-permute-start) | collective-permute-done | bytes 98336 | tf_op jit(solution)/shard_map/ppermute | solution.py:301
  9.7 1.6 %collective-permute-start.4 = (bf16[1152,256]{1,0:T(8,128)(2,1)S(1)}, bf16[1152,256]{1,0:T(8,128)(2,1)S(1)}, u32[]{:S(2)}, u32[]{:S(2)}) collective-permute-start(bf16[1152,256]{1,0:T(8,128)(2,1)S(1)} %get-tuple-element.196.own), channel_id=1, source_target_pairs={{0,3},{1,2},{2,1},{3,0},{4,7},{5,6},{6,5},{7,4},{8,11},{9,10},{10,... | collective-permute-start | bytes 1769480 | tf_op jit(solution)/shard_map/ppermute | solution.py:301
  11.3 2.6 %near_own.3.in_b = f32[1024,256]{1,0:T(8,128)S(1)} custom-call(bf16[2048,256]{1,0:T(8,128)(2,1)S(1)} %get-tuple-element.264.own_l.own, bf16[2048,256]{1,0:T(8,128)(2,1)S(1)} %get-tuple-element.172.own_r, bf16[2432,256]{1,0:T(8,128)(2,1)S(1)} %get-tuple-element.173.whole), custom_call_target="tpu_custom_call" | custom-call | tf_op jit(solution)/shard_map/near_own/pallas_call | solution.py:59
  13.9 2.6 %near_own.2.in_a = f32[1024,256]{1,0:T(8,128)S(1)} custom-call(bf16[2048,256]{1,0:T(8,128)(2,1)S(1)} %get-tuple-element.264.own_l.own, bf16[2048,256]{1,0:T(8,128)(2,1)S(1)} %get-tuple-element.172.own_r, bf16[2432,256]{1,0:T(8,128)(2,1)S(1)} %get-tuple-element.173.whole), custom_call_target="tpu_custom_call" | custom-call | tf_op jit(solution)/shard_map/near_own/pallas_call | solution.py:59
  16.6 1.3 %collective-permute-done.1.got = bf16[232,256]{1,0:T(8,128)(2,1)S(1)} collective-permute-done((bf16[232,256]{1,0:T(8,128)(2,1)S(1)}, bf16[232,256]{1,0:T(8,128)(2,1)S(1)}, u32[]{:S(2)}, u32[]{:S(2)}) %collective-permute-start.1) | collective-permute-done | bytes 118816 | tf_op jit(solution)/shard_map/ppermute | solution.py:301
  17.9 0.6 choose.4
  18.5 0.7 %collective-permute-start.3 = (bf16[2048,128]{1,0:T(8,128)(2,1)S(1)}, bf16[2048,128]{1,0:T(8,128)(2,1)S(1)}, u32[]{:S(2)}, u32[]{:S(2)}) collective-permute-start(bf16[2048,128]{1,0:T(8,128)(2,1)S(1)} %choose.4), channel_id=1, source_target_pairs={{0,1},{1,0},{2,3},{3,2},{4,5},{5,4},{6,7},{7,6},{8,9},{9,8},{10,11... | collective-permute-start | bytes 1572872 | tf_op jit(solution)/shard_map/ppermute | solution.py:301
  19.4 2.5 %collective-permute-start.5 = (bf16[208,256]{1,0:T(8,128)(2,1)S(1)}, bf16[208,256]{1,0:T(8,128)(2,1)S(1)}, u32[]{:S(2)}, u32[]{:S(2)}) collective-permute-start(bf16[208,256]{1,0:T(8,128)(2,1)S(1)} %get-tuple-element.200.mine), channel_id=1, source_target_pairs={{0,6},{1,7},{2,4},{3,5},{4,2},{5,3},{6,0},{7,1},{8,14},{9,15},{10,... | collective-permute-start | bytes 319496 | tf_op jit(solution)/shard_map/ppermute | solution.py:301
  21.9 1.2 %collective-permute-start.6 = (bf16[208,256]{1,0:T(8,128)(2,1)S(1)}, bf16[208,256]{1,0:T(8,128)(2,1)S(1)}, u32[]{:S(2)}, u32[]{:S(2)}) collective-permute-start(bf16[208,256]{1,0:T(8,128)(2,1)S(1)} %get-tuple-element.200.mine), channel_id=1, source_target_pairs={{0,8},{1,9},{2,10},{3,11},{4,12},{5,13},{6,14},{7,15},{8,0},{9,1},... | collective-permute-start | bytes 319496 | tf_op jit(solution)/shard_map/ppermute | solution.py:301
  23.3 1.9 %collective-permute-done.5.got_x.sib_x = bf16[208,256]{1,0:T(8,128)(2,1)S(1)} collective-permute-done((bf16[208,256]{1,0:T(8,128)(2,1)S(1)}, bf16[208,256]{1,0:T(8,128)(2,1)S(1)}, u32[]{:S(2)}, u32[]{:S(2)}) %collective-permute-start.5) | collective-permute-done | bytes 106528 | tf_op jit(solution)/shard_map/ppermute | solution.py:301
  25.2 0.9 %collective-permute-done.6.got_y.sib_y = bf16[208,256]{1,0:T(8,128)(2,1)S(1)} collective-permute-done((bf16[208,256]{1,0:T(8,128)(2,1)S(1)}, bf16[208,256]{1,0:T(8,128)(2,1)S(1)}, u32[]{:S(2)}, u32[]{:S(2)}) %collective-permute-start.6) | collective-permute-done | bytes 106528 | tf_op jit(solution)/shard_map/ppermute | solution.py:301
  26.1 3.0 %collective-permute-done.7.got_xy.sib_xy = bf16[208,256]{1,0:T(8,128)(2,1)S(1)} collective-permute-done((bf16[208,256]{1,0:T(8,128)(2,1)S(1)}, bf16[208,256]{1,0:T(8,128)(2,1)S(1)}, u32[]{:S(2)}, u32[]{:S(2)}) %collective-permute-start.7) | collective-permute-done | bytes 106528 | tf_op jit(solution)/shard_map/ppermute | solution.py:301
  29.1 1.4 %collective-permute-done.4.got.rows_a = bf16[1152,256]{1,0:T(8,128)(2,1)S(1)} collective-permute-done((bf16[1152,256]{1,0:T(8,128)(2,1)S(1)}, bf16[1152,256]{1,0:T(8,128)(2,1)S(1)}, u32[]{:S(2)}, u32[]{:S(2)}) %collective-permute-start.4) | collective-permute-done | bytes 589856 | tf_op jit(solution)/shard_map/ppermute | solution.py:301
  30.5 0.6 choose.5
  31.1 0.7 collective-permute-start.11
  31.8 1.4 %collective-permute-start.12 = (bf16[768,256]{1,0:T(8,128)(2,1)S(1)}, bf16[768,256]{1,0:T(8,128)(2,1)S(1)}, u32[]{:S(2)}, u32[]{:S(2)}) collective-permute-start(bf16[768,256]{1,0:T(8,128)(2,1)S(1)} %get-tuple-element.239.own), channel_id=1, source_target_pairs={{0,3},{1,2},{2,1},{3,0},{4,7},{5,6},{6,5},{7,4},{8,11},{9,10},{10,... | collective-permute-start | bytes 1179656 | tf_op jit(solution)/shard_map/ppermute | solution.py:301
  33.2 4.2 %collective-permute-start.10 = (bf16[128,256]{1,0:T(8,128)(2,1)S(1)}, bf16[128,256]{1,0:T(8,128)(2,1)S(1)}, u32[]{:S(2)}, u32[]{:S(2)}) collective-permute-start(bf16[128,256]{1,0:T(8,128)(2,1)S(1)} %get-tuple-element.234.mine), channel_id=1, source_target_pairs={{0,56},{1,57},{2,58},{3,59},{4,60},{5,61},{6,62},{7,63},{8,48},{9,... | collective-permute-start | bytes 196616 | tf_op jit(solution)/shard_map/ppermute | solution.py:301
  37.8 4.0 %near_chunk.3 = (f32[1024,256]{1,0:T(8,128)S(1)}, f32[1024,256]{1,0:T(8,128)S(1)}) custom-call(bf16[2048,256]{1,0:T(8,128)(2,1)S(1)} %get-tuple-element.264.own_l.own, bf16[2048,128]{1,0:T(8,128)(2,1)S(1)} %collective-permute-done.2.got.pts_a, bf16[1152,256]{1,0:T(8,128)(2,1)S(1)} %collective-permute-done.4.got.rows_a, ...), custom_call_target="tpu_custom_call", output_to_operand_aliasing={{0}: (5, {}), {1}: (6, {})} | custom-call | tf_op jit(solution)/shard_map/near_chunk/pallas_call | solution.py:59
  41.9 1.8 %collective-permute-start.13 = (bf16[512,256]{1,0:T(8,128)(2,1)S(1)}, bf16[512,256]{1,0:T(8,128)(2,1)S(1)}, u32[]{:S(2)}, u32[]{:S(2)}) collective-permute-start(bf16[512,256]{1,0:T(8,128)(2,1)S(1)} %get-tuple-element.244.side), channel_id=1, source_target_pairs={{0,1},{1,0},{2,3},{3,2},{4,5},{5,4},{6,7},{7,6},{8,9},{9,8},{10,11... | collective-permute-start | bytes 786440 | tf_op jit(solution)/shard_map/ppermute | solution.py:301
  43.6 2.7 %collective-permute-start.14 = (bf16[64,256]{1,0:T(8,128)(2,1)S(1)}, bf16[64,256]{1,0:T(8,128)(2,1)S(1)}, u32[]{:S(2)}, u32[]{:S(2)}) collective-permute-start(bf16[64,256]{1,0:T(8,128)(2,1)S(1)} %get-tuple-element.237), channel_id=1, source_target_pairs={{0,96},{1,97},{2,98},{3,99},{4,100},{5,101},{6,102},{7,103},{8,104... | collective-permute-start | bytes 98312 | tf_op jit(solution)/shard_map/ppermute | solution.py:301
  47.6 3.2 %collective-permute-done.15.across_core = bf16[64,256]{1,0:T(8,128)(2,1)S(1)} collective-permute-done((bf16[64,256]{1,0:T(8,128)(2,1)S(1)}, bf16[64,256]{1,0:T(8,128)(2,1)S(1)}, u32[]{:S(2)}, u32[]{:S(2)}) %collective-permute-start.15) | collective-permute-done | bytes 32800 | tf_op jit(solution)/shard_map/ppermute | solution.py:301
  50.9 0.6 choose.6
  52.2 1.1 %top_coupling.1 = (f32[64,256]{1,0:T(8,128)S(1)}, bf16[64,256]{1,0:T(8,128)(2,1)S(1)}) custom-call(bf16[256,256]{1,0:T(8,128)(2,1)S(1)} %get-tuple-element.243.low, bf16[512,256]{1,0:T(8,128)(2,1)S(1)} %get-tuple-element.244.side, bf16[512,256]{1,0:T(8,128)(2,1)S(1)} %collective-permute-done.13.side_core.z_got, ...), custom_call_target="tpu_custom_call" | custom-call | tf_op jit(solution)/shard_map/top_coupling/pallas_call | solution.py:59
  53.3 0.8 %collective-permute-start.16 = (bf16[64,256]{1,0:T(8,128)(2,1)S(1)}, bf16[64,256]{1,0:T(8,128)(2,1)S(1)}, u32[]{:S(2)}, u32[]{:S(2)}) collective-permute-start(bf16[64,256]{1,0:T(8,128)(2,1)S(1)} %get-tuple-element.248), channel_id=1, source_target_pairs={{0,96},{1,97},{2,98},{3,99},{4,100},{5,101},{6,102},{7,103},{8,104... | collective-permute-start | bytes 98312 | tf_op jit(solution)/shard_map/ppermute | solution.py:301
  54.5 4.0 %near_chunk.4 = (f32[1024,256]{1,0:T(8,128)S(1)}, f32[1024,256]{1,0:T(8,128)S(1)}) custom-call(bf16[2048,256]{1,0:T(8,128)(2,1)S(1)} %get-tuple-element.264.own_l.own, bf16[2048,128]{1,0:T(8,128)(2,1)S(1)} %collective-permute-done.2.got.pts_a, bf16[768,256]{1,0:T(8,128)(2,1)S(1)} %collective-permute-done.12.got.rows_a, ...), custom_call_target="tpu_custom_call", output_to_operand_aliasing={{0}: (5, {}), {1}: (6, {})} | custom-call | tf_op jit(solution)/shard_map/near_chunk/pallas_call | solution.py:59
  58.5 1.5 %collective-permute-done.18.got.rows_a = bf16[512,256]{1,0:T(8,128)(2,1)S(1)} collective-permute-done((bf16[512,256]{1,0:T(8,128)(2,1)S(1)}, bf16[512,256]{1,0:T(8,128)(2,1)S(1)}, u32[]{:S(2)}, u32[]{:S(2)}) %collective-permute-start.18) | collective-permute-done | bytes 262176 | tf_op jit(solution)/shard_map/ppermute | solution.py:301
  61.4 0.8 %collective-permute-done.20.rows_b = bf16[512,256]{1,0:T(8,128)(2,1)S(1)} collective-permute-done((bf16[512,256]{1,0:T(8,128)(2,1)S(1)}, bf16[512,256]{1,0:T(8,128)(2,1)S(1)}, u32[]{:S(2)}, u32[]{:S(2)}) %collective-permute-start.20) | collective-permute-done | bytes 262176 | tf_op jit(solution)/shard_map/ppermute | solution.py:301
  62.2 2.9 %near_chunk.5 = (f32[1024,256]{1,0:T(8,128)S(1)}, f32[1024,256]{1,0:T(8,128)S(1)}) custom-call(bf16[2048,256]{1,0:T(8,128)(2,1)S(1)} %get-tuple-element.264.own_l.own, bf16[2048,128]{1,0:T(8,128)(2,1)S(1)} %collective-permute-done.2.got.pts_a, bf16[512,256]{1,0:T(8,128)(2,1)S(1)} %collective-permute-done.18.got.rows_a, ...), custom_call_target="tpu_custom_call", output_to_operand_aliasing={{0}: (5, {}), {1}: (6, {})} | custom-call | tf_op jit(solution)/shard_map/near_chunk/pallas_call | solution.py:59
  65.5 0.9 %collective-permute-done.21.got = bf16[128,256]{1,0:T(8,128)(2,1)S(1)} collective-permute-done((bf16[128,256]{1,0:T(8,128)(2,1)S(1)}, bf16[128,256]{1,0:T(8,128)(2,1)S(1)}, u32[]{:S(2)}, u32[]{:S(2)}) %collective-permute-start.21) | collective-permute-done | bytes 65568 | tf_op jit(solution)/shard_map/ppermute | solution.py:301
  66.5 1.5 %descent.1 = bf16[2048,256]{1,0:T(8,128)(2,1)} custom-call(f32[1024,256]{1,0:T(8,128)S(1)} %get-tuple-element.281.in_a, f32[1024,256]{1,0:T(8,128)S(1)} %get-tuple-element.282.in_b, bf16[2048,256]{1,0:T(8,128)(2,1)S(1)} %copy-done, f32[256,256]{1,0:T(8,128)S(1)} %far.1, bf16[256,256]{1,0:T(8,128)(2,1)S(1)} %get-tuple-element.284.lift, ...), custom_call_target="tpu_custom_call" | custom-call | tf_op jit(solution)/shard_map/descent/pallas_call | solution.py:59
  (36 shorter events, 5.5 us)
Async XLA Ops:
  0.0 17.9 %collective-permute-start.2 = (bf16[2048,128]{1,0:T(8,128)(2,1)}, bf16[2048,128]{1,0:T(8,128)(2,1)S(1)}, u32[]{:S(2)}, u32[]{:S(2)}) collective-permute-start(bf16[2048,128]{1,0:T(8,128)(2,1)} %points_h.1), channel_id=1, source_target_pairs={{0,3},{1,2},{2,1},{3,0},{4,7},{5,6},{6,5},{7,4},{8,11},{9,10},{10,... | collective-permute-start | bytes 1572872 | tf_op jit(solution)/shard_map/ppermute | solution.py:301
  8.0 1.4 %collective-permute-start = (bf16[192,256]{1,0:T(8,128)(2,1)S(1)}, bf16[192,256]{1,0:T(8,128)(2,1)S(1)}, u32[]{:S(2)}, u32[]{:S(2)}) collective-permute-start(bf16[192,256]{1,0:T(8,128)(2,1)S(1)} %get-tuple-element.175.sent), channel_id=1, source_target_pairs={{0,1},{1,0},{2,3},{3,2},{4,5},{5,4},{6,7},{7,6},{8,9},{9,8},{10,11... | collective-permute-start | bytes 294920 | tf_op jit(solution)/shard_map/ppermute | solution.py:301
  9.4 8.5 %collective-permute-start.1 = (bf16[232,256]{1,0:T(8,128)(2,1)S(1)}, bf16[232,256]{1,0:T(8,128)(2,1)S(1)}, u32[]{:S(2)}, u32[]{:S(2)}) collective-permute-start(bf16[232,256]{1,0:T(8,128)(2,1)S(1)} %get-tuple-element.187.sent), channel_id=1, source_target_pairs={{0,2},{1,3},{2,0},{3,1},{4,6},{5,7},{6,4},{7,5},{8,10},{9,11},{10,... | collective-permute-start | bytes 356360 | tf_op jit(solution)/shard_map/ppermute | solution.py:301
  9.7 20.8 %collective-permute-start.4 = (bf16[1152,256]{1,0:T(8,128)(2,1)S(1)}, bf16[1152,256]{1,0:T(8,128)(2,1)S(1)}, u32[]{:S(2)}, u32[]{:S(2)}) collective-permute-start(bf16[1152,256]{1,0:T(8,128)(2,1)S(1)} %get-tuple-element.196.own), channel_id=1, source_target_pairs={{0,3},{1,2},{2,1},{3,0},{4,7},{5,6},{6,5},{7,4},{8,11},{9,10},{10,... | collective-permute-start | bytes 1769480 | tf_op jit(solution)/shard_map/ppermute | solution.py:301
  13.9 3.9 %copy-start.1 = (s32[1,2]{1,0:T(1,128)S(1)}, s32[1,2]{1,0:T(1,128)}, u32[]{:S(2)}) copy-start(s32[1,2]{1,0:T(1,128)} %near.7) | copy-start | bytes 28
  18.5 12.0 %collective-permute-start.3 = (bf16[2048,128]{1,0:T(8,128)(2,1)S(1)}, bf16[2048,128]{1,0:T(8,128)(2,1)S(1)}, u32[]{:S(2)}, u32[]{:S(2)}) collective-permute-start(bf16[2048,128]{1,0:T(8,128)(2,1)S(1)} %choose.4), channel_id=1, source_target_pairs={{0,1},{1,0},{2,3},{3,2},{4,5},{5,4},{6,7},{7,6},{8,9},{9,8},{10,11... | collective-permute-start | bytes 1572872 | tf_op jit(solution)/shard_map/ppermute | solution.py:301
  19.4 5.8 %collective-permute-start.5 = (bf16[208,256]{1,0:T(8,128)(2,1)S(1)}, bf16[208,256]{1,0:T(8,128)(2,1)S(1)}, u32[]{:S(2)}, u32[]{:S(2)}) collective-permute-start(bf16[208,256]{1,0:T(8,128)(2,1)S(1)} %get-tuple-element.200.mine), channel_id=1, source_target_pairs={{0,6},{1,7},{2,4},{3,5},{4,2},{5,3},{6,0},{7,1},{8,14},{9,15},{10,... | collective-permute-start | bytes 319496 | tf_op jit(solution)/shard_map/ppermute | solution.py:301
  21.9 4.2 %collective-permute-start.6 = (bf16[208,256]{1,0:T(8,128)(2,1)S(1)}, bf16[208,256]{1,0:T(8,128)(2,1)S(1)}, u32[]{:S(2)}, u32[]{:S(2)}) collective-permute-start(bf16[208,256]{1,0:T(8,128)(2,1)S(1)} %get-tuple-element.200.mine), channel_id=1, source_target_pairs={{0,8},{1,9},{2,10},{3,11},{4,12},{5,13},{6,14},{7,15},{8,0},{9,1},... | collective-permute-start | bytes 319496 | tf_op jit(solution)/shard_map/ppermute | solution.py:301
  23.2 6.0 %collective-permute-start.7 = (bf16[208,256]{1,0:T(8,128)(2,1)S(1)}, bf16[208,256]{1,0:T(8,128)(2,1)S(1)}, u32[]{:S(2)}, u32[]{:S(2)}) collective-permute-start(bf16[208,256]{1,0:T(8,128)(2,1)S(1)} %get-tuple-element.200.mine), channel_id=1, source_target_pairs={{0,14},{1,15},{2,12},{3,13},{4,10},{5,11},{6,8},{7,9},{8,6},{9,7},... | collective-permute-start | bytes 319496 | tf_op jit(solution)/shard_map/ppermute | solution.py:301
  31.1 6.7 %collective-permute-start.11 = (bf16[1152,256]{1,0:T(8,128)(2,1)S(1)}, bf16[1152,256]{1,0:T(8,128)(2,1)S(1)}, u32[]{:S(2)}, u32[]{:S(2)}) collective-permute-start(bf16[1152,256]{1,0:T(8,128)(2,1)S(1)} %choose.5), channel_id=1, source_target_pairs={{0,1},{1,0},{2,3},{3,2},{4,5},{5,4},{6,7},{7,6},{8,9},{9,8},{10,11... | collective-permute-start | bytes 1769480 | tf_op jit(solution)/shard_map/ppermute | solution.py:301
  31.8 15.3 %collective-permute-start.12 = (bf16[768,256]{1,0:T(8,128)(2,1)S(1)}, bf16[768,256]{1,0:T(8,128)(2,1)S(1)}, u32[]{:S(2)}, u32[]{:S(2)}) collective-permute-start(bf16[768,256]{1,0:T(8,128)(2,1)S(1)} %get-tuple-element.239.own), channel_id=1, source_target_pairs={{0,3},{1,2},{2,1},{3,0},{4,7},{5,6},{6,5},{7,4},{8,11},{9,10},{10,... | collective-permute-start | bytes 1179656 | tf_op jit(solution)/shard_map/ppermute | solution.py:301
  33.2 8.6 %collective-permute-start.10 = (bf16[128,256]{1,0:T(8,128)(2,1)S(1)}, bf16[128,256]{1,0:T(8,128)(2,1)S(1)}, u32[]{:S(2)}, u32[]{:S(2)}) collective-permute-start(bf16[128,256]{1,0:T(8,128)(2,1)S(1)} %get-tuple-element.234.mine), channel_id=1, source_target_pairs={{0,56},{1,57},{2,58},{3,59},{4,60},{5,61},{6,62},{7,63},{8,48},{9,... | collective-permute-start | bytes 196616 | tf_op jit(solution)/shard_map/ppermute | solution.py:301
  37.4 4.4 %collective-permute-start.8 = (bf16[128,256]{1,0:T(8,128)(2,1)S(1)}, bf16[128,256]{1,0:T(8,128)(2,1)S(1)}, u32[]{:S(2)}, u32[]{:S(2)}) collective-permute-start(bf16[128,256]{1,0:T(8,128)(2,1)S(1)} %get-tuple-element.234.mine), channel_id=1, source_target_pairs={{0,24},{1,25},{2,26},{3,27},{4,28},{5,29},{6,30},{7,31},{8,16},{9,... | collective-permute-start | bytes 196616 | tf_op jit(solution)/shard_map/ppermute | solution.py:301
  37.4 4.4 %collective-permute-start.9 = (bf16[128,256]{1,0:T(8,128)(2,1)S(1)}, bf16[128,256]{1,0:T(8,128)(2,1)S(1)}, u32[]{:S(2)}, u32[]{:S(2)}) collective-permute-start(bf16[128,256]{1,0:T(8,128)(2,1)S(1)} %get-tuple-element.234.mine), channel_id=1, source_target_pairs={{0,32},{1,33},{2,34},{3,35},{4,36},{5,37},{6,38},{7,39},{8,40},{9,... | collective-permute-start | bytes 196616 | tf_op jit(solution)/shard_map/ppermute | solution.py:301
  41.9 9.0 %collective-permute-start.13 = (bf16[512,256]{1,0:T(8,128)(2,1)S(1)}, bf16[512,256]{1,0:T(8,128)(2,1)S(1)}, u32[]{:S(2)}, u32[]{:S(2)}) collective-permute-start(bf16[512,256]{1,0:T(8,128)(2,1)S(1)} %get-tuple-element.244.side), channel_id=1, source_target_pairs={{0,1},{1,0},{2,3},{3,2},{4,5},{5,4},{6,7},{7,6},{8,9},{9,8},{10,11... | collective-permute-start | bytes 786440 | tf_op jit(solution)/shard_map/ppermute | solution.py:301
  43.6 4.0 %collective-permute-start.14 = (bf16[64,256]{1,0:T(8,128)(2,1)S(1)}, bf16[64,256]{1,0:T(8,128)(2,1)S(1)}, u32[]{:S(2)}, u32[]{:S(2)}) collective-permute-start(bf16[64,256]{1,0:T(8,128)(2,1)S(1)} %get-tuple-element.237), channel_id=1, source_target_pairs={{0,96},{1,97},{2,98},{3,99},{4,100},{5,101},{6,102},{7,103},{8,104... | collective-permute-start | bytes 98312 | tf_op jit(solution)/shard_map/ppermute | solution.py:301
  46.3 4.6 %collective-permute-start.15 = (bf16[64,256]{1,0:T(8,128)(2,1)S(1)}, bf16[64,256]{1,0:T(8,128)(2,1)S(1)}, u32[]{:S(2)}, u32[]{:S(2)}) collective-permute-start(bf16[64,256]{1,0:T(8,128)(2,1)S(1)} %get-tuple-element.237), channel_id=1, source_target_pairs={{0,97},{1,96},{2,99},{3,98},{4,101},{5,100},{6,103},{7,102},{8,105... | collective-permute-start | bytes 98312 | tf_op jit(solution)/shard_map/ppermute | solution.py:301
  51.5 3.0 %collective-permute-start.17 = (bf16[768,256]{1,0:T(8,128)(2,1)S(1)}, bf16[768,256]{1,0:T(8,128)(2,1)S(1)}, u32[]{:S(2)}, u32[]{:S(2)}) collective-permute-start(bf16[768,256]{1,0:T(8,128)(2,1)S(1)} %choose.6), channel_id=1, source_target_pairs={{0,1},{1,0},{2,3},{3,2},{4,5},{5,4},{6,7},{7,6},{8,9},{9,8},{10,11... | collective-permute-start | bytes 1179656 | tf_op jit(solution)/shard_map/ppermute | solution.py:301
  51.9 8.1 %collective-permute-start.18 = (bf16[512,256]{1,0:T(8,128)(2,1)S(1)}, bf16[512,256]{1,0:T(8,128)(2,1)S(1)}, u32[]{:S(2)}, u32[]{:S(2)}) collective-permute-start(bf16[512,256]{1,0:T(8,128)(2,1)S(1)} %get-tuple-element.263.own), channel_id=1, source_target_pairs={{0,3},{1,2},{2,1},{3,0},{4,7},{5,6},{6,5},{7,4},{8,11},{9,10},{10,... | collective-permute-start | bytes 786440 | tf_op jit(solution)/shard_map/ppermute | solution.py:301
  53.3 6.7 %collective-permute-start.16 = (bf16[64,256]{1,0:T(8,128)(2,1)S(1)}, bf16[64,256]{1,0:T(8,128)(2,1)S(1)}, u32[]{:S(2)}, u32[]{:S(2)}) collective-permute-start(bf16[64,256]{1,0:T(8,128)(2,1)S(1)} %get-tuple-element.248), channel_id=1, source_target_pairs={{0,96},{1,97},{2,98},{3,99},{4,100},{5,101},{6,102},{7,103},{8,104... | collective-permute-start | bytes 98312 | tf_op jit(solution)/shard_map/ppermute | solution.py:301
  60.6 1.6 %collective-permute-start.20 = (bf16[512,256]{1,0:T(8,128)(2,1)S(1)}, bf16[512,256]{1,0:T(8,128)(2,1)S(1)}, u32[]{:S(2)}, u32[]{:S(2)}) collective-permute-start(bf16[512,256]{1,0:T(8,128)(2,1)S(1)} %choose.7), channel_id=1, source_target_pairs={{0,1},{1,0},{2,3},{3,2},{4,5},{5,4},{6,7},{7,6},{8,9},{9,8},{10,11... | collective-permute-start | bytes 786440 | tf_op jit(solution)/shard_map/ppermute | solution.py:301
  61.1 5.3 %copy-start = (bf16[2048,256]{1,0:T(8,128)(2,1)S(1)}, bf16[2048,256]{1,0:T(8,128)(2,1)}, u32[]{:S(2)}) copy-start(bf16[2048,256]{1,0:T(8,128)(2,1)} %bases.1) | copy-start | bytes 3145732
  61.1 4.0 %collective-permute-start.19 = (bf16[64,256]{1,0:T(8,128)(2,1)S(1)}, bf16[64,256]{1,0:T(8,128)(2,1)S(1)}, u32[]{:S(2)}, u32[]{:S(2)}) collective-permute-start(bf16[64,256]{1,0:T(8,128)(2,1)S(1)} %field.1.mine), channel_id=1, source_target_pairs={{0,2},{1,3},{2,0},{3,1},{4,6},{5,7},{6,4},{7,5},{8,10},{9,11},{10,... | collective-permute-start | bytes 98312 | tf_op jit(solution)/shard_map/ppermute | solution.py:301
  65.1 1.3 %collective-permute-start.21 = (bf16[128,256]{1,0:T(8,128)(2,1)S(1)}, bf16[128,256]{1,0:T(8,128)(2,1)S(1)}, u32[]{:S(2)}, u32[]{:S(2)}) collective-permute-start(bf16[128,256]{1,0:T(8,128)(2,1)S(1)} %join.1.half), channel_id=1, source_target_pairs={{0,1},{1,0},{2,3},{3,2},{4,5},{5,4},{6,7},{7,6},{8,9},{9,8},{10,11... | collective-permute-start | bytes 196616 | tf_op jit(solution)/shard_map/ppermute | solution.py:301
